TPU v7x, 256 devices: a whole 4x4x8 slice. The times are simulated.
256 devices in a mesh: dp: 32 (over z, x), mp: 8 (over y, core).
Axes of the slice: x: 4, y: 4, z: 8, core: 2. Of those that a mesh axis runs over, the one named last changes fastest.
Arguments:
- tokens: bfloat16 [32768, 8192], P('dp', 'mp'), may hold values from -6 to 6
- value_weight: bfloat16 [8192, 1024], P('mp'), may hold values from -0.0625 to 0.0625
- adapter_down_panels: bfloat16 [96, 64, 8192], P('dp', None, 'mp'), may hold values from -0.0625 to 0.0625
- adapter_up_panels: bfloat16 [96, 64, 1024], P('dp', None, 'mp'), may hold values from -0.75 to 0.75
- cotangent: bfloat16 [32768, 1024], P('dp', 'mp'), may hold values from -6 to 6
- block_list_entry: int32 [1024], P('dp'), may hold values from 0 to 31, as said below
- device_tenant_list: int32 [1024], P('dp'), may hold values from 0 to 95, as said below
- tenant_location_map: int32 [96], replicated, may hold values from 0 to 95, as said below
Outputs:
- values: bfloat16 [32768, 1024], P('dp', 'mp')
- token_gradient: bfloat16 [32768, 8192], P('dp', 'mp')
- grad_a: bfloat16 [96, 64, 8192], P('dp', None, 'mp')
- grad_b: bfloat16 [96, 64, 1024], P('dp', None, 'mp')
Inputs may be any that keep to these rules, and one draw needn't show every extreme that they name: `device_tenant_list`: each entry names a tenant; no tenant stands twice in one list. Of one device's 32 entries, at most 2 name tenants whose storage location tenant_location_map[t] lies on one dp index (tenant_location_map[t] // 3), and every device's list has 2 entries on some one dp index. A permutation: tenant t's panels are row tenant_location_map[t] of adapter_down_panels and adapter_up_panels. `block_list_entry`: every entry of a device's tenant list is named by at least one of that device's row blocks.
All inputs are finite; a program needn't handle non-finite values.
Results may differ from a plain program's by a relative error of at most 0.0057.
Values may be sent and summed in bfloat16 or wider, within the bound.
A program may use at most 128 MiB of HBM per device.

v0:
```python
import jax
import jax.numpy as jnp
from jax import lax
from jax.sharding import PartitionSpec as P

MOST = 2


def compare_table(left, right):
    return left[:, None] == right[None, :]


def shards(
    tokens,
    value_weight,
    adapter_down_panels,
    adapter_up_panels,
    cotangent,
    block_list_entry,
    device_tenant_list,
    tenant_location_map,
):
    rows, width_loc = tokens.shape
    stored_panels, adapter_rank_size, ignored_result = adapter_down_panels.shape
    output_location = adapter_up_panels.shape[2]
    blocks = block_list_entry.shape[0]
    block_rows = rows // blocks
    listed = device_tenant_list.shape[0]
    tenants = tenant_location_map.shape[0]
    capacity = lax.axis_size("dp") * MOST
    slot_ids = jnp.arange(listed, dtype=jnp.int32)
    tenant_ids = jnp.arange(tenants, dtype=jnp.int32)
    storage_location = jnp.sum(
        jnp.where(compare_table(device_tenant_list, tenant_ids), tenant_location_map[None, :], 0),
        axis=1,
    )
    holder = storage_location // stored_panels
    local_row = storage_location % stored_panels
    earlier = slot_ids[:, None] > slot_ids[None, :]
    rank_at = jnp.sum(jnp.where(compare_table(holder, holder) & earlier, 1, 0), axis=1).astype(
        jnp.int32
    )
    position = holder * MOST + rank_at
    canonical = jnp.min(
        jnp.where(compare_table(device_tenant_list, device_tenant_list), slot_ids[None, :], listed),
        axis=1,
    )
    block_canon = jnp.sum(
        jnp.where(compare_table(block_list_entry, slot_ids), canonical[None, :], 0), axis=1
    )
    requests = jnp.zeros((capacity,), jnp.int32).at[position].set(local_row + 1)
    incoming = lax.all_to_all(requests, "dp", split_axis=0, concat_axis=0, tiled=True)
    serve_adapters = compare_table(
        incoming, jnp.arange(1, stored_panels + 1, dtype=jnp.int32)
    ).astype(jnp.bfloat16)
    returned_down_panel = jnp.einsum(
        "vj,jiz->viz", serve_adapters, adapter_down_panels, preferred_element_type=jnp.float32
    ).astype(jnp.bfloat16)
    returned_up_panel = jnp.einsum(
        "wu,une->wne", serve_adapters, adapter_up_panels, preferred_element_type=jnp.float32
    ).astype(jnp.bfloat16)
    got_a, got_b = (
        lax.all_to_all(returned_down_panel, "dp", split_axis=0, concat_axis=0, tiled=True),
        lax.all_to_all(returned_up_panel, "dp", split_axis=0, concat_axis=0, tiled=True),
    )
    slot_a = got_a[position]
    slot_b = got_b[position]
    w_cols = value_weight
    base_flipped_weight = lax.psum_scatter(
        lax.dot_general(
            w_cols, tokens, (((0,), (1,)), ((), ())), preferred_element_type=jnp.float32
        ),
        "mp",
        scatter_dimension=0,
        tiled=True,
    )
    token_blocks = tokens.reshape(blocks, block_rows, width_loc)
    cot_blocks = cotangent.reshape(blocks, block_rows, output_location)
    block_down_panel = slot_a[block_list_entry]
    block_up_panel = slot_b[block_list_entry]
    down_part = jnp.einsum(
        "bnd,brd->bnr", token_blocks, block_down_panel, preferred_element_type=jnp.float32
    )
    down_low = lax.psum(down_part, "mp").astype(jnp.bfloat16)
    adapter_output = jnp.einsum(
        "afq,aqy->afy", down_low, block_up_panel, preferred_element_type=jnp.float32
    ).reshape(rows, output_location)
    values = (base_flipped_weight.T + adapter_output).astype(jnp.bfloat16)
    up_part = jnp.einsum(
        "bnc,brc->bnr", cot_blocks, block_up_panel, preferred_element_type=jnp.float32
    )
    up_grad = lax.psum(up_part, "mp").astype(jnp.bfloat16)
    w_cols = value_weight
    base_backward_pass = lax.dot_general(
        lax.all_gather(cotangent, "mp", axis=1, tiled=True),
        w_cols,
        (((1,), (1,)), ((), ())),
        preferred_element_type=jnp.float32,
    )
    adapter_backward_pass = jnp.einsum(
        "swq,sqj->swj", up_grad, block_down_panel, preferred_element_type=jnp.float32
    ).reshape(rows, width_loc)
    token_gradient = (base_backward_pass + adapter_backward_pass).astype(jnp.bfloat16)
    block_grad_a = jnp.einsum(
        "bnr,bnd->brd", up_grad, token_blocks, preferred_element_type=jnp.float32
    )
    block_grad_b = jnp.einsum(
        "bnr,bnc->brc", down_low, cot_blocks, preferred_element_type=jnp.float32
    )
    gather_slots = compare_table(block_canon, slot_ids).astype(jnp.float32)
    share_a = jnp.einsum(
        "bs,brd->srd", gather_slots, block_grad_a, precision=lax.Precision.HIGHEST
    ).astype(jnp.bfloat16)
    share_b = jnp.einsum(
        "bs,brc->src", gather_slots, block_grad_b, precision=lax.Precision.HIGHEST
    ).astype(jnp.bfloat16)
    send_a = (
        jnp.zeros((capacity, adapter_rank_size, width_loc), jnp.bfloat16).at[position].set(share_a)
    )
    send_b = (
        jnp.zeros((capacity, adapter_rank_size, output_location), jnp.bfloat16)
        .at[position]
        .set(share_b)
    )
    back_a, back_b = (
        lax.all_to_all(send_a, "dp", split_axis=0, concat_axis=0, tiled=True),
        lax.all_to_all(send_b, "dp", split_axis=0, concat_axis=0, tiled=True),
    )
    grad_a = jnp.einsum(
        "qk,qrd->krd", serve_adapters, back_a, preferred_element_type=jnp.float32
    ).astype(jnp.bfloat16)
    grad_b = jnp.einsum(
        "qk,qrc->krc", serve_adapters, back_b, preferred_element_type=jnp.float32
    ).astype(jnp.bfloat16)
    return (values, token_gradient, grad_a, grad_b)


def solution(mesh):
    in_specs = (
        P("dp", "mp"),
        P("mp", None),
        P("dp", None, "mp"),
        P("dp", None, "mp"),
        P("dp", "mp"),
        P("dp"),
        P("dp"),
        P(),
    )
    out_specs = (P("dp", "mp"), P("dp", "mp"), P("dp", None, "mp"), P("dp", None, "mp"))
    return jax.shard_map(shards, mesh=mesh, in_specs=in_specs, out_specs=out_specs, check_vma=False)
```

profile of v0, /device:TPU:127, one launch (start us, length us, event | category | flops | bytes accessed | tf_op | source)
XLA Modules:
  0.0 603.8 jit_solution(13908184175450942226)
XLA Ops:
  7.2 1.0 select_reduce_fusion.3
  8.4 0.7 scatter_custom_fusion
  9.1 0.7 all_to_all.18
  9.8 9.6 %all-to-all-start = ((s32[32,2,1]{1,2,0:T(1,128)}), s32[32,2,1]{1,2,0:T(1,128)S(1)}, u32[]{:S(2)}, u32[]{:S(2)}) async-start(s32[32,2,1]{1,2,0:T(1,128)} %bitcast.5), calls=%async_computation.1 | async-start | bytes 32768 | tf_op jit(solution)/shard_map/all_to_all | solution.py:52
  19.5 4.4 all-to-all-done
  23.9 0.5 broadcast.150
  24.4 0.7 reduce.3
  25.2 1.4 convolution_convert_fusion.1
  26.5 1.6 copy.51
  28.2 8.7 %all-to-all-start.2 = ((bf16[64,64,128]{2,1,0:T(8,128)(2,1)}), bf16[64,64,128]{2,1,0:T(8,128)(2,1)}, u32[]{:S(2)}, u32[]{:S(2)}) async-start(bf16[64,64,128]{2,1,0:T(8,128)(2,1)} %copy.51), calls=%async_computation.3 | async-start | bytes 2097152 | tf_op jit(solution)/shard_map/all_to_all | solution.py:64
  36.9 5.7 convolution_convert_fusion
  42.6 11.3 %copy.49 = bf16[64,64,1024]{2,1,0:T(8,128)(2,1)} copy(bf16[64,64,1024]{2,0,1:T(8,128)(2,1)} %convolution_convert_fusion) | data formatting | bytes 16777216 | tf_op jit(solution)/shard_map/convert_element_type | solution.py:58
  53.9 7.4 %all-to-all-done.2 = bf16[64,64,128]{2,1,0:T(8,128)(2,1)} async-done(((bf16[64,64,128]{2,1,0:T(8,128)(2,1)}), bf16[64,64,128]{2,1,0:T(8,128)(2,1)}, u32[]{:S(2)}, u32[]{:S(2)}) %all-to-all-start.2) | async-done | bytes 1048608 | tf_op jit(solution)/shard_map/all_to_all | solution.py:64
  61.3 19.3 %all-to-all-start.1 = ((bf16[64,64,1024]{2,1,0:T(8,128)(2,1)}), bf16[64,64,1024]{2,1,0:T(8,128)(2,1)}, u32[]{:S(2)}, u32[]{:S(2)}) async-start(bf16[64,64,1024]{2,1,0:T(8,128)(2,1)} %copy.49), calls=%async_computation.2 | async-start | bytes 16777216 | tf_op jit(solution)/shard_map/all_to_all | solution.py:63
  81.0 1.9 gather_fusion.2
  82.9 0.6 gather_fusion.3
  83.5 0.4 convolution_bitcast_fusion
  83.9 184.2 %all-to-all-done.1 = bf16[64,64,1024]{2,1,0:T(8,128)(2,1)} async-done(((bf16[64,64,1024]{2,1,0:T(8,128)(2,1)}), bf16[64,64,1024]{2,1,0:T(8,128)(2,1)}, u32[]{:S(2)}, u32[]{:S(2)}) %all-to-all-start.1) | async-done | bytes 8388640 | tf_op jit(solution)/shard_map/all_to_all | solution.py:63
  268.1 6.2 %gather_fusion = bf16[32,64,1024]{2,1,0:T(8,128)(2,1)} fusion(bf16[64,64,1024]{2,1,0:T(8,128)(2,1)} %all-to-all-done.1, s32[1024]{0:T(1024)S(1)} %pad_clamp_fusion.1), kind=kCustom, calls=%fused_computation | custom fusion | bytes 8388736 | tf_op jit(solution)/shard_map/gather | solution.py:66
  274.3 4.9 gather_fusion.1
  279.2 4.2 convolution_bitcast_fusion.1
  283.4 52.8 %all-reduce.2 = (bf16[32,32,64]{2,1,0:T(8,128)(2,1)}, bf16[32,32,64]{2,1,0:T(8,128)(2,1)}) all-reduce(f32[32,32,64]{2,1,0:T(8,128)} %convolution_bitcast_fusion.1, f32[32,32,64]{2,1,0:T(8,128)S(1)} %convolution_bitcast_fusion), channel_id=1, replica_groups=mesh['dp'=32,'mp'=8] {'mp'}, use_global_device_ids=true, to_apply=%region_4.5 | all-reduce | flops 131072 | bytes 786432 | tf_op jit(solution)/shard_map/psum | solution.py:84
  336.3 1.3 fusion.55
  337.6 1.3 convolution_convert_fusion.2
  339.1 1.2 broadcast_in_dim.80
  340.3 4.4 scatter_fusion.1
  344.7 6.9 %all-to-all-start.4 = ((bf16[64,64,128]{2,1,0:T(8,128)(2,1)}), bf16[64,64,128]{2,1,0:T(8,128)(2,1)}, u32[]{:S(2)}, u32[]{:S(2)}) async-start(bf16[64,64,128]{2,1,0:T(8,128)(2,1)} %scatter_fusion.1), calls=%async_computation.5 | async-start | bytes 2097152 | tf_op jit(solution)/shard_map/all_to_all | solution.py:127
  351.6 1.3 fusion.53
  352.8 7.6 %fusion.5 = bf16[32,64,1024]{2,0,1:T(8,128)(2,1)S(1)} fusion(f32[32,64,1024]{2,1,0:T(8,128)S(1)} %fusion.53, s32[32]{0:T(128)S(1)} %select_reduce_fusion), kind=kOutput, calls=%fused_computation.14 | convolution fusion | flops 807404544 | bytes 12583040 | tf_op jit(solution)/shard_map/bs,brd->srd/dot_general | solution.py:111
  360.5 4.2 copy.54
  364.7 4.3 broadcast_in_dim.77
  369.0 11.5 %scatter_fusion = bf16[64,64,1024]{2,1,0:T(8,128)(2,1)} fusion(bf16[64,64,1024]{2,1,0:T(8,128)(2,1)} %broadcast_in_dim.77, s32[32]{0:T(128)S(1)} %fusion.49, bf16[32,64,1024]{2,1,0:T(8,128)(2,1)} %copy.54), kind=kCustom, calls=%fused_computation.5 | custom fusion | bytes 12583040 | tf_op jit(solution)/shard_map/scatter | solution.py:118
  380.5 9.1 %all-to-all-start.3 = ((bf16[64,64,1024]{2,1,0:T(8,128)(2,1)}), bf16[64,64,1024]{2,1,0:T(8,128)(2,1)}, u32[]{:S(2)}, u32[]{:S(2)}) async-start(bf16[64,64,1024]{2,1,0:T(8,128)(2,1)} %scatter_fusion), calls=%async_computation.4 | async-start | bytes 16777216 | tf_op jit(solution)/shard_map/all_to_all | solution.py:126
  389.7 5.9 fusion.52
  395.7 0.2 all-gather.2.cloned.1.call-start
  395.9 0.5 all-gather.2.cloned.1.call-update
  396.6 0.3 fusion.56
  397.1 39.0 %reduce-scatter.2.cloned.1.call-done = f32[128,1024]{1,0:T(8,128)} async-done(((f32[1024,1024]{1,0:T(8,128)}), f32[128,1024]{1,0:T(8,128)}) %reduce-scatter.2.cloned.1.call-update) | async-done | bytes 524304 | tf_op jit(solution)/shard_map/reduce_scatter | solution.py:69
  436.1 1.1 fusion.13
  437.2 0.8 copy.59
  438.0 4.9 fusion.54
  443.0 25.0 %all-gather.2.cloned.1.call-done = bf16[1024,1024]{1,0:T(8,128)(2,1)} async-done(((bf16[1024,128]{1,0:T(8,128)(2,1)}), bf16[1024,1024]{1,0:T(8,128)(2,1)}) %all-gather.2.cloned.1.call-update) | async-done | bytes 2097168 | tf_op jit(solution)/shard_map/all_gather | solution.py:95
  468.0 7.1 %fusion.4 = bf16[1024,1024]{1,0:T(8,128)(2,1)} fusion(f32[32,32,1024]{2,1,0:T(8,128)} %fusion.54, bf16[1024,1024]{1,0:T(8,128)(2,1)} %all-gather.2.cloned.1.call-done, bf16[1024,1024]{1,0:T(8,128)(2,1)} %param.9), kind=kOutput, calls=%fused_computation.13 | convolution fusion | flops 2149580800 | bytes 10485760 | tf_op jit(solution)/shard_map/dot_general | solution.py:94
  475.1 1.9 convolution_convert_fusion.3
  477.0 0.6 copy.61
  477.6 105.8 %all-to-all-done.3 = bf16[64,64,1024]{2,1,0:T(8,128)(2,1)} async-done(((bf16[64,64,1024]{2,1,0:T(8,128)(2,1)}), bf16[64,64,1024]{2,1,0:T(8,128)(2,1)}, u32[]{:S(2)}, u32[]{:S(2)}) %all-to-all-start.3) | async-done | bytes 8388640 | tf_op jit(solution)/shard_map/all_to_all | solution.py:126
  583.4 12.3 %fusion.8 = bf16[3,64,1024]{2,0,1:T(4,128)(2,1)S(1)} fusion(bf16[64,64,1024]{2,1,0:T(8,128)(2,1)} %all-to-all-done.3, s32[64]{0:T(128)S(1)} %eq.42, s32[3]{0:T(128)S(1)} %iota_add_fusion), kind=kOutput, calls=%fused_computation.16 | convolution fusion | flops 25362624 | bytes 8782092 | tf_op jit(solution)/shard_map/qk,qrd->krd/dot_general | solution.py:129
  595.7 0.9 copy.60
  (29 shorter events, 1.4 us)
Async XLA Ops:
  7.2 272.1 %copy-start = (bf16[1024,1024]{1,0:T(8,128)(2,1)S(1)}, bf16[1024,1024]{1,0:T(8,128)(2,1)}, u32[]{:S(2)}) copy-start(bf16[1024,1024]{1,0:T(8,128)(2,1)} %param.8) | copy-start | bytes 6291460
  7.2 29.7 %copy-start.4 = (bf16[3,64,1024]{2,1,0:T(8,128)(2,1)S(1)}, bf16[3,64,1024]{2,1,0:T(8,128)(2,1)}, u32[]{:S(2)}) copy-start(bf16[3,64,1024]{2,1,0:T(8,128)(2,1)} %param.10) | copy-start | bytes 1179652
  9.8 14.0 %all-to-all-start = ((s32[32,2,1]{1,2,0:T(1,128)}), s32[32,2,1]{1,2,0:T(1,128)S(1)}, u32[]{:S(2)}, u32[]{:S(2)}) async-start(s32[32,2,1]{1,2,0:T(1,128)} %bitcast.5), calls=%async_computation.1 | async-start | bytes 32768 | tf_op jit(solution)/shard_map/all_to_all | solution.py:52
  28.2 33.1 %all-to-all-start.2 = ((bf16[64,64,128]{2,1,0:T(8,128)(2,1)}), bf16[64,64,128]{2,1,0:T(8,128)(2,1)}, u32[]{:S(2)}, u32[]{:S(2)}) async-start(bf16[64,64,128]{2,1,0:T(8,128)(2,1)} %copy.51), calls=%async_computation.3 | async-start | bytes 2097152 | tf_op jit(solution)/shard_map/all_to_all | solution.py:64
  53.9 26.7 %copy-start.6 = (s32[32]{0:T(128)S(1)}, s32[32]{0:T(128)}, u32[]{:S(2)}) copy-start(s32[32]{0:T(128)} %param.13) | copy-start | bytes 388
  53.9 26.7 %copy-start.5 = (s32[32]{0:T(128)S(1)}, s32[32]{0:T(128)}, u32[]{:S(2)}) copy-start(s32[32]{0:T(128)} %param.14) | copy-start | bytes 388
  53.9 29.7 %copy-start.1 = (bf16[1024,128]{1,0:T(8,128)(2,1)S(1)}, bf16[1024,128]{1,0:T(8,128)(2,1)}, u32[]{:S(2)}) copy-start(bf16[1024,128]{1,0:T(8,128)(2,1)} %param.12) | copy-start | bytes 786436
  61.3 206.8 %all-to-all-start.1 = ((bf16[64,64,1024]{2,1,0:T(8,128)(2,1)}), bf16[64,64,1024]{2,1,0:T(8,128)(2,1)}, u32[]{:S(2)}, u32[]{:S(2)}) async-start(bf16[64,64,1024]{2,1,0:T(8,128)(2,1)} %copy.49), calls=%async_computation.2 | async-start | bytes 16777216 | tf_op jit(solution)/shard_map/all_to_all | solution.py:63
  336.3 15.3 %copy-start.3 = (bf16[32,32,64]{2,1,0:T(8,128)(2,1)S(1)}, bf16[32,32,64]{2,1,0:T(8,128)(2,1)}, u32[]{:S(2)}) copy-start(bf16[32,32,64]{2,1,0:T(8,128)(2,1)} %get-tuple-element.21) | copy-start | bytes 393220
  344.7 35.8 %all-to-all-start.4 = ((bf16[64,64,128]{2,1,0:T(8,128)(2,1)}), bf16[64,64,128]{2,1,0:T(8,128)(2,1)}, u32[]{:S(2)}, u32[]{:S(2)}) async-start(bf16[64,64,128]{2,1,0:T(8,128)(2,1)} %scatter_fusion.1), calls=%async_computation.5 | async-start | bytes 2097152 | tf_op jit(solution)/shard_map/all_to_all | solution.py:127
  380.5 202.9 %all-to-all-start.3 = ((bf16[64,64,1024]{2,1,0:T(8,128)(2,1)}), bf16[64,64,1024]{2,1,0:T(8,128)(2,1)}, u32[]{:S(2)}, u32[]{:S(2)}) async-start(bf16[64,64,1024]{2,1,0:T(8,128)(2,1)} %scatter_fusion), calls=%async_computation.4 | async-start | bytes 16777216 | tf_op jit(solution)/shard_map/all_to_all | solution.py:126
  389.7 46.4 %reduce-scatter.2.cloned.1.call-start = ((), (), s32[]{:S(2)}) async-start(), calls=%async_computation.6 | async-start | bytes 4718592 | tf_op jit(solution)/shard_map/reduce_scatter | solution.py:69
  395.6 0.9 copy-start.2
  395.7 72.3 %all-gather.2.cloned.1.call-start = ((), (), s32[]{:S(2)}) async-start(), calls=%async_computation.7 | async-start | bytes 2359296 | tf_op jit(solution)/shard_map/all_gather | solution.py:95
Sparse Core Ops, SparseCore 0:
  395.8 40.2 reduce-scatter.1
  437.9 30.0 all-gather.1
where the time goes:
time: 613 us; the launch traced here: 604 us
  waiting for transfers between devices  366 us (60%)
  local copies, waits for them, and re-layouts  57.1 us (9%)
  matrix products  55.7 us (9%)
  starting transfers between devices  53.8 us (9%)
  blocking collectives  52.8 us (9%)
  between operations  14.7 us (2%)
    all_to_all x1, waiting for transfers between devices, shards(): lax.all_to_all(returned_down_panel, 'dp', split_axis=0, concat_axis=0, ti...  184 us
    all_to_all x1, waiting for transfers between devices, shards(): lax.all_to_all(send_a, 'dp', split_axis=0, concat_axis=0, tiled=True)  106 us
    psum x1, blocking collectives, shards(): down_low = lax.psum(down_part, 'mp').astype(jnp.bfloat16)  52.8 us
    reduce_scatter x1, waiting for transfers between devices, shards(): lax.psum_scatter(lax.dot_general(w_cols, tokens, (((0,), (1,)), ((), ()))...  39 us
    all_gather x1, waiting for transfers between devices, shards(): lax.all_gather(cotangent, 'mp', axis=1, tiled=True)  25 us
    all_to_all x1, starting transfers between devices, shards(): lax.all_to_all(returned_down_panel, 'dp', split_axis=0, concat_axis=0, ti...  19.3 us
    dot_general x1, matrix products, shards(): jnp.einsum('qk,qrd->krd', serve_adapters, back_a, preferred_element_type=...  12.3 us
  transfers between devices with their start and end apart: 7, of which 6 were waited for; matrix products, arithmetic and copies ran while one was open for 12% of the time, Pallas kernels for 0%

commit v1 on v0

v1 whole, which is shorter than its diff:
```python
import jax
import jax.numpy as jnp
from jax import lax
from jax.sharding import PartitionSpec as P

MOST = 2


def earlier_same(holder):
    count = holder.shape[-1]
    ids = jnp.arange(count, dtype=jnp.int32)
    same = (holder[..., :, None] == holder[..., None, :]) & (ids[:, None] > ids[None, :])
    return jnp.sum(same.astype(jnp.int32), axis=-1)


def shards(
    tokens,
    value_weight,
    adapter_down_panels,
    adapter_up_panels,
    cotangent,
    block_list_entry,
    device_tenant_list,
    tenant_location_map,
):
    rows, width_loc = tokens.shape
    stored, rank, _ = adapter_down_panels.shape
    out_loc = adapter_up_panels.shape[2]
    blocks = block_list_entry.shape[0]
    blk = rows // blocks
    n_dp = lax.axis_size("dp")
    capacity = n_dp * MOST
    me = lax.axis_index("dp")

    tenant = jnp.take(device_tenant_list, block_list_entry, mode="clip")
    location = jnp.take(tenant_location_map, tenant, mode="clip")
    holder = location // stored
    position = holder * MOST + earlier_same(holder)

    slot_ids = jnp.arange(capacity, dtype=jnp.int32)
    block_ids = jnp.arange(blocks, dtype=jnp.int32)
    source = jnp.sum(
        jnp.where(position[None, :] == slot_ids[:, None], block_ids[None, :], 0), axis=1
    )

    all_location = lax.all_gather(location, "dp", axis=0, tiled=False)
    all_holder = all_location // stored
    all_rank = earlier_same(all_holder)
    mine = all_holder == me
    slot_row = jnp.stack(
        [
            jnp.sum(jnp.where(mine & (all_rank == r), all_location % stored + 1, 0), axis=1)
            for r in range(MOST)
        ],
        axis=1,
    ).reshape(capacity) - 1
    pick = slot_row[:, None] == jnp.arange(stored, dtype=jnp.int32)[None, :]

    base_t = lax.psum_scatter(
        lax.dot_general(
            value_weight, tokens, (((0,), (1,)), ((), ())), preferred_element_type=jnp.float32
        ),
        "mp",
        scatter_dimension=0,
        tiled=True,
    )
    cot_full = lax.all_gather(cotangent, "mp", axis=1, tiled=True)
    base_bwd = lax.dot_general(
        cot_full, value_weight, (((1,), (1,)), ((), ())), preferred_element_type=jnp.float32
    )

    token_blocks = tokens.reshape(blocks, blk, width_loc)
    cot_blocks = cotangent.reshape(blocks, blk, out_loc)
    send = jnp.concatenate(
        [jnp.take(token_blocks, source, axis=0), jnp.take(cot_blocks, source, axis=0)], axis=2
    )
    recv = lax.all_to_all(send, "dp", split_axis=0, concat_axis=0, tiled=True)
    recv_rows = recv.reshape(capacity * blk, width_loc + out_loc)
    tok_recv = recv_rows[:, :width_loc]
    cot_recv = recv_rows[:, width_loc:]

    down_flat = adapter_down_panels.reshape(stored * rank, width_loc)
    up_flat = adapter_up_panels.reshape(stored * rank, out_loc)
    pick_rows = jnp.broadcast_to(pick[:, None, :, None], (capacity, blk, stored, rank)).reshape(
        capacity * blk, stored * rank
    )

    def select(all_cols):
        parts = jnp.where(pick_rows, all_cols, 0.0).reshape(capacity * blk, stored, rank)
        return jnp.sum(parts, axis=1)

    down_part = select(
        lax.dot_general(tok_recv, down_flat, (((1,), (1,)), ((), ())), preferred_element_type=jnp.float32)
    )
    up_part = select(
        lax.dot_general(cot_recv, up_flat, (((1,), (1,)), ((), ())), preferred_element_type=jnp.float32)
    )
    both = lax.psum(jnp.stack([down_part, up_part]), "mp").astype(jnp.bfloat16)
    down_low = both[0]
    up_grad = both[1]

    def spread(small):
        wide = jnp.broadcast_to(small[:, None, :], (capacity * blk, stored, rank)).reshape(
            capacity * blk, stored * rank
        )
        return jnp.where(pick_rows, wide, jnp.zeros_like(wide))

    down_wide = spread(down_low)
    up_wide = spread(up_grad)

    adapter_out = jnp.dot(down_wide, up_flat, preferred_element_type=jnp.float32)
    adapter_bwd = jnp.dot(up_wide, down_flat, preferred_element_type=jnp.float32)
    back_send = jnp.concatenate(
        [adapter_bwd.astype(jnp.bfloat16), adapter_out.astype(jnp.bfloat16)], axis=1
    ).reshape(capacity, blk, width_loc + out_loc)

    grad_a = lax.dot_general(
        up_wide, tok_recv, (((0,), (0,)), ((), ())), preferred_element_type=jnp.float32
    ).astype(jnp.bfloat16).reshape(stored, rank, width_loc)
    grad_b = lax.dot_general(
        down_wide, cot_recv, (((0,), (0,)), ((), ())), preferred_element_type=jnp.float32
    ).astype(jnp.bfloat16).reshape(stored, rank, out_loc)

    back = lax.all_to_all(back_send, "dp", split_axis=0, concat_axis=0, tiled=True)
    mine_back = jnp.take(back, position, axis=0).reshape(rows, width_loc + out_loc)

    values = (base_t.T + mine_back[:, width_loc:].astype(jnp.float32)).astype(jnp.bfloat16)
    token_gradient = (base_bwd + mine_back[:, :width_loc].astype(jnp.float32)).astype(jnp.bfloat16)
    return (values, token_gradient, grad_a, grad_b)


def solution(mesh):
    in_specs = (
        P("dp", "mp"),
        P("mp", None),
        P("dp", None, "mp"),
        P("dp", None, "mp"),
        P("dp", "mp"),
        P("dp"),
        P("dp"),
        P(),
    )
    out_specs = (P("dp", "mp"), P("dp", "mp"), P("dp", None, "mp"), P("dp", None, "mp"))
    return jax.shard_map(shards, mesh=mesh, in_specs=in_specs, out_specs=out_specs, check_vma=False)
```

time: 613 us -> 389 us (0.63)
  the two profiles are of different devices: /device:TPU:127 before, /device:TPU:1 now
where the time goes in v1:
time: 389 us; the launch traced here: 385 us
  blocking collectives  159 us (41%)
  waiting for transfers between devices  85.8 us (22%)
  local copies, waits for them, and re-layouts  50.3 us (13%)
  matrix products  29.7 us (8%)
  other arithmetic  24.9 us (6%)
  starting transfers between devices  20.6 us (5%)
  between operations  15 us (4%)
    unnamed x1, blocking collectives  105 us
    all_to_all x1, waiting for transfers between devices, shards(): lax.all_to_all(back_send, 'dp', split_axis=0, concat_axis=0, tiled=True)  85.1 us
    psum x1, blocking collectives, shards(): both = lax.psum(jnp.stack([down_part, up_part]), 'mp').astype(jnp.bfloat16)  53.5 us
    all_to_all x1, starting transfers between devices, shards(): recv = lax.all_to_all(send, 'dp', split_axis=0, concat_axis=0, tiled=True)  12.1 us
    select_n x2, local copies, waits for them, and re-layouts, spread(): return jnp.where(pick_rows, wide, jnp.zeros_like(wide))  9.06 us
    gather x2, local copies, waits for them, and re-layouts, shards(): jnp.take(back, position, axis=0).reshape(rows, width_loc + out_loc)  8.81 us
    all_to_all x1, starting transfers between devices, shards(): lax.all_to_all(back_send, 'dp', split_axis=0, concat_axis=0, tiled=True)  8.14 us
  transfers between devices with their start and end apart: 4, of which 1 were waited for; matrix products, arithmetic and copies ran while one was open for 23% of the time, Pallas kernels for 0%

profile of v1, /device:TPU:1, one launch (start us, length us, event | category | flops | bytes accessed | tf_op | source)
XLA Modules:
  0.0 385.0 jit_solution(8853946348867833675)
XLA Ops:
  7.2 0.8 pad_clamp_fusion.3
  8.0 1.4 gather_fusion
  9.3 1.4 gather_fusion.1
  10.7 0.6 add_select_fusion.2
  11.6 1.6 gather_fusion.3
  13.2 2.7 gather_fusion.2
  16.1 2.6 broadcast_select_fusion
  18.7 2.8 pad_maximum_fusion
  21.5 12.1 %all-to-all-start = ((bf16[64,32,1152]{2,1,0:T(8,128)(2,1)}), bf16[64,32,1152]{2,1,0:T(8,128)(2,1)}, u32[]{:S(2)}, u32[]{:S(2)}) async-start(bf16[64,32,1152]{2,1,0:T(8,128)(2,1)} %pad_maximum_fusion), calls=%async_computation.1 | async-start | bytes 9437184 | tf_op jit(solution)/shard_map/all_to_all | solution.py:77
  33.7 0.7 all-gather.3.cloned.1.call-update
  34.4 0.6 dynamic-slice
  35.9 105.5 %all-reduce = s32[1024]{0:T(1024)S(1)} all-reduce(s32[1024]{0:T(1024)S(1)} %dynamic-update-slice), channel_id=2, replica_groups=mesh['dp'=32,'mp'=8] {'dp'}, use_global_device_ids=true, to_apply=%add | all-reduce | flops 1024 | bytes 8192
  141.7 0.8 convert_reduce_fusion
  142.9 0.6 broadcast_in_dim.109
  143.5 2.5 reshape.219
  146.0 1.7 copy.49
  147.7 2.6 convolution_select_fusion
  150.2 4.9 %fusion.4 = f32[2048,192]{0,1:T(8,128)} fusion(pred[2048,192]{0,1:T(32,128)(4,1)S(1)} %copy.49, bf16[192,1024]{1,0:T(8,128)(2,1)S(1)} %bitcast.72, bf16[2048,1152]{1,0:T(8,128)(2,1)} %bitcast.8), kind=kOutput, calls=%fused_computation.15 | convolution fusion | flops 805699584 | bytes 6553600 | tf_op jit(solution)/shard_map/dot_general | solution.py:93
  155.1 2.4 reduce_sum.74
  157.5 2.3 reduce_sum.73
  159.8 1.3 pad_maximum_fusion.2
  161.1 53.5 %all-reduce.2 = bf16[2,2048,64]{1,2,0:T(8,128)(2,1)} all-reduce(f32[2,2048,64]{1,2,0:T(8,128)S(1)} %pad_maximum_fusion.2), channel_id=1, replica_groups=mesh['dp'=32,'mp'=8] {'mp'}, use_global_device_ids=true, to_apply=%region_8.9 | all-reduce | flops 262144 | bytes 1572864 | tf_op jit(solution)/shard_map/psum | solution.py:98
  214.6 1.9 slice_bitcast_fusion
  216.8 0.3 copy.51
  217.1 3.6 broadcast_select_fusion.3
  220.7 4.1 %select_n.147 = bf16[2048,192]{1,0:T(8,128)(2,1)S(1)} reshape(bf16[64,32,3,64]{3,2,1,0:T(4,128)(2,1)} %get-tuple-element.36) | data formatting | bytes 1572864 | tf_op jit(solution)/shard_map/jit(_where)/select_n | solution.py:106
  224.8 4.9 %select_n.149 = bf16[2048,192]{1,0:T(8,128)(2,1)} reshape(bf16[64,32,3,64]{3,2,1,0:T(4,128)(2,1)} %get-tuple-element.37) | data formatting | bytes 1572864 | tf_op jit(solution)/shard_map/jit(_where)/select_n | solution.py:106
  229.8 1.7 convolution_convert_fusion.1
  231.5 1.3 convolution_convert_fusion
  232.8 2.5 pad_maximum_fusion.1
  235.4 6.7 %copy.53 = bf16[2048,1152]{1,0:T(8,128)(2,1)} copy(bf16[2048,1152]{0,1:T(8,128)(2,1)} %pad_maximum_fusion.1) | data formatting | bytes 9437184 | tf_op jit(solution)/shard_map/concatenate | solution.py:113
  242.1 8.1 %all-to-all-start.1 = ((bf16[64,32,1152]{2,1,0:T(8,128)(2,1)}), bf16[64,32,1152]{2,1,0:T(8,128)(2,1)}, u32[]{:S(2)}, u32[]{:S(2)}) async-start(bf16[64,32,1152]{2,1,0:T(8,128)(2,1)} %bitcast.61), calls=%async_computation.2 | async-start | bytes 9437184 | tf_op jit(solution)/shard_map/all_to_all | solution.py:124
  250.5 5.9 %fusion.24 = f32[1024,1024]{1,0:T(8,128)} fusion(bf16[1024,1024]{1,0:T(8,128)(2,1)} %param.9, bf16[1024,1024]{1,0:T(8,128)(2,1)S(1)} %copy-done), kind=kOutput, calls=%fused_computation.71 | convolution fusion | flops 2147483648 | bytes 8388608 | tf_op jit(solution)/shard_map/dot_general | solution.py:60
  256.6 0.4 copy-done.5
  257.1 1.0 broadcast_in_dim.125
  258.1 1.3 copy.57
  259.4 1.0 broadcast_in_dim.123
  260.5 1.3 copy.56
  261.8 2.5 convolution_convert_fusion.2
  264.3 4.3 %fusion.7 = bf16[192,1024]{1,0:T(8,128)(2,1)} fusion(bf16[2048,1152]{1,0:T(8,128)(2,1)} %bitcast.8, pred[2048,192]{1,0:T(32,128)(4,1)S(1)} %copy-done.1, bf16[2048,192]{1,0:T(8,128)(2,1)} %copy.56), kind=kOutput, calls=%fused_computation.20 | convolution fusion | flops 805896192 | bytes 6029312 | tf_op jit(solution)/shard_map/dot_general | solution.py:117
  268.5 85.1 %all-to-all-done.1 = bf16[64,32,1152]{2,1,0:T(8,128)(2,1)} async-done(((bf16[64,32,1152]{2,1,0:T(8,128)(2,1)}), bf16[64,32,1152]{2,1,0:T(8,128)(2,1)}, u32[]{:S(2)}, u32[]{:S(2)}) %all-to-all-start.1) | async-done | bytes 4718624 | tf_op jit(solution)/shard_map/all_to_all | solution.py:124
  353.6 4.5 %gather_fusion.4 = bf16[32,32,1152]{2,1,0:T(8,128)(2,1)} fusion(bf16[64,32,1152]{2,1,0:T(8,128)(2,1)} %all-to-all-done.1, s32[1024]{0:T(1024)S(1)} %pad_clamp_fusion), kind=kCustom, calls=%fused_computation.4 | custom fusion | bytes 4718720 | tf_op jit(solution)/shard_map/jit(_take)/gather | solution.py:125
  358.1 4.3 %copy.54 = bf16[1024,1152]{0,1:T(8,128)(2,1)} copy(bf16[1024,1152]{1,0:T(8,128)(2,1)} %bitcast.62) | data formatting | bytes 4718592 | tf_op jit(solution)/shard_map/jit(_take)/gather | solution.py:125
  362.4 3.3 broadcast_select_fusion.1
  365.7 6.6 %add_convert_fusion = bf16[1024,1024]{0,1:T(8,128)(2,1)} fusion(bf16[1024,1152]{0,1:T(8,128)(2,1)} %broadcast_select_fusion.1, bf16[1024,1024]{1,0:T(8,128)(2,1)} %all-gather.3.cloned.1.call-done, bf16[1024,1024]{1,0:T(8,128)(2,1)} %param.9), kind=kOutput, calls=%fused_computation.7 | convolution fusion | flops 2150629376 | bytes 8388608 | tf_op jit(solution)/shard_map/dot_general | solution.py:68
  372.2 3.9 %copy.59 = bf16[1024,1024]{1,0:T(8,128)(2,1)} copy(bf16[1024,1024]{0,1:T(8,128)(2,1)} %add_convert_fusion) | data formatting | bytes 4194304
  376.2 1.2 fusion.12
  377.3 0.8 copy.58
  (48 shorter events, 2.2 us)
Async XLA Ops:
  7.2 6.0 %copy-start = (bf16[1024,1024]{1,0:T(8,128)(2,1)S(1)}, bf16[1024,1024]{1,0:T(8,128)(2,1)}, u32[]{:S(2)}) copy-start(bf16[1024,1024]{1,0:T(8,128)(2,1)} %param.8) | copy-start | bytes 6291460
  10.7 25.0 %copy-start.4 = (s32[32]{0:T(128)}, s32[32]{0:T(128)S(1)}, u32[]{:S(2)}) copy-start(s32[32]{0:T(128)S(1)} %gather_fusion.1) | copy-start | bytes 388
  21.5 12.9 %copy-start.7 = (u32[256]{0:T(256)S(1)}, u32[256]{0:T(256)}, u32[]{:S(2)}) copy-start(u32[256]{0:T(256)} %constant.90) | copy-start | bytes 3076
  21.5 126.1 %all-to-all-start = ((bf16[64,32,1152]{2,1,0:T(8,128)(2,1)}), bf16[64,32,1152]{2,1,0:T(8,128)(2,1)}, u32[]{:S(2)}, u32[]{:S(2)}) async-start(bf16[64,32,1152]{2,1,0:T(8,128)(2,1)} %pad_maximum_fusion), calls=%async_computation.1 | async-start | bytes 9437184 | tf_op jit(solution)/shard_map/all_to_all | solution.py:77
  33.7 116.6 %copy-start.2 = (bf16[3,64,1024]{2,1,0:T(8,128)(2,1)S(1)}, bf16[3,64,1024]{2,1,0:T(8,128)(2,1)}, u32[]{:S(2)}) copy-start(bf16[3,64,1024]{2,1,0:T(8,128)(2,1)} %param.10) | copy-start | bytes 1179652
  33.7 332.0 %all-gather.3.cloned.1.call-start = ((), (), s32[]{:S(2)}) async-start(), calls=%async_computation.4 | async-start | bytes 2359296 | tf_op jit(solution)/shard_map/all_gather | solution.py:67
  220.7 10.8 %copy-start.3 = (bf16[3,64,1024]{2,1,0:T(8,128)(2,1)S(1)}, bf16[3,64,1024]{2,1,0:T(8,128)(2,1)}, u32[]{:S(2)}) copy-start(bf16[3,64,1024]{2,1,0:T(8,128)(2,1)} %param.10) | copy-start | bytes 1179652
  242.1 111.5 %all-to-all-start.1 = ((bf16[64,32,1152]{2,1,0:T(8,128)(2,1)}), bf16[64,32,1152]{2,1,0:T(8,128)(2,1)}, u32[]{:S(2)}, u32[]{:S(2)}) async-start(bf16[64,32,1152]{2,1,0:T(8,128)(2,1)} %bitcast.61), calls=%async_computation.2 | async-start | bytes 9437184 | tf_op jit(solution)/shard_map/all_to_all | solution.py:124
  250.2 125.9 %reduce-scatter.2.cloned.1.call-start = ((), (), s32[]{:S(2)}) async-start(), calls=%async_computation.3 | async-start | bytes 4718592 | tf_op jit(solution)/shard_map/reduce_scatter | solution.py:59
  256.4 0.6 copy-start.5
  256.4 0.6 copy-start.6
  256.4 5.3 %copy-start.1 = (pred[2048,192]{1,0:T(32,128)(4,1)S(1)}, pred[2048,192]{1,0:T(32,128)(4,1)}, u32[]{:S(2)}) copy-start(pred[2048,192]{1,0:T(32,128)(4,1)} %reshape.219) | copy-start | bytes 1179652
Sparse Core Ops, SparseCore 0:
  36.3 31.8 all-gather.2
  256.6 39.9 reduce-scatter.1

commit v2 on v1

--- a/solution.py
+++ b/solution.py
@@ -95,7 +95,14 @@
     up_part = select(
         lax.dot_general(cot_recv, up_flat, (((1,), (1,)), ((), ())), preferred_element_type=jnp.float32)
     )
-    both = lax.psum(jnp.stack([down_part, up_part]), "mp").astype(jnp.bfloat16)
+    both = lax.all_gather(
+        lax.psum_scatter(jnp.stack([down_part, up_part]), "mp", scatter_dimension=1, tiled=True).astype(
+            jnp.bfloat16
+        ),
+        "mp",
+        axis=1,
+        tiled=True,
+    )
     down_low = both[0]
     up_grad = both[1]
 

time: 389 us -> 389 us (level)
  blocking collectives: 159 us -> 122 us
  waiting for transfers between devices: 85.8 us -> 122 us
    psum x1 -> x0, blocking collectives: 53.5 us -> none  [shards(): both = lax.psum(jnp.stack([down_part, up_part]), 'mp').astype(jnp.bfloat16)]
    reduce_scatter x0 -> x1, waiting for transfers between devices: none -> 34.4 us  [shards(): lax.psum_scatter(jnp.stack([down_part, up_part]), 'mp', scatter_dimension...]
    all_gather x0 -> x1, blocking collectives: none -> 16.3 us  [shards(): lax.all_gather(lax.psum_scatter(jnp.stack([down_part, up_part]), 'mp', sc...]
  transfers between devices with their start and end apart: 4 -> 5, of which waited for: 1 -> 2; matrix products, arithmetic and copies ran while one was open for 23% -> 19% of each run, Pallas kernels for 0% -> 0%
where the time goes in v2:
time: 389 us; the launch traced here: 384 us
  blocking collectives  122 us (31%)
  waiting for transfers between devices  122 us (31%)
  local copies, waits for them, and re-layouts  49.4 us (13%)
  matrix products  29.7 us (8%)
  other arithmetic  23.9 us (6%)
  starting transfers between devices  22.2 us (6%)
  between operations  14.7 us (4%)
    unnamed x1, blocking collectives  106 us
    all_to_all x1, waiting for transfers between devices, shards(): lax.all_to_all(back_send, 'dp', split_axis=0, concat_axis=0, tiled=True)  86.6 us
    reduce_scatter x1, waiting for transfers between devices, shards(): lax.psum_scatter(jnp.stack([down_part, up_part]), 'mp', scatter_dimension...  34.4 us
    all_gather x1, blocking collectives, shards(): lax.all_gather(lax.psum_scatter(jnp.stack([down_part, up_part]), 'mp', sc...  16.3 us
    all_to_all x1, starting transfers between devices, shards(): recv = lax.all_to_all(send, 'dp', split_axis=0, concat_axis=0, tiled=True)  12.1 us
    all_to_all x1, starting transfers between devices, shards(): lax.all_to_all(back_send, 'dp', split_axis=0, concat_axis=0, tiled=True)  9.72 us
    select_n x2, local copies, waits for them, and re-layouts, spread(): return jnp.where(pick_rows, wide, jnp.zeros_like(wide))  9.17 us
    gather x2, local copies, waits for them, and re-layouts, shards(): jnp.take(back, position, axis=0).reshape(rows, width_loc + out_loc)  8.81 us
  transfers between devices with their start and end apart: 5, of which 2 were waited for; matrix products, arithmetic and copies ran while one was open for 19% of the time, Pallas kernels for 0%

profile of v2, /device:TPU:1, one launch (start us, length us, event | category | flops | bytes accessed | tf_op | source)
XLA Modules:
  0.0 383.9 jit_solution(7027239868767776627)
XLA Ops:
  7.2 0.8 pad_clamp_fusion.3
  8.0 1.4 gather_fusion
  9.3 1.4 gather_fusion.1
  10.7 0.5 add_select_fusion.2
  11.6 1.6 gather_fusion.3
  13.2 2.7 gather_fusion.2
  16.1 2.6 broadcast_select_fusion
  18.7 2.8 pad_maximum_fusion
  21.5 12.1 %all-to-all-start = ((bf16[64,32,1152]{2,1,0:T(8,128)(2,1)}), bf16[64,32,1152]{2,1,0:T(8,128)(2,1)}, u32[]{:S(2)}, u32[]{:S(2)}) async-start(bf16[64,32,1152]{2,1,0:T(8,128)(2,1)} %pad_maximum_fusion), calls=%async_computation.1 | async-start | bytes 9437184 | tf_op jit(solution)/shard_map/all_to_all | solution.py:77
  33.7 0.6 dynamic-slice
  35.2 106.1 %all-reduce = s32[1024]{0:T(1024)S(1)} all-reduce(s32[1024]{0:T(1024)S(1)} %dynamic-update-slice), channel_id=2, replica_groups=mesh['dp'=32,'mp'=8] {'dp'}, use_global_device_ids=true, to_apply=%add | all-reduce | flops 1024 | bytes 8192
  141.6 0.8 convert_reduce_fusion
  142.8 0.6 broadcast_in_dim.109
  143.5 2.5 reshape.219
  145.9 1.7 copy.49
  147.6 2.6 convolution_select_fusion
  150.2 4.9 %fusion.4 = f32[2048,192]{0,1:T(8,128)} fusion(pred[2048,192]{0,1:T(32,128)(4,1)S(1)} %copy.49, bf16[192,1024]{1,0:T(8,128)(2,1)S(1)} %bitcast.72, bf16[2048,1152]{1,0:T(8,128)(2,1)} %bitcast.8), kind=kOutput, calls=%fused_computation.15 | convolution fusion | flops 805699584 | bytes 6553600 | tf_op jit(solution)/shard_map/dot_general | solution.py:93
  155.1 1.6 reduce_sum.74
  156.6 1.6 reduce_sum.73
  158.2 1.0 pad_maximum_fusion.2
  159.3 0.7 all-gather.3.cloned.1.call-update
  160.0 34.4 %reduce-scatter.5.cloned.1.call-done = f32[2,256,64]{1,2,0:T(8,128)} async-done(((f32[2,2048,64]{1,2,0:T(8,128)}), f32[2,256,64]{1,2,0:T(8,128)}) %reduce-scatter.5.cloned.1.call-update) | async-done | bytes 131088 | tf_op jit(solution)/shard_map/reduce_scatter | solution.py:99
  194.4 0.9 convert_element_type.35
  195.3 16.3 %all_gather.11 = bf16[2,2048,64]{1,2,0:T(8,128)(2,1)S(1)} all-gather(bf16[2,256,64]{1,2,0:T(8,128)(2,1)S(1)} %convert_element_type.35), channel_id=1, replica_groups=mesh['dp'=32,'mp'=8] {'mp'}, dimensions={1}, use_global_device_ids=true | all-gather | bytes 589824 | tf_op jit(solution)/shard_map/all_gather | solution.py:98
  211.6 0.9 slice_bitcast_fusion
  213.1 3.6 broadcast_select_fusion.3
  216.7 4.2 %select_n.147 = bf16[2048,192]{1,0:T(8,128)(2,1)S(1)} reshape(bf16[64,32,3,64]{3,2,1,0:T(4,128)(2,1)} %get-tuple-element.36) | data formatting | bytes 1572864 | tf_op jit(solution)/shard_map/jit(_where)/select_n | solution.py:113
  220.9 4.9 %select_n.149 = bf16[2048,192]{1,0:T(8,128)(2,1)} reshape(bf16[64,32,3,64]{3,2,1,0:T(4,128)(2,1)} %get-tuple-element.37) | data formatting | bytes 1572864 | tf_op jit(solution)/shard_map/jit(_where)/select_n | solution.py:113
  225.9 1.7 convolution_convert_fusion.1
  227.6 1.3 convolution_convert_fusion
  228.9 2.5 pad_maximum_fusion.1
  231.5 6.7 %copy.53 = bf16[2048,1152]{1,0:T(8,128)(2,1)} copy(bf16[2048,1152]{0,1:T(8,128)(2,1)} %pad_maximum_fusion.1) | data formatting | bytes 9437184 | tf_op jit(solution)/shard_map/concatenate | solution.py:120
  238.2 9.7 %all-to-all-start.1 = ((bf16[64,32,1152]{2,1,0:T(8,128)(2,1)}), bf16[64,32,1152]{2,1,0:T(8,128)(2,1)}, u32[]{:S(2)}, u32[]{:S(2)}) async-start(bf16[64,32,1152]{2,1,0:T(8,128)(2,1)} %bitcast.61), calls=%async_computation.3 | async-start | bytes 9437184 | tf_op jit(solution)/shard_map/all_to_all | solution.py:131
  248.2 5.9 %fusion.24 = f32[1024,1024]{1,0:T(8,128)} fusion(bf16[1024,1024]{1,0:T(8,128)(2,1)} %param.9, bf16[1024,1024]{1,0:T(8,128)(2,1)S(1)} %copy-done), kind=kOutput, calls=%fused_computation.71 | convolution fusion | flops 2147483648 | bytes 8388608 | tf_op jit(solution)/shard_map/dot_general | solution.py:60
  254.8 1.0 broadcast_in_dim.125
  255.8 1.3 copy.57
  257.1 1.0 broadcast_in_dim.123
  258.2 1.3 copy.56
  259.5 2.5 convolution_convert_fusion.2
  261.9 4.3 %fusion.7 = bf16[192,1024]{1,0:T(8,128)(2,1)} fusion(bf16[2048,1152]{1,0:T(8,128)(2,1)} %bitcast.8, pred[2048,192]{1,0:T(32,128)(4,1)S(1)} %copy-done.1, bf16[2048,192]{1,0:T(8,128)(2,1)} %copy.56), kind=kOutput, calls=%fused_computation.20 | convolution fusion | flops 805896192 | bytes 6029312 | tf_op jit(solution)/shard_map/dot_general | solution.py:124
  266.2 86.6 %all-to-all-done.1 = bf16[64,32,1152]{2,1,0:T(8,128)(2,1)} async-done(((bf16[64,32,1152]{2,1,0:T(8,128)(2,1)}), bf16[64,32,1152]{2,1,0:T(8,128)(2,1)}, u32[]{:S(2)}, u32[]{:S(2)}) %all-to-all-start.1) | async-done | bytes 4718624 | tf_op jit(solution)/shard_map/all_to_all | solution.py:131
  352.8 4.5 %gather_fusion.4 = bf16[32,32,1152]{2,1,0:T(8,128)(2,1)} fusion(bf16[64,32,1152]{2,1,0:T(8,128)(2,1)} %all-to-all-done.1, s32[1024]{0:T(1024)S(1)} %pad_clamp_fusion), kind=kCustom, calls=%fused_computation.4 | custom fusion | bytes 4718720 | tf_op jit(solution)/shard_map/jit(_take)/gather | solution.py:132
  357.4 4.3 %copy.54 = bf16[1024,1152]{0,1:T(8,128)(2,1)} copy(bf16[1024,1152]{1,0:T(8,128)(2,1)} %bitcast.62) | data formatting | bytes 4718592 | tf_op jit(solution)/shard_map/jit(_take)/gather | solution.py:132
  361.6 3.3 broadcast_select_fusion.1
  364.9 6.6 %add_convert_fusion = bf16[1024,1024]{0,1:T(8,128)(2,1)} fusion(bf16[1024,1152]{0,1:T(8,128)(2,1)} %broadcast_select_fusion.1, bf16[1024,1024]{1,0:T(8,128)(2,1)} %all-gather.3.cloned.1.call-done, bf16[1024,1024]{1,0:T(8,128)(2,1)} %param.9), kind=kOutput, calls=%fused_computation.7 | convolution fusion | flops 2150629376 | bytes 8388608 | tf_op jit(solution)/shard_map/dot_general | solution.py:68
  371.5 3.9 %copy.59 = bf16[1024,1024]{1,0:T(8,128)(2,1)} copy(bf16[1024,1024]{0,1:T(8,128)(2,1)} %add_convert_fusion) | data formatting | bytes 4194304
  375.4 1.2 fusion.12
  376.6 0.8 copy.58
  (52 shorter events, 3.0 us)
Async XLA Ops:
  7.2 6.0 %copy-start = (bf16[1024,1024]{1,0:T(8,128)(2,1)S(1)}, bf16[1024,1024]{1,0:T(8,128)(2,1)}, u32[]{:S(2)}) copy-start(bf16[1024,1024]{1,0:T(8,128)(2,1)} %param.8) | copy-start | bytes 6291460
  10.7 24.3 %copy-start.4 = (s32[32]{0:T(128)}, s32[32]{0:T(128)S(1)}, u32[]{:S(2)}) copy-start(s32[32]{0:T(128)S(1)} %gather_fusion.1) | copy-start | bytes 388
  21.5 12.2 %copy-start.7 = (u32[256]{0:T(256)S(1)}, u32[256]{0:T(256)}, u32[]{:S(2)}) copy-start(u32[256]{0:T(256)} %constant.90) | copy-start | bytes 3076
  21.5 126.1 %all-to-all-start = ((bf16[64,32,1152]{2,1,0:T(8,128)(2,1)}), bf16[64,32,1152]{2,1,0:T(8,128)(2,1)}, u32[]{:S(2)}, u32[]{:S(2)}) async-start(bf16[64,32,1152]{2,1,0:T(8,128)(2,1)} %pad_maximum_fusion), calls=%async_computation.1 | async-start | bytes 9437184 | tf_op jit(solution)/shard_map/all_to_all | solution.py:77
  33.6 116.6 %copy-start.2 = (bf16[3,64,1024]{2,1,0:T(8,128)(2,1)S(1)}, bf16[3,64,1024]{2,1,0:T(8,128)(2,1)}, u32[]{:S(2)}) copy-start(bf16[3,64,1024]{2,1,0:T(8,128)(2,1)} %param.10) | copy-start | bytes 1179652
  33.6 160.8 %reduce-scatter.5.cloned.1.call-start = ((), (), s32[]{:S(2)}) async-start(), calls=%async_computation.5 | async-start | bytes 1179648 | tf_op jit(solution)/shard_map/reduce_scatter | solution.py:99
  159.3 205.6 %all-gather.3.cloned.1.call-start = ((), (), s32[]{:S(2)}) async-start(), calls=%async_computation.6 | async-start | bytes 2359296 | tf_op jit(solution)/shard_map/all_gather | solution.py:67
  216.7 10.9 %copy-start.3 = (bf16[3,64,1024]{2,1,0:T(8,128)(2,1)S(1)}, bf16[3,64,1024]{2,1,0:T(8,128)(2,1)}, u32[]{:S(2)}) copy-start(bf16[3,64,1024]{2,1,0:T(8,128)(2,1)} %param.10) | copy-start | bytes 1179652
  238.2 114.6 %all-to-all-start.1 = ((bf16[64,32,1152]{2,1,0:T(8,128)(2,1)}), bf16[64,32,1152]{2,1,0:T(8,128)(2,1)}, u32[]{:S(2)}, u32[]{:S(2)}) async-start(bf16[64,32,1152]{2,1,0:T(8,128)(2,1)} %bitcast.61), calls=%async_computation.3 | async-start | bytes 9437184 | tf_op jit(solution)/shard_map/all_to_all | solution.py:131
  247.9 127.5 %reduce-scatter.3.cloned.1.call-start = ((), (), s32[]{:S(2)}) async-start(), calls=%async_computation.4 | async-start | bytes 4718592 | tf_op jit(solution)/shard_map/reduce_scatter | solution.py:59
  254.1 0.7 copy-start.5
  254.1 0.7 copy-start.6
  254.1 5.4 %copy-start.1 = (pred[2048,192]{1,0:T(32,128)(4,1)S(1)}, pred[2048,192]{1,0:T(32,128)(4,1)}, u32[]{:S(2)}) copy-start(pred[2048,192]{1,0:T(32,128)(4,1)} %reshape.219) | copy-start | bytes 1179652
Sparse Core Ops, SparseCore 0:
  159.4 34.9 reduce-scatter.4
  196.3 31.5 all-gather.2
  254.3 37.8 reduce-scatter.2

commit v3 on v1

--- a/solution.py
+++ b/solution.py
@@ -54,7 +54,6 @@
         ],
         axis=1,
     ).reshape(capacity) - 1
-    pick = slot_row[:, None] == jnp.arange(stored, dtype=jnp.int32)[None, :]
 
     base_t = lax.psum_scatter(
         lax.dot_general(
@@ -74,54 +73,65 @@
     send = jnp.concatenate(
         [jnp.take(token_blocks, source, axis=0), jnp.take(cot_blocks, source, axis=0)], axis=2
     )
-    recv = lax.all_to_all(send, "dp", split_axis=0, concat_axis=0, tiled=True)
-    recv_rows = recv.reshape(capacity * blk, width_loc + out_loc)
-    tok_recv = recv_rows[:, :width_loc]
-    cot_recv = recv_rows[:, width_loc:]
-
     down_flat = adapter_down_panels.reshape(stored * rank, width_loc)
     up_flat = adapter_up_panels.reshape(stored * rank, out_loc)
-    pick_rows = jnp.broadcast_to(pick[:, None, :, None], (capacity, blk, stored, rank)).reshape(
-        capacity * blk, stored * rank
-    )
+    send = send.reshape(n_dp, MOST, blk, width_loc + out_loc)
+    slot_row = slot_row.reshape(n_dp, MOST)
+    backs = []
+    grad_a = 0.0
+    grad_b = 0.0
+    for r in range(MOST):
+        recv = lax.all_to_all(send[:, r], "dp", split_axis=0, concat_axis=0, tiled=True)
+        recv_rows = recv.reshape(n_dp * blk, width_loc + out_loc)
+        tok_recv = recv_rows[:, :width_loc]
+        cot_recv = recv_rows[:, width_loc:]
+        pick = slot_row[:, r][:, None] == jnp.arange(stored, dtype=jnp.int32)[None, :]
+        pick_rows = jnp.broadcast_to(pick[:, None, :, None], (n_dp, blk, stored, rank)).reshape(
+            n_dp * blk, stored * rank
+        )
 
-    def select(all_cols):
-        parts = jnp.where(pick_rows, all_cols, 0.0).reshape(capacity * blk, stored, rank)
-        return jnp.sum(parts, axis=1)
+        def select(all_cols):
+            parts = jnp.where(pick_rows, all_cols, 0.0).reshape(n_dp * blk, stored, rank)
+            return jnp.sum(parts, axis=1)
 
-    down_part = select(
-        lax.dot_general(tok_recv, down_flat, (((1,), (1,)), ((), ())), preferred_element_type=jnp.float32)
-    )
-    up_part = select(
-        lax.dot_general(cot_recv, up_flat, (((1,), (1,)), ((), ())), preferred_element_type=jnp.float32)
-    )
-    both = lax.psum(jnp.stack([down_part, up_part]), "mp").astype(jnp.bfloat16)
-    down_low = both[0]
-    up_grad = both[1]
+        down_part = select(
+            lax.dot_general(tok_recv, down_flat, (((1,), (1,)), ((), ())), preferred_element_type=jnp.float32)
+        )
+        up_part = select(
+            lax.dot_general(cot_recv, up_flat, (((1,), (1,)), ((), ())), preferred_element_type=jnp.float32)
+        )
+        both = lax.all_gather(
+            lax.psum_scatter(jnp.stack([down_part, up_part]), "mp", scatter_dimension=1, tiled=True).astype(
+                jnp.bfloat16
+            ),
+            "mp",
+            axis=1,
+            tiled=True,
+        )
 
-    def spread(small):
-        wide = jnp.broadcast_to(small[:, None, :], (capacity * blk, stored, rank)).reshape(
-            capacity * blk, stored * rank
+        def spread(small):
+            wide = jnp.broadcast_to(small[:, None, :], (n_dp * blk, stored, rank)).reshape(
+                n_dp * blk, stored * rank
+            )
+            return jnp.where(pick_rows, wide, jnp.zeros_like(wide))
+
+        down_wide = spread(both[0])
+        up_wide = spread(both[1])
+        adapter_out = jnp.dot(down_wide, up_flat, preferred_element_type=jnp.float32)
+        adapter_bwd = jnp.dot(up_wide, down_flat, preferred_element_type=jnp.float32)
+        back_send = jnp.concatenate(
+            [adapter_bwd.astype(jnp.bfloat16), adapter_out.astype(jnp.bfloat16)], axis=1
+        ).reshape(n_dp, blk, width_loc + out_loc)
+        backs.append(lax.all_to_all(back_send, "dp", split_axis=0, concat_axis=0, tiled=True))
+        grad_a = grad_a + lax.dot_general(
+            up_wide, tok_recv, (((0,), (0,)), ((), ())), preferred_element_type=jnp.float32
         )
-        return jnp.where(pick_rows, wide, jnp.zeros_like(wide))
-
-    down_wide = spread(down_low)
-    up_wide = spread(up_grad)
-
-    adapter_out = jnp.dot(down_wide, up_flat, preferred_element_type=jnp.float32)
-    adapter_bwd = jnp.dot(up_wide, down_flat, preferred_element_type=jnp.float32)
-    back_send = jnp.concatenate(
-        [adapter_bwd.astype(jnp.bfloat16), adapter_out.astype(jnp.bfloat16)], axis=1
-    ).reshape(capacity, blk, width_loc + out_loc)
-
-    grad_a = lax.dot_general(
-        up_wide, tok_recv, (((0,), (0,)), ((), ())), preferred_element_type=jnp.float32
-    ).astype(jnp.bfloat16).reshape(stored, rank, width_loc)
-    grad_b = lax.dot_general(
-        down_wide, cot_recv, (((0,), (0,)), ((), ())), preferred_element_type=jnp.float32
-    ).astype(jnp.bfloat16).reshape(stored, rank, out_loc)
-
-    back = lax.all_to_all(back_send, "dp", split_axis=0, concat_axis=0, tiled=True)
+        grad_b = grad_b + lax.dot_general(
+            down_wide, cot_recv, (((0,), (0,)), ((), ())), preferred_element_type=jnp.float32
+        )
+    grad_a = grad_a.astype(jnp.bfloat16).reshape(stored, rank, width_loc)
+    grad_b = grad_b.astype(jnp.bfloat16).reshape(stored, rank, out_loc)
+    back = jnp.stack(backs, axis=1).reshape(capacity, blk, width_loc + out_loc)
     mine_back = jnp.take(back, position, axis=0).reshape(rows, width_loc + out_loc)
 
     values = (base_t.T + mine_back[:, width_loc:].astype(jnp.float32)).astype(jnp.bfloat16)

time: 389 us -> 392 us (level)
  blocking collectives: 159 us -> 151 us
  waiting for transfers between devices: 85.8 us -> 93.4 us
  local copies, waits for them, and re-layouts: 50.3 us -> 46.1 us
  other arithmetic: 24.9 us -> 29 us
    all_to_all x0 -> x1, blocking collectives: none -> 68 us  [shards(): lax.all_to_all(send[:, r], 'dp', split_axis=0, concat_axis=0, tiled=True)]
    psum x1 -> x0, blocking collectives: 53.5 us -> none  [shards(): both = lax.psum(jnp.stack([down_part, up_part]), 'mp').astype(jnp.bfloat16)]
    unnamed x1, blocking collectives: 105 us -> 55.8 us
    all_gather x0 -> x2, blocking collectives: none -> 27.1 us  [shards(): lax.all_gather(lax.psum_scatter(jnp.stack([down_part, up_part]), 'mp', sc...]
    reduce_scatter x0 -> x2, waiting for transfers between devices: none -> 23.2 us  [shards(): lax.psum_scatter(jnp.stack([down_part, up_part]), 'mp', scatter_dimension...]
    all_to_all x1 -> x2, waiting for transfers between devices: 85.1 us -> 69.4 us  [shards(): lax.all_to_all(back_send, 'dp', split_axis=0, concat_axis=0, tiled=True)]
    all_to_all x1 -> x2, starting transfers between devices: 8.14 us -> 17.8 us  [shards(): lax.all_to_all(back_send, 'dp', split_axis=0, concat_axis=0, tiled=True)]
    all_to_all x1, starting transfers between devices: 12.1 us -> 4.93 us  [shards(): lax.all_to_all(send[:, r], 'dp', split_axis=0, concat_axis=0, tiled=True)]
  transfers between devices with their start and end apart: 4 -> 7, of which waited for: 1 -> 3; matrix products, arithmetic and copies ran while one was open for 23% -> 24% of each run, Pallas kernels for 0% -> 0%
where the time goes in v3:
time: 392 us; the launch traced here: 391 us
  blocking collectives  151 us (39%)
  waiting for transfers between devices  93.4 us (24%)
  local copies, waits for them, and re-layouts  46.1 us (12%)
  matrix products  33.3 us (8%)
  other arithmetic  29 us (7%)
  starting transfers between devices  22.9 us (6%)
  between operations  15 us (4%)
    all_to_all x2, waiting for transfers between devices, shards(): lax.all_to_all(back_send, 'dp', split_axis=0, concat_axis=0, tiled=True)  69.4 us
    all_to_all x1, blocking collectives, shards(): lax.all_to_all(send[:, r], 'dp', split_axis=0, concat_axis=0, tiled=True)  68 us
    unnamed x1, blocking collectives  55.8 us
    all_gather x2, blocking collectives, shards(): lax.all_gather(lax.psum_scatter(jnp.stack([down_part, up_part]), 'mp', sc...  27.1 us
    reduce_scatter x2, waiting for transfers between devices, shards(): lax.psum_scatter(jnp.stack([down_part, up_part]), 'mp', scatter_dimension...  23.2 us
    all_to_all x2, starting transfers between devices, shards(): lax.all_to_all(back_send, 'dp', split_axis=0, concat_axis=0, tiled=True)  17.8 us
    gather x2, local copies, waits for them, and re-layouts, shards(): jnp.take(back, position, axis=0).reshape(rows, width_loc + out_loc)  8.86 us
    concatenate x2, local copies, waits for them, and re-layouts, shards(): jnp.concatenate([adapter_bwd.astype(jnp.bfloat16), adapter_out.astype(jnp...  8.66 us
  transfers between devices with their start and end apart: 7, of which 3 were waited for; matrix products, arithmetic and copies ran while one was open for 24% of the time, Pallas kernels for 0%

profile of v3, /device:TPU:1, one launch (start us, length us, event | category | flops | bytes accessed | tf_op | source)
XLA Modules:
  0.0 390.5 jit_solution(13518384598934776665)
XLA Ops:
  8.0 1.4 gather_fusion
  9.4 1.4 gather_fusion.1
  11.2 2.8 gather_fusion.2
  14.6 2.6 broadcast_select_fusion
  17.4 1.7 fusion.1
  19.1 68.0 %all_to_all.20 = bf16[32,32,1152]{2,1,0:T(8,128)(2,1)} all-to-all(bf16[32,32,1152]{2,1,0:T(8,128)(2,1)S(1)} %get-tuple-element.32), channel_id=1, replica_groups=mesh['dp'=32,'mp'=8] {'dp'}, dimensions={0} | all-to-all | bytes 4718592 | tf_op jit(solution)/shard_map/all_to_all | solution.py:84
  87.2 4.9 %all-to-all-start.2 = ((bf16[32,32,1152]{2,1,0:T(8,128)(2,1)}), bf16[32,32,1152]{2,1,0:T(8,128)(2,1)}, u32[]{:S(2)}, u32[]{:S(2)}) async-start(bf16[32,32,1152]{2,1,0:T(8,128)(2,1)} %get-tuple-element.33), calls=%async_computation.4 | async-start | bytes 4718592 | tf_op jit(solution)/shard_map/all_to_all | solution.py:84
  93.7 55.8 %all-reduce = s32[1024]{0:T(1024)S(1)} all-reduce(s32[1024]{0:T(1024)S(1)} %dynamic-update-slice), channel_id=2, replica_groups=mesh['dp'=32,'mp'=8] {'dp'}, use_global_device_ids=true, to_apply=%add | all-reduce | flops 1024 | bytes 8192
  152.3 3.4 fusion.11
  155.7 1.2 reduce_sum.94
  156.9 1.3 convolution_select_fusion.1
  160.7 3.4 fusion.14
  164.1 1.2 reduce_sum.96
  165.3 1.3 convolution_select_fusion
  167.3 1.8 pad_maximum_fusion.5
  169.9 23.2 %reduce-scatter.6.cloned.1.call-done = f32[2,128,64]{1,2,0:T(8,128)} async-done(((f32[2,1024,64]{1,2,0:T(8,128)}), f32[2,128,64]{1,2,0:T(8,128)}) %reduce-scatter.6.cloned.1.call-update) | async-done | bytes 65552 | tf_op jit(solution)/shard_map/reduce_scatter | solution.py:104
  193.1 0.8 convert_element_type.44
  193.9 14.6 %all_gather.14 = bf16[2,1024,64]{1,2,0:T(8,128)(2,1)S(1)} all-gather(bf16[2,128,64]{1,2,0:T(8,128)(2,1)S(1)} %convert_element_type.44), channel_id=1, replica_groups=mesh['dp'=32,'mp'=8] {'mp'}, dimensions={1}, use_global_device_ids=true | all-gather | bytes 294912 | tf_op jit(solution)/shard_map/all_gather | solution.py:103
  211.0 3.1 broadcast_select_fusion.5
  214.1 3.2 select_n.184
  217.3 1.3 select_n.186
  218.6 1.3 convolution_convert_fusion.3
  220.0 1.9 convolution_convert_fusion.1
  221.9 1.6 pad_maximum_fusion.2
  223.5 4.3 %copy.68 = bf16[1024,1152]{1,0:T(8,128)(2,1)} copy(bf16[1024,1152]{0,1:T(8,128)(2,1)} %pad_maximum_fusion.2) | data formatting | bytes 4718592 | tf_op jit(solution)/shard_map/concatenate | solution.py:122
  227.9 9.7 %all-to-all-start.1 = ((bf16[32,32,1152]{2,1,0:T(8,128)(2,1)}), bf16[32,32,1152]{2,1,0:T(8,128)(2,1)}, u32[]{:S(2)}, u32[]{:S(2)}) async-start(bf16[32,32,1152]{2,1,0:T(8,128)(2,1)} %bitcast.96), calls=%async_computation.3 | async-start | bytes 4718592 | tf_op jit(solution)/shard_map/all_to_all | solution.py:125
  237.6 6.0 %fusion.47 = f32[1024,1024]{1,0:T(8,128)} fusion(bf16[1024,1024]{1,0:T(8,128)(2,1)} %param.9, bf16[1024,1024]{1,0:T(8,128)(2,1)S(1)} %copy-done), kind=kOutput, calls=%fused_computation.105 | convolution fusion | flops 2147483648 | bytes 8388608 | tf_op jit(solution)/shard_map/dot_general | solution.py:59
  243.7 0.8 convert_element_type.47
  244.6 12.6 %all_gather.15 = bf16[2,1024,64]{1,2,0:T(8,128)(2,1)S(1)} all-gather(bf16[2,128,64]{1,2,0:T(8,128)(2,1)S(1)} %convert_element_type.47), channel_id=1, replica_groups=mesh['dp'=32,'mp'=8] {'mp'}, dimensions={1}, use_global_device_ids=true | all-gather | bytes 294912 | tf_op jit(solution)/shard_map/all_gather | solution.py:103
  258.2 1.1 broadcast_select_fusion.3
  261.8 1.6 pad_maximum_fusion.3
  263.4 4.3 %copy.73 = bf16[1024,1152]{1,0:T(8,128)(2,1)} copy(bf16[1024,1152]{0,1:T(8,128)(2,1)} %pad_maximum_fusion.3) | data formatting | bytes 4718592 | tf_op jit(solution)/shard_map/concatenate | solution.py:122
  267.7 23.7 %all-to-all-done.1 = bf16[32,32,1152]{2,1,0:T(8,128)(2,1)} async-done(((bf16[32,32,1152]{2,1,0:T(8,128)(2,1)}), bf16[32,32,1152]{2,1,0:T(8,128)(2,1)}, u32[]{:S(2)}, u32[]{:S(2)}) %all-to-all-start.1) | async-done | bytes 2359328 | tf_op jit(solution)/shard_map/all_to_all | solution.py:125
  291.4 8.1 %all-to-all-start.3 = ((bf16[32,32,1152]{2,1,0:T(8,128)(2,1)}), bf16[32,32,1152]{2,1,0:T(8,128)(2,1)}, u32[]{:S(2)}, u32[]{:S(2)}) async-start(bf16[32,32,1152]{2,1,0:T(8,128)(2,1)} %bitcast.97), calls=%async_computation.6 | async-start | bytes 4718592 | tf_op jit(solution)/shard_map/all_to_all | solution.py:125
  301.0 1.3 fusion.26
  302.3 2.1 fusion.23
  304.4 2.2 fusion.3
  306.6 1.4 fusion.20
  308.0 45.7 %all-to-all-done.3 = bf16[32,32,1152]{2,1,0:T(8,128)(2,1)} async-done(((bf16[32,32,1152]{2,1,0:T(8,128)(2,1)}), bf16[32,32,1152]{2,1,0:T(8,128)(2,1)}, u32[]{:S(2)}, u32[]{:S(2)}) %all-to-all-start.3) | async-done | bytes 2359328 | tf_op jit(solution)/shard_map/all_to_all | solution.py:125
  353.7 2.8 pad_maximum_fusion
  356.5 2.8 copy.74
  359.3 4.6 %gather_fusion.4 = bf16[32,32,1152]{2,1,0:T(8,128)(2,1)} fusion(bf16[64,32,1152]{2,1,0:T(8,128)(2,1)} %bitcast.95, s32[1024]{0:T(1024)S(1)} %pad_clamp_fusion), kind=kCustom, calls=%fused_computation.4 | custom fusion | bytes 4718720 | tf_op jit(solution)/shard_map/jit(_take)/gather | solution.py:135
  363.8 4.3 %copy.75 = bf16[1024,1152]{0,1:T(8,128)(2,1)} copy(bf16[1024,1152]{1,0:T(8,128)(2,1)} %bitcast.98) | data formatting | bytes 4718592 | tf_op jit(solution)/shard_map/jit(_take)/gather | solution.py:135
  368.1 3.3 broadcast_select_fusion.1
  371.4 6.7 %add_convert_fusion = bf16[1024,1024]{0,1:T(8,128)(2,1)} fusion(bf16[1024,1152]{0,1:T(8,128)(2,1)} %broadcast_select_fusion.1, bf16[1024,1024]{1,0:T(8,128)(2,1)} %all-gather.3.cloned.1.call-done, bf16[1024,1024]{1,0:T(8,128)(2,1)} %param.9), kind=kOutput, calls=%fused_computation.8 | convolution fusion | flops 2150629376 | bytes 8388608 | tf_op jit(solution)/shard_map/dot_general | solution.py:67
  378.1 3.9 %copy.82 = bf16[1024,1024]{1,0:T(8,128)(2,1)} copy(bf16[1024,1024]{0,1:T(8,128)(2,1)} %add_convert_fusion) | data formatting | bytes 4194304
  382.0 1.2 fusion.24
  383.2 0.8 copy.81
  (102 shorter events, 17.0 us)
Async XLA Ops:
  7.2 4.0 %copy-start = (bf16[1024,1024]{1,0:T(8,128)(2,1)S(1)}, bf16[1024,1024]{1,0:T(8,128)(2,1)}, u32[]{:S(2)}) copy-start(bf16[1024,1024]{1,0:T(8,128)(2,1)} %param.8) | copy-start | bytes 6291460
  11.2 2.8 copy-start.3
  87.2 5.0 %copy-start.15 = (u32[256]{0:T(256)S(1)}, u32[256]{0:T(256)}, u32[]{:S(2)}) copy-start(u32[256]{0:T(256)} %constant.90) | copy-start | bytes 3076
  87.2 65.1 %copy-start.4 = (bf16[3,64,1024]{2,1,0:T(8,128)(2,1)S(1)}, bf16[3,64,1024]{2,1,0:T(8,128)(2,1)}, u32[]{:S(2)}) copy-start(bf16[3,64,1024]{2,1,0:T(8,128)(2,1)} %param.10) | copy-start | bytes 1179652
  87.2 73.5 %all-to-all-start.2 = ((bf16[32,32,1152]{2,1,0:T(8,128)(2,1)}), bf16[32,32,1152]{2,1,0:T(8,128)(2,1)}, u32[]{:S(2)}, u32[]{:S(2)}) async-start(bf16[32,32,1152]{2,1,0:T(8,128)(2,1)} %get-tuple-element.33), calls=%async_computation.4 | async-start | bytes 4718592 | tf_op jit(solution)/shard_map/all_to_all | solution.py:84
  92.1 101.0 %reduce-scatter.6.cloned.1.call-start = ((), (), s32[]{:S(2)}) async-start(), calls=%async_computation.8 | async-start | bytes 589824 | tf_op jit(solution)/shard_map/reduce_scatter | solution.py:104
  151.9 3.8 copy-start.6
  152.2 3.4 copy-start.10
  152.3 4.6 %copy-start.8 = (bf16[3,64,128]{2,1,0:T(8,128)(2,1)S(1)}, bf16[3,64,128]{2,1,0:T(8,128)(2,1)}, u32[]{:S(2)}) copy-start(bf16[3,64,128]{2,1,0:T(8,128)(2,1)} %param.11) | copy-start | bytes 147460
  159.1 84.6 %reduce-scatter.8.cloned.1.call-start = ((), (), s32[]{:S(2)}) async-start(), calls=%async_computation.9 | async-start | bytes 589824 | tf_op jit(solution)/shard_map/reduce_scatter | solution.py:104
  160.6 3.4 copy-start.9
  169.1 202.3 %all-gather.3.cloned.1.call-start = ((), (), s32[]{:S(2)}) async-start(), calls=%async_computation.10 | async-start | bytes 2359296 | tf_op jit(solution)/shard_map/all_gather | solution.py:66
  227.9 63.6 %all-to-all-start.1 = ((bf16[32,32,1152]{2,1,0:T(8,128)(2,1)}), bf16[32,32,1152]{2,1,0:T(8,128)(2,1)}, u32[]{:S(2)}, u32[]{:S(2)}) async-start(bf16[32,32,1152]{2,1,0:T(8,128)(2,1)} %bitcast.96), calls=%async_computation.3 | async-start | bytes 4718592 | tf_op jit(solution)/shard_map/all_to_all | solution.py:125
  237.6 144.4 %reduce-scatter.4.cloned.1.call-start = ((), (), s32[]{:S(2)}) async-start(), calls=%async_computation.7 | async-start | bytes 4718592 | tf_op jit(solution)/shard_map/reduce_scatter | solution.py:58
  259.4 1.7 copy-start.5
  291.4 8.3 %copy-start.12 = (bf16[1024,64]{0,1:T(8,128)(2,1)S(1)}, bf16[1024,64]{0,1:T(8,128)(2,1)}, u32[]{:S(2)}) copy-start(bf16[1024,64]{0,1:T(8,128)(2,1)} %get-tuple-element.38) | copy-start | bytes 393220
  291.4 8.6 %copy-start.14 = (bf16[1024,64]{0,1:T(8,128)(2,1)S(1)}, bf16[1024,64]{0,1:T(8,128)(2,1)}, u32[]{:S(2)}) copy-start(bf16[1024,64]{0,1:T(8,128)(2,1)} %get-tuple-element.34) | copy-start | bytes 393220
  291.4 62.2 %all-to-all-start.3 = ((bf16[32,32,1152]{2,1,0:T(8,128)(2,1)}), bf16[32,32,1152]{2,1,0:T(8,128)(2,1)}, u32[]{:S(2)}, u32[]{:S(2)}) async-start(bf16[32,32,1152]{2,1,0:T(8,128)(2,1)} %bitcast.97), calls=%async_computation.6 | async-start | bytes 4718592 | tf_op jit(solution)/shard_map/all_to_all | solution.py:125
  299.5 0.9 copy-start.13
  299.5 1.2 copy-start.11
  300.0 1.0 copy-start.7
  302.3 4.3 %copy-start.2 = (bf16[32,32,1152]{2,1,0:T(8,128)(2,1)S(1)}, bf16[32,32,1152]{2,1,0:T(8,128)(2,1)}, u32[]{:S(2)}) copy-start(bf16[32,32,1152]{2,1,0:T(8,128)(2,1)} %all_to_all.20) | copy-start | bytes 7077892
  371.4 12.6 %copy-start.1 = (bf16[1024,1024]{1,0:T(8,128)(2,1)S(1)}, bf16[1024,1024]{1,0:T(8,128)(2,1)}, u32[]{:S(2)}) copy-start(bf16[1024,1024]{1,0:T(8,128)(2,1)} %param.8) | copy-start | bytes 6291460
Sparse Core Ops, SparseCore 0:
  159.2 33.8 reduce-scatter.5
  195.8 32.3 reduce-scatter.7
  230.0 33.3 all-gather.2
  265.8 38.2 reduce-scatter.3

commit v4 on v2

v4 whole, which is shorter than its diff:
```python
import jax
import jax.numpy as jnp
import numpy as np
from jax import lax
from jax.sharding import Mesh
from jax.sharding import PartitionSpec as P

MOST = 2
DP = ("dz", "dx")


def earlier_same(group):
    count = group.shape[-1]
    ids = jnp.arange(count, dtype=jnp.int32)
    same = (group[..., :, None] == group[..., None, :]) & (ids[:, None] > ids[None, :])
    return jnp.sum(same.astype(jnp.int32), axis=-1)


def shards(
    tokens,
    value_weight,
    adapter_down_panels,
    adapter_up_panels,
    cotangent,
    block_list_entry,
    device_tenant_list,
    tenant_location_map,
):
    rows, width_loc = tokens.shape
    stored, rank, _ = adapter_down_panels.shape
    out_loc = adapter_up_panels.shape[2]
    blocks = block_list_entry.shape[0]
    blk = rows // blocks
    n_z = lax.axis_size("dz")
    n_x = lax.axis_size("dx")
    per_x = min(MOST * n_z, blocks)
    capacity = n_x * per_x
    my_x = lax.axis_index("dx")
    column = n_z * stored

    tenant = jnp.take(device_tenant_list, block_list_entry, mode="clip")
    location = jnp.take(tenant_location_map, tenant, mode="clip")
    owner_x = (location // stored) % n_x
    position = owner_x * per_x + earlier_same(owner_x)

    slot_ids = jnp.arange(capacity, dtype=jnp.int32)
    block_ids = jnp.arange(blocks, dtype=jnp.int32)
    source = jnp.sum(
        jnp.where(position[None, :] == slot_ids[:, None], block_ids[None, :], 0), axis=1
    )

    x_location = lax.all_gather(location, "dx", axis=0, tiled=False)
    x_owner_x = (x_location // stored) % n_x
    x_rank = earlier_same(x_owner_x)
    in_column = (x_location // stored // n_x) * stored + x_location % stored
    mine = x_owner_x == my_x
    slot_panel = jnp.stack(
        [jnp.sum(jnp.where(mine & (x_rank == c), in_column + 1, 0), axis=1) for c in range(per_x)],
        axis=1,
    ).reshape(capacity) - 1
    pick = slot_panel[:, None] == jnp.arange(column, dtype=jnp.int32)[None, :]

    down_col = lax.all_gather(adapter_down_panels, "dz", axis=0, tiled=True)
    up_col = lax.all_gather(adapter_up_panels, "dz", axis=0, tiled=True)

    base_t = lax.psum_scatter(
        lax.dot_general(
            value_weight, tokens, (((0,), (1,)), ((), ())), preferred_element_type=jnp.float32
        ),
        "mp",
        scatter_dimension=0,
        tiled=True,
    )
    cot_full = lax.all_gather(cotangent, "mp", axis=1, tiled=True)
    base_bwd = lax.dot_general(
        cot_full, value_weight, (((1,), (1,)), ((), ())), preferred_element_type=jnp.float32
    )

    token_blocks = tokens.reshape(blocks, blk, width_loc)
    cot_blocks = cotangent.reshape(blocks, blk, out_loc)
    send = jnp.concatenate(
        [jnp.take(token_blocks, source, axis=0), jnp.take(cot_blocks, source, axis=0)], axis=2
    )
    recv = lax.all_to_all(send, "dx", split_axis=0, concat_axis=0, tiled=True)
    tok_recv = recv[:, :, :width_loc]
    cot_recv = recv[:, :, width_loc:]

    panel_at = jnp.clip(slot_panel, 0, column - 1)
    down_sel = jnp.take(down_col, panel_at, axis=0)
    up_sel = jnp.take(up_col, panel_at, axis=0)
    down_part = jnp.einsum("snd,srd->snr", tok_recv, down_sel, preferred_element_type=jnp.float32)
    up_part = jnp.einsum("snc,src->snr", cot_recv, up_sel, preferred_element_type=jnp.float32)
    both = lax.all_gather(
        lax.psum_scatter(jnp.stack([down_part, up_part]), "mp", scatter_dimension=1, tiled=True).astype(
            jnp.bfloat16
        ),
        "mp",
        axis=1,
        tiled=True,
    )
    down_low = both[0]
    up_grad = both[1]

    adapter_out = jnp.einsum("snr,src->snc", down_low, up_sel, preferred_element_type=jnp.float32)
    adapter_bwd = jnp.einsum("snr,srd->snd", up_grad, down_sel, preferred_element_type=jnp.float32)
    back_send = jnp.concatenate(
        [adapter_bwd.astype(jnp.bfloat16), adapter_out.astype(jnp.bfloat16)], axis=2
    )
    back = lax.all_to_all(back_send, "dx", split_axis=0, concat_axis=0, tiled=True)

    pick_rows = jnp.broadcast_to(pick[:, None, :, None], (capacity, blk, column, rank)).reshape(
        capacity * blk, column * rank
    )

    def spread(small):
        wide = jnp.broadcast_to(small.reshape(capacity * blk, 1, rank), (capacity * blk, column, rank))
        wide = wide.reshape(capacity * blk, column * rank)
        return jnp.where(pick_rows, wide, jnp.zeros_like(wide))

    grad_a_col = lax.dot_general(
        spread(up_grad),
        tok_recv.reshape(capacity * blk, width_loc),
        (((0,), (0,)), ((), ())),
        preferred_element_type=jnp.float32,
    )
    grad_b_col = lax.dot_general(
        spread(down_low),
        cot_recv.reshape(capacity * blk, out_loc),
        (((0,), (0,)), ((), ())),
        preferred_element_type=jnp.float32,
    )
    grad_a = lax.psum_scatter(grad_a_col, "dz", scatter_dimension=0, tiled=True)
    grad_b = lax.psum_scatter(grad_b_col, "dz", scatter_dimension=0, tiled=True)
    grad_a = grad_a.astype(jnp.bfloat16).reshape(stored, rank, width_loc)
    grad_b = grad_b.astype(jnp.bfloat16).reshape(stored, rank, out_loc)

    mine_back = jnp.take(back, position, axis=0).reshape(rows, width_loc + out_loc)
    values = (base_t.T + mine_back[:, width_loc:].astype(jnp.float32)).astype(jnp.bfloat16)
    token_gradient = (base_bwd + mine_back[:, :width_loc].astype(jnp.float32)).astype(jnp.bfloat16)
    return (values, token_gradient, grad_a, grad_b)


def split_dp(mesh):
    devices = np.asarray(mesh.devices)
    n_dp, n_mp = devices.shape
    try:
        n_x = len({tuple(d.coords)[0] for d in devices[:, 0]})
    except (AttributeError, TypeError):
        n_x = 1
    if n_x < 1 or n_dp % n_x:
        n_x = 1
    return Mesh(devices.reshape(n_dp // n_x, n_x, n_mp), ("dz", "dx", "mp"))


def solution(mesh):
    in_specs = (
        P(DP, "mp"),
        P("mp", None),
        P(DP, None, "mp"),
        P(DP, None, "mp"),
        P(DP, "mp"),
        P(DP),
        P(DP),
        P(),
    )
    out_specs = (P(DP, "mp"), P(DP, "mp"), P(DP, None, "mp"), P(DP, None, "mp"))
    return jax.shard_map(
        shards, mesh=split_dp(mesh), in_specs=in_specs, out_specs=out_specs, check_vma=False
    )
```

time: 389 us -> 419 us (1.077)
  local copies, waits for them, and re-layouts: 49.4 us -> 78.7 us
  blocking collectives: 122 us -> 94.7 us
  waiting for transfers between devices: 122 us -> 143 us
  matrix products: 29.7 us -> 45.1 us
  starting transfers between devices: 22.2 us -> 10.7 us
  other arithmetic: 23.9 us -> 29.5 us
    unnamed x1, blocking collectives: 106 us -> 53.5 us
    unnamed x3 -> x7, waiting for transfers between devices: 0.73 us -> 36.3 us
    all_to_all x2, waiting for transfers between devices: 86.6 us -> 52.7 us  [the longest x1 52.7 us: shards(): lax.all_to_all(back_send, 'dx', split_axis=0, concat_axis=0, tiled=True)]
    select_n x2, local copies, waits for them, and re-layouts: 9.17 us -> 33.8 us  [spread(): return jnp.where(pick_rows, wide, jnp.zeros_like(wide))]
    all_gather x0 -> x1, blocking collectives: none -> 24.2 us  [shards(): up_col = lax.all_gather(adapter_up_panels, 'dz', axis=0, tiled=True)]
    reduce_scatter x1 -> x2, waiting for transfers between devices: 34.4 us -> 54.5 us  [the longest x1 54.4 us: shards(): grad_a = lax.psum_scatter(grad_a_col, 'dz', scatter_dimension=0, tiled=True)]
    dot_general x6, matrix products: 17.2 us -> 32.4 us  [the longest x1 11.8 us: shards(): lax.dot_general(spread(up_grad), tok_recv.reshape(capacity * blk, width_l...]
    all_to_all x2, starting transfers between devices: 21.8 us -> 10.2 us  [the longest x1 5.13 us: shards(): recv = lax.all_to_all(send, 'dx', split_axis=0, concat_axis=0, tiled=True)]
  transfers between devices with their start and end apart: 5 -> 8, of which waited for: 2 -> 3; matrix products, arithmetic and copies ran while one was open for 19% -> 23% of each run, Pallas kernels for 0% -> 0%
where the time goes in v4:
time: 419 us; the launch traced here: 417 us
  waiting for transfers between devices  143 us (34%)
  blocking collectives  94.7 us (23%)
  local copies, waits for them, and re-layouts  78.7 us (19%)
  matrix products  45.1 us (11%)
  other arithmetic  29.5 us (7%)
  between operations  15 us (4%)
  starting transfers between devices  10.7 us (3%)
    reduce_scatter x1, waiting for transfers between devices, shards(): grad_a = lax.psum_scatter(grad_a_col, 'dz', scatter_dimension=0, tiled=True)  54.4 us
    unnamed x1, blocking collectives  53.5 us
    all_to_all x1, waiting for transfers between devices, shards(): lax.all_to_all(back_send, 'dx', split_axis=0, concat_axis=0, tiled=True)  52.7 us
    unnamed x7, waiting for transfers between devices  36.3 us
    select_n x2, local copies, waits for them, and re-layouts, spread(): return jnp.where(pick_rows, wide, jnp.zeros_like(wide))  33.8 us
    all_gather x1, blocking collectives, shards(): up_col = lax.all_gather(adapter_up_panels, 'dz', axis=0, tiled=True)  24.2 us
    all_gather x1, blocking collectives, shards(): lax.all_gather(lax.psum_scatter(jnp.stack([down_part, up_part]), 'mp', sc...  17 us
    dot_general x1, matrix products, shards(): lax.dot_general(spread(up_grad), tok_recv.reshape(capacity * blk, width_l...  11.8 us
  transfers between devices with their start and end apart: 8, of which 3 were waited for; matrix products, arithmetic and copies ran while one was open for 23% of the time, Pallas kernels for 0%

profile of v4, /device:TPU:1, one launch (start us, length us, event | category | flops | bytes accessed | tf_op | source)
XLA Modules:
  0.0 417.2 jit_solution(15197474575198803912)
XLA Ops:
  7.2 0.7 all-gather.4.cloned.1.call-update
  7.9 0.7 pad_clamp_fusion.4
  8.6 1.4 gather_fusion
  9.9 1.4 gather_fusion.1
  11.3 0.5 and_select_fusion.1
  12.1 1.6 gather_fusion.3
  13.8 2.7 gather_fusion.2
  16.6 2.6 broadcast_select_fusion.3
  19.3 2.8 pad_maximum_fusion
  22.0 5.1 %all-to-all-start = ((bf16[64,32,1152]{2,1,0:T(8,128)(2,1)}), bf16[64,32,1152]{2,1,0:T(8,128)(2,1)}, u32[]{:S(2)}, u32[]{:S(2)}) async-start(bf16[64,32,1152]{2,1,0:T(8,128)(2,1)} %pad_maximum_fusion), calls=%async_computation.1 | async-start | bytes 9437184 | tf_op jit(solution)/shard_map/all_to_all | solution.py:84
  27.3 0.6 dynamic-slice
  28.8 53.5 %all-reduce = s32[128]{0:T(128)S(1)} all-reduce(s32[128]{0:T(128)S(1)} %dynamic-update-slice), channel_id=2, replica_groups=mesh['dz'=8,'dx'=4,'mp'=8] {'dx'}, use_global_device_ids=true, to_apply=%add | all-reduce | flops 128 | bytes 1024
  85.0 24.2 %all_gather.18 = bf16[24,64,128]{2,1,0:T(8,128)(2,1)S(1)} all-gather(bf16[3,64,128]{2,1,0:T(8,128)(2,1)S(1)} %copy-done.5), channel_id=1, replica_groups=mesh['dz'=8,'dx'=4,'mp'=8] {'dz'}, dimensions={0}, use_global_device_ids=true | all-gather | bytes 442368 | tf_op jit(solution)/shard_map/all_gather | solution.py:64
  109.2 0.7 gather_fusion.5
  110.0 2.7 convolution_bitcast_fusion
  112.7 7.2 %gather_fusion.4 = bf16[64,64,1024]{2,1,0:T(8,128)(2,1)} fusion(bf16[24,64,1024]{2,1,0:T(8,128)(2,1)} %all-gather.4.cloned.1.call-done, s32[1024]{0:T(1024)S(1)} %pad_clamp_fusion.1), kind=kCustom, calls=%fused_computation.4 | custom fusion | bytes 16777472 | tf_op jit(solution)/shard_map/jit(_take)/gather | solution.py:89
  120.0 7.1 %fusion.3 = f32[1,64,32,64]{3,2,1,0:T(8,128)S(1)} fusion(bf16[64,64,1024]{2,1,0:T(8,128)(2,1)} %gather_fusion.4, pred[64]{0:T(512)(128)(4,1)S(1)} %compare_and_fusion, bf16[64,32,1152]{2,1,0:T(8,128)(2,1)} %all-to-all-done), kind=kOutput, calls=%fused_computation.20 | convolution fusion | flops 272629760 | bytes 13107264 | tf_op jit(solution)/shard_map/snd,srd->snr/dot_general | solution.py:91
  127.1 1.6 copy_bitcast_fusion
  128.6 2.9 reshape.353
  131.7 1.9 slice.39
  133.6 35.0 %reduce-scatter.13.cloned.1.call-done = f32[8,4096]{1,0:T(8,128)} async-done(((f32[64,4096]{1,0:T(8,128)}), f32[8,4096]{1,0:T(8,128)}) %reduce-scatter.13.cloned.1.call-update) | async-done | bytes 131088
  168.6 1.1 reshape.354
  169.7 17.0 %all_gather.19 = bf16[2,64,32,64]{3,2,1,0:T(8,128)(2,1)S(1)} all-gather(bf16[2,8,32,64]{3,2,1,0:T(8,128)(2,1)S(1)} %copy.69), channel_id=1, replica_groups=mesh['dz'=8,'dx'=4,'mp'=8] {'mp'}, dimensions={1}, use_global_device_ids=true | all-gather | bytes 589824 | tf_op jit(solution)/shard_map/all_gather | solution.py:93
  186.7 1.0 copy-done.2
  187.7 9.4 %broadcast_select_fusion = (bf16[64,32,24,64]{3,2,1,0:T(8,128)(2,1)}, bf16[64,32,24,64]{3,2,1,0:T(8,128)(2,1)}) fusion(pred[64,24]{1,0:T(8,128)(4,1)S(1)} %iota_compare_fusion, bf16[64,32,64]{2,1,0:T(8,128)(2,1)S(1)} %get-tuple-element.42, bf16[64,32,64]{2,1,0:T(8,128)(2,1)S(1)} %get-tuple-element.43), kind=kLoop, calls=%fused_computation.7 | loop fusion | flops 6291456 | bytes 13108736 | tf_op jit(solution)/shard_map/jit(_where)/select_n | solution.py:118
  197.1 16.8 %select_n.261 = bf16[2048,1536]{1,0:T(8,128)(2,1)} reshape(bf16[64,32,24,64]{3,2,1,0:T(8,128)(2,1)} %get-tuple-element.44) | data formatting | bytes 12582912 | tf_op jit(solution)/shard_map/jit(_where)/select_n | solution.py:118
  213.9 5.6 %fusion.24 = f32[1536,128]{1,0:T(8,128)} fusion(bf16[2048,1536]{1,0:T(8,128)(2,1)} %select_n.261, bf16[2048,128]{1,0:T(8,128)(2,1)} %bitcast.82), kind=kOutput, calls=%fused_computation.112 | convolution fusion | flops 805306368 | bytes 7602176 | tf_op jit(solution)/shard_map/dot_general | solution.py:126
  219.6 0.5 all-gather.6.cloned.1.call-update
  220.2 6.0 %fusion.22 = f32[1024,1024]{1,0:T(8,128)} fusion(bf16[1024,1024]{1,0:T(8,128)(2,1)} %param.9, bf16[1024,1024]{1,0:T(8,128)(2,1)S(1)} %copy-done), kind=kOutput, calls=%fused_computation.110 | convolution fusion | flops 2147483648 | bytes 8388608 | tf_op jit(solution)/shard_map/dot_general | solution.py:67
  226.5 5.0 %slice.38 = bf16[64,32,1024]{2,1,0:T(8,128)(2,1)} slice(bf16[64,32,1152]{2,1,0:T(8,128)(2,1)} %all-to-all-done), slice={[0:64], [0:32], [0:1024]} | slice | bytes 8388608 | tf_op jit(solution)/shard_map/slice | solution.py:85
  231.5 16.9 %select_n.259 = bf16[2048,1536]{1,0:T(8,128)(2,1)} reshape(bf16[64,32,24,64]{3,2,1,0:T(8,128)(2,1)} %get-tuple-element.45) | data formatting | bytes 12582912 | tf_op jit(solution)/shard_map/jit(_where)/select_n | solution.py:118
  248.4 11.8 %fusion.23 = f32[1536,1024]{1,0:T(8,128)} fusion(bf16[2048,1536]{1,0:T(8,128)(2,1)} %select_n.259, bf16[2048,1024]{1,0:T(8,128)(2,1)} %bitcast.80), kind=kOutput, calls=%fused_computation.111 | convolution fusion | flops 6442450944 | bytes 16777216 | tf_op jit(solution)/shard_map/dot_general | solution.py:120
  260.3 1.2 copy-done.3
  261.5 0.5 convolution_convert_fusion
  261.9 4.7 %fusion.2 = bf16[64,32,1024]{2,1,0:T(8,128)(2,1)S(1)} fusion(bf16[64,64,1024]{2,1,0:T(8,128)(2,1)} %gather_fusion.4, pred[64]{0:T(512)(128)(4,1)S(1)} %compare_and_fusion, bf16[2,64,32,64]{3,2,1,0:T(8,128)(2,1)S(1)} %copy-done.3), kind=kOutput, calls=%fused_computation.16 | convolution fusion | flops 274726912 | bytes 13107712 | tf_op jit(solution)/shard_map/snr,srd->snd/dot_general | solution.py:105
  266.6 2.8 pad_maximum_fusion.1
  269.5 5.1 %all-to-all-start.1 = ((bf16[64,32,1152]{2,1,0:T(8,128)(2,1)}), bf16[64,32,1152]{2,1,0:T(8,128)(2,1)}, u32[]{:S(2)}, u32[]{:S(2)}) async-start(bf16[64,32,1152]{2,1,0:T(8,128)(2,1)} %pad_maximum_fusion.1), calls=%async_computation.2 | async-start | bytes 9437184 | tf_op jit(solution)/shard_map/all_to_all | solution.py:109
  274.8 1.5 convert_element_type.43
  276.3 52.7 %all-to-all-done.1 = bf16[64,32,1152]{2,1,0:T(8,128)(2,1)} async-done(((bf16[64,32,1152]{2,1,0:T(8,128)(2,1)}), bf16[64,32,1152]{2,1,0:T(8,128)(2,1)}, u32[]{:S(2)}, u32[]{:S(2)}) %all-to-all-start.1) | async-done | bytes 4718624 | tf_op jit(solution)/shard_map/all_to_all | solution.py:109
  329.0 4.6 %gather_fusion.6 = bf16[32,32,1152]{2,1,0:T(8,128)(2,1)} fusion(bf16[64,32,1152]{2,1,0:T(8,128)(2,1)} %all-to-all-done.1, s32[1024]{0:T(1024)S(1)} %pad_clamp_fusion), kind=kCustom, calls=%fused_computation.6 | custom fusion | bytes 4718720 | tf_op jit(solution)/shard_map/jit(_take)/gather | solution.py:137
  333.6 4.3 %copy.60 = bf16[1024,1152]{0,1:T(8,128)(2,1)} copy(bf16[1024,1152]{1,0:T(8,128)(2,1)} %bitcast.79) | data formatting | bytes 4718592 | tf_op jit(solution)/shard_map/jit(_take)/gather | solution.py:137
  337.9 3.3 broadcast_select_fusion.8
  341.2 6.7 %add_convert_fusion = bf16[1024,1024]{0,1:T(8,128)(2,1)} fusion(bf16[1024,1152]{0,1:T(8,128)(2,1)} %broadcast_select_fusion.8, bf16[1024,1024]{1,0:T(8,128)(2,1)} %all-gather.6.cloned.1.call-done, bf16[1024,1024]{1,0:T(8,128)(2,1)} %param.9), kind=kOutput, calls=%fused_computation.12 | convolution fusion | flops 2150629376 | bytes 8388608 | tf_op jit(solution)/shard_map/dot_general | solution.py:75
  348.0 3.9 copy.63
  351.9 1.2 fusion.4
  353.1 0.8 copy.62
  353.9 54.4 %reduce-scatter.9.cloned.1.call-done = f32[192,1024]{1,0:T(8,128)} async-done(((f32[1536,1024]{1,0:T(8,128)}), f32[192,1024]{1,0:T(8,128)}) %reduce-scatter.9.cloned.1.call-update) | async-done | bytes 786448 | tf_op jit(solution)/shard_map/reduce_scatter | solution.py:132
  408.4 1.9 convert_element_type.42
  (82 shorter events, 4.3 us)
Async XLA Ops:
  7.2 6.6 %copy-start = (bf16[1024,1024]{1,0:T(8,128)(2,1)S(1)}, bf16[1024,1024]{1,0:T(8,128)(2,1)}, u32[]{:S(2)}) copy-start(bf16[1024,1024]{1,0:T(8,128)(2,1)} %param.8) | copy-start | bytes 6291460
  7.2 105.5 %all-gather.4.cloned.1.call-start = ((), (), s32[]{:S(2)}) async-start(), calls=%async_computation.7 | async-start | bytes 3538944 | tf_op jit(solution)/shard_map/all_gather | solution.py:63
  11.3 17.2 %copy-start.6 = (s32[32]{0:T(128)}, s32[32]{0:T(128)S(1)}, u32[]{:S(2)}) copy-start(s32[32]{0:T(128)S(1)} %gather_fusion.1) | copy-start | bytes 388
  22.0 5.2 %copy-start.9 = (u32[256]{0:T(256)S(1)}, u32[256]{0:T(256)}, u32[]{:S(2)}) copy-start(u32[256]{0:T(256)} %constant.169) | copy-start | bytes 3076
  22.0 62.9 %copy-start.5 = (bf16[3,64,128]{2,1,0:T(8,128)(2,1)S(1)}, bf16[3,64,128]{2,1,0:T(8,128)(2,1)}, u32[]{:S(2)}) copy-start(bf16[3,64,128]{2,1,0:T(8,128)(2,1)} %param.11) | copy-start | bytes 147460
  22.0 87.9 %all-to-all-start = ((bf16[64,32,1152]{2,1,0:T(8,128)(2,1)}), bf16[64,32,1152]{2,1,0:T(8,128)(2,1)}, u32[]{:S(2)}, u32[]{:S(2)}) async-start(bf16[64,32,1152]{2,1,0:T(8,128)(2,1)} %pad_maximum_fusion), calls=%async_computation.1 | async-start | bytes 9437184 | tf_op jit(solution)/shard_map/all_to_all | solution.py:84
  27.2 141.4 %reduce-scatter.13.cloned.1.call-start = ((), (), s32[]{:S(2)}) async-start(), calls=%async_computation.11 | async-start | bytes 1179648
  120.0 7.1 %copy-start.4 = (f32[1,64,32,64]{3,2,1,0:T(8,128)S(1)}, f32[1,64,32,64]{3,2,1,0:T(8,128)}, u32[]{:S(2)}) copy-start(f32[1,64,32,64]{3,2,1,0:T(8,128)} %convolution_bitcast_fusion) | copy-start | bytes 1572868
  131.6 143.2 %reduce-scatter.11.cloned.1.call-start = ((), (), s32[]{:S(2)}) async-start(), calls=%async_computation.10 | async-start | bytes 884736 | tf_op jit(solution)/shard_map/reduce_scatter | solution.py:133
  186.7 1.0 copy-start.2
  219.5 121.7 %all-gather.6.cloned.1.call-start = ((), (), s32[]{:S(2)}) async-start(), calls=%async_computation.8 | async-start | bytes 2359296 | tf_op jit(solution)/shard_map/all_gather | solution.py:74
  220.1 131.8 %reduce-scatter.7.cloned.1.call-start = ((), (), s32[]{:S(2)}) async-start(), calls=%async_computation.6 | async-start | bytes 4718592 | tf_op jit(solution)/shard_map/reduce_scatter | solution.py:66
  226.2 182.2 %reduce-scatter.9.cloned.1.call-start = ((), (), s32[]{:S(2)}) async-start(), calls=%async_computation.9 | async-start | bytes 7077888 | tf_op jit(solution)/shard_map/reduce_scatter | solution.py:132
  260.2 1.2 copy-start.3
  269.5 5.3 %copy-start.7 = (s32[32]{0:T(128)S(1)}, s32[32]{0:T(128)}, u32[]{:S(2)}) copy-start(s32[32]{0:T(128)} %copy-done.6) | copy-start | bytes 388
  269.5 5.3 %copy-start.8 = (s32[32]{0:T(128)S(1)}, s32[32]{0:T(128)}, u32[]{:S(2)}) copy-start(s32[32]{0:T(128)} %get-tuple-element.39) | copy-start | bytes 388
  269.5 59.5 %all-to-all-start.1 = ((bf16[64,32,1152]{2,1,0:T(8,128)(2,1)}), bf16[64,32,1152]{2,1,0:T(8,128)(2,1)}, u32[]{:S(2)}, u32[]{:S(2)}) async-start(bf16[64,32,1152]{2,1,0:T(8,128)(2,1)} %pad_maximum_fusion.1), calls=%async_computation.2 | async-start | bytes 9437184 | tf_op jit(solution)/shard_map/all_to_all | solution.py:109
  341.2 69.1 %copy-start.1 = (bf16[1024,1024]{1,0:T(8,128)(2,1)S(1)}, bf16[1024,1024]{1,0:T(8,128)(2,1)}, u32[]{:S(2)}) copy-start(bf16[1024,1024]{1,0:T(8,128)(2,1)} %param.8) | copy-start | bytes 6291460
Sparse Core Ops, SparseCore 0:
  9.8 48.5 all-gather.3
  131.7 36.8 reduce-scatter.12
  219.6 32.7 reduce-scatter.10
  254.3 33.2 all-gather.5
  290.2 39.1 reduce-scatter.6
  331.9 76.4 reduce-scatter.8

commit v5 on v4

--- a/solution.py
+++ b/solution.py
@@ -58,10 +58,24 @@
         [jnp.sum(jnp.where(mine & (x_rank == c), in_column + 1, 0), axis=1) for c in range(per_x)],
         axis=1,
     ).reshape(capacity) - 1
-    pick = slot_panel[:, None] == jnp.arange(column, dtype=jnp.int32)[None, :]
+    panel_ids = jnp.arange(column, dtype=jnp.int32)
+    slot_of = x_rank + (jnp.arange(n_x, dtype=jnp.int32) * per_x)[:, None]
+    panel_slot = jnp.sum(
+        jnp.where(
+            mine[None, :, :] & (in_column[None, :, :] == panel_ids[:, None, None]),
+            slot_of[None, :, :] + 1,
+            0,
+        ),
+        axis=2,
+    ) - 1
+    panel_used = panel_slot >= 0
+    panel_slot = jnp.clip(panel_slot, 0, capacity - 1)
 
-    down_col = lax.all_gather(adapter_down_panels, "dz", axis=0, tiled=True)
-    up_col = lax.all_gather(adapter_up_panels, "dz", axis=0, tiled=True)
+    both_col = lax.all_gather(
+        jnp.concatenate([adapter_down_panels, adapter_up_panels], axis=2), "dz", axis=0, tiled=True
+    )
+    down_col = both_col[:, :, :width_loc]
+    up_col = both_col[:, :, width_loc:]
 
     base_t = lax.psum_scatter(
         lax.dot_general(
@@ -108,27 +122,23 @@
     )
     back = lax.all_to_all(back_send, "dx", split_axis=0, concat_axis=0, tiled=True)
 
-    pick_rows = jnp.broadcast_to(pick[:, None, :, None], (capacity, blk, column, rank)).reshape(
-        capacity * blk, column * rank
-    )
+    def by_panel(small, wide):
+        small_p = jnp.take(small, panel_slot.reshape(-1), axis=0).reshape(column, n_x, blk, rank)
+        small_p = jnp.where(panel_used[:, :, None, None], small_p, jnp.zeros_like(small_p))
+        wide_p = jnp.take(wide, panel_slot.reshape(-1), axis=0)
+        return (
+            small_p.reshape(column, n_x * blk, rank),
+            wide_p.reshape(column, n_x * blk, wide.shape[2]),
+        )
 
-    def spread(small):
-        wide = jnp.broadcast_to(small.reshape(capacity * blk, 1, rank), (capacity * blk, column, rank))
-        wide = wide.reshape(capacity * blk, column * rank)
-        return jnp.where(pick_rows, wide, jnp.zeros_like(wide))
-
-    grad_a_col = lax.dot_general(
-        spread(up_grad),
-        tok_recv.reshape(capacity * blk, width_loc),
-        (((0,), (0,)), ((), ())),
-        preferred_element_type=jnp.float32,
-    )
-    grad_b_col = lax.dot_general(
-        spread(down_low),
-        cot_recv.reshape(capacity * blk, out_loc),
-        (((0,), (0,)), ((), ())),
-        preferred_element_type=jnp.float32,
-    )
+    up_p, tok_p = by_panel(up_grad, tok_recv)
+    grad_a_col = jnp.einsum(
+        "pnr,pnd->prd", up_p, tok_p, preferred_element_type=jnp.float32
+    ).reshape(column * rank, width_loc)
+    low_p, cot_p = by_panel(down_low, cot_recv)
+    grad_b_col = jnp.einsum(
+        "pnr,pnc->prc", low_p, cot_p, preferred_element_type=jnp.float32
+    ).reshape(column * rank, out_loc)
     grad_a = lax.psum_scatter(grad_a_col, "dz", scatter_dimension=0, tiled=True)
     grad_b = lax.psum_scatter(grad_b_col, "dz", scatter_dimension=0, tiled=True)
     grad_a = grad_a.astype(jnp.bfloat16).reshape(stored, rank, width_loc)

time: 419 us -> 381 us (0.909)
  blocking collectives: 94.7 us -> 70.2 us
  matrix products: 45.1 us -> 35.5 us
  local copies, waits for them, and re-layouts: 78.7 us -> 69.9 us
  other arithmetic: 29.5 us -> 34.9 us
    select_n x2 -> x0, local copies, waits for them, and re-layouts: 33.8 us -> none  [spread(): return jnp.where(pick_rows, wide, jnp.zeros_like(wide))]
    all_gather x1 -> x0, blocking collectives: 24.2 us -> none  [shards(): up_col = lax.all_gather(adapter_up_panels, 'dz', axis=0, tiled=True)]
    gather x0 -> x4, local copies, waits for them, and re-layouts: none -> 16.1 us  [the longest x2 10.8 us: by_panel(): wide_p = jnp.take(wide, panel_slot.reshape(-1), axis=0)]
    dot_general x2, matrix products: 17.4 us -> 8.87 us  [the longest x1 6.5 us: shards(): jnp.einsum('pnr,pnd->prd', up_p, tok_p, preferred_element_type=jnp.float32)]
    reduce_scatter x1, waiting for transfers between devices: 54.4 us -> 61.8 us  [shards(): grad_a = lax.psum_scatter(grad_a_col, 'dz', scatter_dimension=0, tiled=True)]
    unnamed x7, waiting for transfers between devices: 36.3 us -> 29 us
    slice x0 -> x2, local copies, waits for them, and re-layouts: none -> 4.99 us  [the longest x1 3.97 us: shards(): down_col = both_col[:, :, :width_loc]]
    select_n x1 -> x6, other arithmetic: 9.39 us -> 11.8 us  [the longest x3 9.05 us: by_panel(): wide_p = jnp.take(wide, panel_slot.reshape(-1), axis=0)]
  transfers between devices with their start and end apart: 8 -> 8, of which waited for: 3 -> 3; matrix products, arithmetic and copies ran while one was open for 23% -> 28% of each run, Pallas kernels for 0% -> 0%
where the time goes in v5:
time: 381 us; the launch traced here: 380 us
  waiting for transfers between devices  144 us (38%)
  blocking collectives  70.2 us (18%)
  local copies, waits for them, and re-layouts  69.9 us (18%)
  matrix products  35.5 us (9%)
  other arithmetic  34.9 us (9%)
  between operations  15.1 us (4%)
  starting transfers between devices  10.6 us (3%)
    reduce_scatter x1, waiting for transfers between devices, shards(): grad_a = lax.psum_scatter(grad_a_col, 'dz', scatter_dimension=0, tiled=True)  61.8 us
    unnamed x1, blocking collectives  53.4 us
    all_to_all x1, waiting for transfers between devices, shards(): lax.all_to_all(back_send, 'dx', split_axis=0, concat_axis=0, tiled=True)  52.7 us
    unnamed x7, waiting for transfers between devices  29 us
    all_gather x1, blocking collectives, shards(): lax.all_gather(lax.psum_scatter(jnp.stack([down_part, up_part]), 'mp', sc...  16.8 us
    unnamed x36, local copies, waits for them, and re-layouts  12.2 us
    gather x2, local copies, waits for them, and re-layouts, by_panel(): wide_p = jnp.take(wide, panel_slot.reshape(-1), axis=0)  10.8 us
    select_n x3, other arithmetic, by_panel(): wide_p = jnp.take(wide, panel_slot.reshape(-1), axis=0)  9.05 us
  transfers between devices with their start and end apart: 8, of which 3 were waited for; matrix products, arithmetic and copies ran while one was open for 28% of the time, Pallas kernels for 0%

profile of v5, /device:TPU:1, one launch (start us, length us, event | category | flops | bytes accessed | tf_op | source)
XLA Modules:
  0.0 379.7 jit_solution(2439899745153106531)
XLA Ops:
  7.2 2.0 pad_maximum_fusion.3
  9.9 1.4 gather_fusion
  11.2 1.4 gather_fusion.1
  13.8 1.6 gather_fusion.3
  15.4 2.7 gather_fusion.2
  18.3 2.6 broadcast_select_fusion.1
  20.9 2.7 pad_maximum_fusion
  23.7 5.2 %all-to-all-start = ((bf16[64,32,1152]{2,1,0:T(8,128)(2,1)}), bf16[64,32,1152]{2,1,0:T(8,128)(2,1)}, u32[]{:S(2)}, u32[]{:S(2)}) async-start(bf16[64,32,1152]{2,1,0:T(8,128)(2,1)} %pad_maximum_fusion), calls=%async_computation.1 | async-start | bytes 9437184 | tf_op jit(solution)/shard_map/all_to_all | solution.py:98
  30.4 53.4 %all-reduce = s32[128]{0:T(128)S(1)} all-reduce(s32[128]{0:T(128)S(1)} %dynamic-update-slice), channel_id=2, replica_groups=mesh['dz'=8,'dx'=4,'mp'=8] {'dx'}, use_global_device_ids=true, to_apply=%add | all-reduce | flops 128 | bytes 1024
  87.5 1.0 slice.57
  89.3 4.0 %slice.55 = bf16[24,64,1024]{2,1,0:T(8,128)(2,1)} slice(bf16[24,64,1152]{2,1,0:T(8,128)(2,1)} %all-gather.4.cloned.1.call-done), slice={[0:24], [0:64], [0:1024]} | slice | bytes 6291456 | tf_op jit(solution)/shard_map/slice | solution.py:77
  93.3 7.3 %gather_fusion.4 = bf16[64,64,1024]{2,1,0:T(8,128)(2,1)} fusion(bf16[24,64,1024]{2,1,0:T(8,128)(2,1)} %slice.55, s32[1024]{0:T(1024)S(1)} %pad_clamp_fusion.3), kind=kCustom, calls=%fused_computation.6 | custom fusion | bytes 16777472 | tf_op jit(solution)/shard_map/jit(_take)/gather | solution.py:103
  100.6 1.8 convolution_bitcast_fusion
  102.4 7.0 %fusion.3 = f32[1,64,32,64]{3,2,1,0:T(8,128)S(1)} fusion(bf16[64,64,1024]{2,1,0:T(8,128)(2,1)} %gather_fusion.4, pred[64]{0:T(512)(128)(4,1)S(1)} %copy-done.11, bf16[64,32,1152]{2,1,0:T(8,128)(2,1)} %all-to-all-done), kind=kOutput, calls=%fused_computation.23 | convolution fusion | flops 272629760 | bytes 13107264 | tf_op jit(solution)/shard_map/snd,srd->snr/dot_general | solution.py:105
  109.4 1.6 copy_bitcast_fusion
  111.0 2.9 reshape.439
  115.1 1.9 slice.56
  116.9 2.6 gather_fusion.8
  119.6 2.3 bitcast_select_fusion.1
  121.9 28.4 %reduce-scatter.13.cloned.1.call-done = f32[8,4096]{1,0:T(8,128)} async-done(((f32[64,4096]{1,0:T(8,128)}), f32[8,4096]{1,0:T(8,128)}) %reduce-scatter.13.cloned.1.call-update) | async-done | bytes 131088
  150.3 1.1 reshape.440
  151.3 16.8 %all_gather.15 = bf16[2,64,32,64]{3,2,1,0:T(8,128)(2,1)S(1)} all-gather(bf16[2,8,32,64]{3,2,1,0:T(8,128)(2,1)S(1)} %copy.81), channel_id=1, replica_groups=mesh['dz'=8,'dx'=4,'mp'=8] {'mp'}, dimensions={1}, use_global_device_ids=true | all-gather | bytes 589824 | tf_op jit(solution)/shard_map/all_gather | solution.py:107
  168.2 1.0 copy-done.2
  169.1 1.1 slice_bitcast_fusion
  170.2 2.7 gather_fusion.10
  172.9 2.6 gather_fusion.9
  175.5 2.8 broadcast_select_fusion.10
  178.2 1.4 copy.73
  179.7 2.4 fusion.5
  182.3 5.9 %fusion.34 = f32[1024,1024]{1,0:T(8,128)} fusion(bf16[1024,1024]{1,0:T(8,128)(2,1)} %param.11, bf16[1024,1024]{1,0:T(8,128)(2,1)S(1)} %copy-done), kind=kOutput, calls=%fused_computation.140 | convolution fusion | flops 2147483648 | bytes 8388608 | tf_op jit(solution)/shard_map/dot_general | solution.py:81
  188.9 5.0 %slice.54 = bf16[64,32,1024]{2,1,0:T(8,128)(2,1)} slice(bf16[64,32,1152]{2,1,0:T(8,128)(2,1)} %all-to-all-done), slice={[0:64], [0:32], [0:1024]} | slice | bytes 8388608 | tf_op jit(solution)/shard_map/slice | solution.py:99
  193.8 8.2 %gather_fusion.7 = bf16[96,32,1024]{2,1,0:T(8,128)(2,1)} fusion(bf16[64,32,1024]{2,1,0:T(8,128)(2,1)} %slice.54, s32[1024]{0:T(1024)S(1)} %pad_clamp_fusion), kind=kCustom, calls=%fused_computation.9 | custom fusion | bytes 12583296 | tf_op jit(solution)/shard_map/jit(_take)/gather | solution.py:128
  202.0 6.7 %bitcast_select_fusion = bf16[24,128,1024]{2,1,0:T(8,128)(2,1)} fusion(pred[24,128]{1,0:T(8,128)(4,1)S(1)} %broadcast_in_dim.192, bf16[24,128,1024]{2,1,0:T(8,128)(2,1)} %bitcast.84), kind=kLoop, calls=%fused_computation.12 | loop fusion | flops 3145728 | bytes 12585984 | tf_op jit(solution)/shard_map/jit(_take)/select_n | solution.py:128
  209.1 6.5 %fusion.7 = f32[24,64,1024]{2,1,0:T(8,128)} fusion(bf16[24,128,1024]{2,1,0:T(8,128)(2,1)} %bitcast_select_fusion, bf16[24,128,64]{1,2,0:T(8,128)(2,1)S(1)} %copy.70, pred[24,128]{1,0:T(8,128)(4,1)S(1)} %broadcast_in_dim.189), kind=kOutput, calls=%fused_computation.38 | convolution fusion | flops 402849792 | bytes 12979200 | tf_op jit(solution)/shard_map/pnr,pnd->prd/dot_general | solution.py:135
  215.6 1.2 copy-done.3
  217.3 4.7 %fusion.2 = bf16[64,32,1024]{2,1,0:T(8,128)(2,1)S(1)} fusion(bf16[64,64,1024]{2,1,0:T(8,128)(2,1)} %gather_fusion.4, pred[64]{0:T(512)(128)(4,1)S(1)} %copy-done.12, bf16[2,64,32,64]{3,2,1,0:T(8,128)(2,1)S(1)} %copy-done.3), kind=kOutput, calls=%fused_computation.19 | convolution fusion | flops 274726912 | bytes 13107712 | tf_op jit(solution)/shard_map/snr,srd->snd/dot_general | solution.py:119
  222.0 2.8 pad_maximum_fusion.1
  224.8 5.1 %all-to-all-start.1 = ((bf16[64,32,1152]{2,1,0:T(8,128)(2,1)}), bf16[64,32,1152]{2,1,0:T(8,128)(2,1)}, u32[]{:S(2)}, u32[]{:S(2)}) async-start(bf16[64,32,1152]{2,1,0:T(8,128)(2,1)} %pad_maximum_fusion.1), calls=%async_computation.2 | async-start | bytes 9437184 | tf_op jit(solution)/shard_map/all_to_all | solution.py:123
  230.1 1.5 convert_element_type.43
  231.6 52.7 %all-to-all-done.1 = bf16[64,32,1152]{2,1,0:T(8,128)(2,1)} async-done(((bf16[64,32,1152]{2,1,0:T(8,128)(2,1)}), bf16[64,32,1152]{2,1,0:T(8,128)(2,1)}, u32[]{:S(2)}, u32[]{:S(2)}) %all-to-all-start.1) | async-done | bytes 4718624 | tf_op jit(solution)/shard_map/all_to_all | solution.py:123
  284.3 4.6 %gather_fusion.6 = bf16[32,32,1152]{2,1,0:T(8,128)(2,1)} fusion(bf16[64,32,1152]{2,1,0:T(8,128)(2,1)} %all-to-all-done.1, s32[1024]{0:T(1024)S(1)} %pad_clamp_fusion.2), kind=kCustom, calls=%fused_computation.8 | custom fusion | bytes 4718720 | tf_op jit(solution)/shard_map/jit(_take)/gather | solution.py:147
  288.9 4.3 %copy.66 = bf16[1024,1152]{0,1:T(8,128)(2,1)} copy(bf16[1024,1152]{1,0:T(8,128)(2,1)} %bitcast.85) | data formatting | bytes 4718592 | tf_op jit(solution)/shard_map/jit(_take)/gather | solution.py:147
  293.1 3.3 broadcast_select_fusion.6
  296.4 1.2 fusion.4
  298.4 6.7 %add_convert_fusion = bf16[1024,1024]{0,1:T(8,128)(2,1)} fusion(bf16[1024,1152]{0,1:T(8,128)(2,1)} %broadcast_select_fusion.6, bf16[1024,1024]{1,0:T(8,128)(2,1)} %all-gather.6.cloned.1.call-done, bf16[1024,1024]{1,0:T(8,128)(2,1)} %param.11), kind=kOutput, calls=%fused_computation.15 | convolution fusion | flops 2150629376 | bytes 8388608 | tf_op jit(solution)/shard_map/dot_general | solution.py:89
  305.1 4.0 %copy.75 = bf16[1024,1024]{1,0:T(8,128)(2,1)} copy(bf16[1024,1024]{0,1:T(8,128)(2,1)} %add_convert_fusion) | data formatting | bytes 4194304
  309.1 61.8 %reduce-scatter.9.cloned.1.call-done = f32[192,1024]{1,0:T(8,128)} async-done(((f32[1536,1024]{1,0:T(8,128)}), f32[192,1024]{1,0:T(8,128)}) %reduce-scatter.9.cloned.1.call-update) | async-done | bytes 786448 | tf_op jit(solution)/shard_map/reduce_scatter | solution.py:142
  370.9 1.9 convert_element_type.42
  (115 shorter events, 11.3 us)
Async XLA Ops:
  7.2 8.2 %copy-start = (bf16[1024,1024]{1,0:T(8,128)(2,1)S(1)}, bf16[1024,1024]{1,0:T(8,128)(2,1)}, u32[]{:S(2)}) copy-start(bf16[1024,1024]{1,0:T(8,128)(2,1)} %param.10) | copy-start | bytes 6291460
  7.2 80.3 %all-gather.4.cloned.1.call-start = ((), (), s32[]{:S(2)}) async-start(), calls=%async_computation.7 | async-start | bytes 3981312 | tf_op jit(solution)/shard_map/all_gather | solution.py:74
  12.6 17.6 %copy-start.8 = (s32[32]{0:T(128)}, s32[32]{0:T(128)S(1)}, u32[]{:S(2)}) copy-start(s32[32]{0:T(128)S(1)} %gather_fusion.1) | copy-start | bytes 388
  13.3 0.5 copy-start.5
  23.7 5.2 %copy-start.13 = (u32[256]{0:T(256)S(1)}, u32[256]{0:T(256)}, u32[]{:S(2)}) copy-start(u32[256]{0:T(256)} %constant.209) | copy-start | bytes 3076
  23.7 76.9 %all-to-all-start = ((bf16[64,32,1152]{2,1,0:T(8,128)(2,1)}), bf16[64,32,1152]{2,1,0:T(8,128)(2,1)}, u32[]{:S(2)}, u32[]{:S(2)}) async-start(bf16[64,32,1152]{2,1,0:T(8,128)(2,1)} %pad_maximum_fusion), calls=%async_computation.1 | async-start | bytes 9437184 | tf_op jit(solution)/shard_map/all_to_all | solution.py:98
  28.8 121.4 %reduce-scatter.13.cloned.1.call-start = ((), (), s32[]{:S(2)}) async-start(), calls=%async_computation.11 | async-start | bytes 1179648
  93.3 7.3 %copy-start.11 = (pred[64]{0:T(512)(128)(4,1)S(1)}, pred[64]{0:T(512)(128)(4,1)}, u32[]{:S(2)}) copy-start(pred[64]{0:T(512)(128)(4,1)} %compare_and_fusion.2) | copy-start | bytes 196
  109.4 4.6 %copy-start.7 = (pred[4,32]{1,0:T(4,128)(4,1)S(1)}, pred[4,32]{1,0:T(4,128)(4,1)}, u32[]{:S(2)}) copy-start(pred[4,32]{1,0:T(4,128)(4,1)} %get-tuple-element.42) | copy-start | bytes 388
  113.9 116.2 %reduce-scatter.11.cloned.1.call-start = ((), (), s32[]{:S(2)}) async-start(), calls=%async_computation.10 | async-start | bytes 884736 | tf_op jit(solution)/shard_map/reduce_scatter | solution.py:143
  168.2 1.0 copy-start.2
  182.0 114.4 %reduce-scatter.7.cloned.1.call-start = ((), (), s32[]{:S(2)}) async-start(), calls=%async_computation.6 | async-start | bytes 4718592 | tf_op jit(solution)/shard_map/reduce_scatter | solution.py:80
  188.2 110.2 %all-gather.6.cloned.1.call-start = ((), (), s32[]{:S(2)}) async-start(), calls=%async_computation.8 | async-start | bytes 2359296 | tf_op jit(solution)/shard_map/all_gather | solution.py:88
  188.8 182.1 %reduce-scatter.9.cloned.1.call-start = ((), (), s32[]{:S(2)}) async-start(), calls=%async_computation.9 | async-start | bytes 7077888 | tf_op jit(solution)/shard_map/reduce_scatter | solution.py:142
  202.0 6.7 %copy-start.4 = (bf16[96,32,64]{2,1,0:T(8,128)(2,1)S(1)}, bf16[96,32,64]{2,1,0:T(8,128)(2,1)}, u32[]{:S(2)}) copy-start(bf16[96,32,64]{2,1,0:T(8,128)(2,1)} %get-tuple-element.49) | copy-start | bytes 1179652
  215.6 1.2 copy-start.3
  215.6 1.2 copy-start.12
  224.7 5.2 %copy-start.6 = (s32[32]{0:T(128)S(1)}, s32[32]{0:T(128)}, u32[]{:S(2)}) copy-start(s32[32]{0:T(128)} %copy-done.5) | copy-start | bytes 388
  224.8 5.2 %copy-start.9 = (s32[32]{0:T(128)S(1)}, s32[32]{0:T(128)}, u32[]{:S(2)}) copy-start(s32[32]{0:T(128)} %copy-done.8) | copy-start | bytes 388
  224.8 5.2 %copy-start.10 = (s32[32]{0:T(128)S(1)}, s32[32]{0:T(128)}, u32[]{:S(2)}) copy-start(s32[32]{0:T(128)} %get-tuple-element.40) | copy-start | bytes 388
  224.8 59.5 %all-to-all-start.1 = ((bf16[64,32,1152]{2,1,0:T(8,128)(2,1)}), bf16[64,32,1152]{2,1,0:T(8,128)(2,1)}, u32[]{:S(2)}, u32[]{:S(2)}) async-start(bf16[64,32,1152]{2,1,0:T(8,128)(2,1)} %pad_maximum_fusion.1), calls=%async_computation.2 | async-start | bytes 9437184 | tf_op jit(solution)/shard_map/all_to_all | solution.py:123
  298.4 74.4 %copy-start.1 = (bf16[1024,1024]{1,0:T(8,128)(2,1)S(1)}, bf16[1024,1024]{1,0:T(8,128)(2,1)}, u32[]{:S(2)}) copy-start(bf16[1024,1024]{1,0:T(8,128)(2,1)} %param.10) | copy-start | bytes 6291460
Sparse Core Ops, SparseCore 0:
  10.4 52.4 all-gather.3
  114.0 36.1 reduce-scatter.12
  182.2 32.3 reduce-scatter.10
  217.1 41.9 reduce-scatter.6
  260.9 31.6 all-gather.5
  295.2 75.7 reduce-scatter.8

commit v6 on v5

--- a/solution.py
+++ b/solution.py
@@ -77,17 +77,9 @@
     down_col = both_col[:, :, :width_loc]
     up_col = both_col[:, :, width_loc:]
 
-    base_t = lax.psum_scatter(
-        lax.dot_general(
-            value_weight, tokens, (((0,), (1,)), ((), ())), preferred_element_type=jnp.float32
-        ),
-        "mp",
-        scatter_dimension=0,
-        tiled=True,
-    )
-    cot_full = lax.all_gather(cotangent, "mp", axis=1, tiled=True)
-    base_bwd = lax.dot_general(
-        cot_full, value_weight, (((1,), (1,)), ((), ())), preferred_element_type=jnp.float32
+    n_mp = lax.axis_size("mp")
+    base_part = lax.dot_general(
+        value_weight, tokens, (((0,), (1,)), ((), ())), preferred_element_type=jnp.float32
     )
 
     token_blocks = tokens.reshape(blocks, blk, width_loc)
@@ -104,14 +96,20 @@
     up_sel = jnp.take(up_col, panel_at, axis=0)
     down_part = jnp.einsum("snd,srd->snr", tok_recv, down_sel, preferred_element_type=jnp.float32)
     up_part = jnp.einsum("snc,src->snr", cot_recv, up_sel, preferred_element_type=jnp.float32)
-    both = lax.all_gather(
-        lax.psum_scatter(jnp.stack([down_part, up_part]), "mp", scatter_dimension=1, tiled=True).astype(
-            jnp.bfloat16
-        ),
-        "mp",
-        axis=1,
-        tiled=True,
+    prod = jnp.stack([down_part, up_part]).reshape(2, n_mp, -1).transpose(1, 0, 2)
+    prod = prod.reshape(out_loc * n_mp, -1)
+    summed = lax.psum_scatter(
+        jnp.concatenate([base_part, prod], axis=1), "mp", scatter_dimension=0, tiled=True
     )
+    base_t = summed[:, :rows]
+    prod_mine = summed[:, rows:].reshape(-1).astype(jnp.bfloat16)
+    gathered = lax.all_gather(
+        jnp.concatenate([cotangent.reshape(-1), prod_mine]), "mp", axis=0, tiled=False
+    )
+    cot_full = gathered[:, : rows * out_loc].reshape(n_mp, rows, out_loc).transpose(1, 0, 2)
+    cot_full = cot_full.reshape(rows, n_mp * out_loc)
+    both = gathered[:, rows * out_loc:].reshape(n_mp, 2, -1, rank).transpose(1, 0, 2, 3)
+    both = both.reshape(2, capacity, blk, rank)
     down_low = both[0]
     up_grad = both[1]
 
@@ -139,11 +137,17 @@
     grad_b_col = jnp.einsum(
         "pnr,pnc->prc", low_p, cot_p, preferred_element_type=jnp.float32
     ).reshape(column * rank, out_loc)
-    grad_a = lax.psum_scatter(grad_a_col, "dz", scatter_dimension=0, tiled=True)
-    grad_b = lax.psum_scatter(grad_b_col, "dz", scatter_dimension=0, tiled=True)
+    grads = lax.psum_scatter(
+        jnp.concatenate([grad_a_col, grad_b_col], axis=1), "dz", scatter_dimension=0, tiled=True
+    )
+    grad_a = grads[:, :width_loc]
+    grad_b = grads[:, width_loc:]
     grad_a = grad_a.astype(jnp.bfloat16).reshape(stored, rank, width_loc)
     grad_b = grad_b.astype(jnp.bfloat16).reshape(stored, rank, out_loc)
 
+    base_bwd = lax.dot_general(
+        cot_full, value_weight, (((1,), (1,)), ((), ())), preferred_element_type=jnp.float32
+    )
     mine_back = jnp.take(back, position, axis=0).reshape(rows, width_loc + out_loc)
     values = (base_t.T + mine_back[:, width_loc:].astype(jnp.float32)).astype(jnp.bfloat16)
     token_gradient = (base_bwd + mine_back[:, :width_loc].astype(jnp.float32)).astype(jnp.bfloat16)

time: 381 us -> 317 us (0.83)
  waiting for transfers between devices: 144 us -> 105 us
  blocking collectives: 70.2 us -> 53.4 us
  local copies, waits for them, and re-layouts: 69.9 us -> 63.5 us
  matrix products: 35.5 us -> 30.6 us
    unnamed x7 -> x4, waiting for transfers between devices: 29 us -> 0.07 us
    all_gather x1 -> x0, blocking collectives: 16.8 us -> none  [shards(): lax.all_gather(lax.psum_scatter(jnp.stack([down_part, up_part]), 'mp', sc...]
    reduce_scatter x3 -> x2, waiting for transfers between devices: 61.8 us -> 46.7 us  [the longest x1 44.1 us: shards(): lax.psum_scatter(jnp.concatenate([base_part, prod], axis=1), 'mp', scatte...]
    unnamed x36 -> x16, local copies, waits for them, and re-layouts: 12.2 us -> 0.91 us
    concatenate x0 -> x3, other arithmetic: none -> 9.73 us  [the longest x1 5.43 us: shards(): jnp.concatenate([base_part, prod], axis=1)]
    all_gather x1, waiting for transfers between devices: 0.01 us -> 7.57 us  [shards(): lax.all_gather(jnp.concatenate([cotangent.reshape(-1), prod_mine]), 'mp',...]
    slice x0 -> x7, local copies, waits for them, and re-layouts: none -> 6.63 us  [the longest x1 3.05 us: shards(): gathered[:, :rows * out_loc].reshape(n_mp, rows, out_loc).transpose(1, 0, 2)]
    all_gather x0 -> x1, local copies, waits for them, and re-layouts: none -> 4.36 us  [shards(): lax.all_gather(jnp.concatenate([cotangent.reshape(-1), prod_mine]), 'mp',...]
  transfers between devices with their start and end apart: 8 -> 6, of which waited for: 3 -> 4; matrix products, arithmetic and copies ran while one was open for 28% -> 23% of each run, Pallas kernels for 0% -> 0%
where the time goes in v6:
time: 317 us; the launch traced here: 316 us
  waiting for transfers between devices  105 us (33%)
  local copies, waits for them, and re-layouts  63.5 us (20%)
  blocking collectives  53.4 us (17%)
  other arithmetic  37.4 us (12%)
  matrix products  30.6 us (10%)
  between operations  14.8 us (5%)
  starting transfers between devices  10.8 us (3%)
    unnamed x1, blocking collectives  53.4 us
    all_to_all x1, waiting for transfers between devices, shards(): lax.all_to_all(back_send, 'dx', split_axis=0, concat_axis=0, tiled=True)  50.9 us
    reduce_scatter x1, waiting for transfers between devices, shards(): lax.psum_scatter(jnp.concatenate([base_part, prod], axis=1), 'mp', scatte...  44.1 us
    gather x2, local copies, waits for them, and re-layouts, by_panel(): wide_p = jnp.take(wide, panel_slot.reshape(-1), axis=0)  8.84 us
    select_n x3, other arithmetic, by_panel(): wide_p = jnp.take(wide, panel_slot.reshape(-1), axis=0)  8.02 us
    all_gather x1, waiting for transfers between devices, shards(): lax.all_gather(jnp.concatenate([cotangent.reshape(-1), prod_mine]), 'mp',...  7.57 us
    gather x1, local copies, waits for them, and re-layouts, shards(): down_sel = jnp.take(down_col, panel_at, axis=0)  7.26 us
    dot_general x1, matrix products, shards(): jnp.einsum('snd,srd->snr', tok_recv, down_sel, preferred_element_type=jnp...  7.03 us
  transfers between devices with their start and end apart: 6, of which 4 were waited for; matrix products, arithmetic and copies ran while one was open for 23% of the time, Pallas kernels for 0%

profile of v6, /device:TPU:1, one launch (start us, length us, event | category | flops | bytes accessed | tf_op | source)
XLA Modules:
  0.0 315.7 jit_solution(14253720448633094890)
XLA Ops:
  7.2 2.0 pad_maximum_fusion.4
  9.9 1.4 gather_fusion
  11.2 1.4 gather_fusion.1
  12.9 1.6 gather_fusion.3
  14.6 2.7 gather_fusion.2
  17.5 2.6 broadcast_select_fusion.1
  20.1 2.8 pad_maximum_fusion.2
  22.9 5.2 %all-to-all-start = ((bf16[64,32,1152]{2,1,0:T(8,128)(2,1)}), bf16[64,32,1152]{2,1,0:T(8,128)(2,1)}, u32[]{:S(2)}, u32[]{:S(2)}) async-start(bf16[64,32,1152]{2,1,0:T(8,128)(2,1)} %pad_maximum_fusion.2), calls=%async_computation | async-start | bytes 9437184 | tf_op jit(solution)/shard_map/all_to_all | solution.py:90
  29.6 53.4 %all-reduce = s32[128]{0:T(128)S(1)} all-reduce(s32[128]{0:T(128)S(1)} %dynamic-update-slice), channel_id=2, replica_groups=mesh['dz'=8,'dx'=4,'mp'=8] {'dx'}, use_global_device_ids=true, to_apply=%add | all-reduce | flops 128 | bytes 1024
  85.7 5.9 %fusion.41 = f32[1024,1024]{0,1:T(8,128)} fusion(bf16[1024,1024]{1,0:T(8,128)(2,1)S(1)} %copy-done, bf16[1024,1024]{1,0:T(8,128)(2,1)} %param.11), kind=kOutput, calls=%fused_computation.144 | convolution fusion | flops 2147483648 | bytes 8388608 | tf_op jit(solution)/shard_map/dot_general | solution.py:81
  91.7 1.0 slice.86
  93.5 1.8 fusion.10
  95.9 4.1 %slice.84 = bf16[24,64,1024]{2,1,0:T(8,128)(2,1)} slice(bf16[24,64,1152]{2,1,0:T(8,128)(2,1)} %all-gather.5.cloned.1.call-done), slice={[0:24], [0:64], [0:1024]} | slice | bytes 6291456 | tf_op jit(solution)/shard_map/slice | solution.py:77
  100.0 7.3 %gather_fusion.4 = bf16[64,64,1024]{2,1,0:T(8,128)(2,1)} fusion(bf16[24,64,1024]{2,1,0:T(8,128)(2,1)} %slice.84, s32[1024]{0:T(1024)S(1)} %pad_clamp_fusion.3), kind=kCustom, calls=%fused_computation.6 | custom fusion | bytes 16777472 | tf_op jit(solution)/shard_map/jit(_take)/gather | solution.py:95
  107.3 7.0 %fusion.1 = f32[64,32,64]{2,1,0:T(8,128)S(1)} fusion(bf16[64,64,1024]{2,1,0:T(8,128)(2,1)} %gather_fusion.4, pred[64]{0:T(512)(128)(4,1)S(1)} %compare_and_fusion.3, bf16[64,32,1152]{2,1,0:T(8,128)(2,1)} %all-to-all-done), kind=kOutput, calls=%fused_computation.20 | convolution fusion | flops 272629760 | bytes 13107264 | tf_op jit(solution)/shard_map/snd,srd->snr/dot_general | solution.py:97
  115.0 0.9 maximum_bitcast_fusion
  115.9 0.9 reshape.351
  117.2 5.4 %pad_maximum_fusion.1 = f32[1024,1280]{0,1:T(8,128)} fusion(f32[1024,256]{0,1:T(8,128)S(1)} %copy.64, f32[1024,1024]{0,1:T(8,128)} %fusion.41), kind=kLoop, calls=%fused_computation.14 | loop fusion | flops 1310720 | bytes 10485760 | tf_op jit(solution)/shard_map/concatenate | solution.py:102
  122.7 44.1 %reduce-scatter.3.cloned.1.call-done = f32[128,1280]{0,1:T(8,128)} async-done(((f32[1024,1280]{0,1:T(8,128)}), f32[128,1280]{0,1:T(8,128)}) %reduce-scatter.3.cloned.1.call-update) | async-done | bytes 655376 | tf_op jit(solution)/shard_map/reduce_scatter | solution.py:101
  166.8 0.9 slice.109
  170.0 1.1 slice.85
  171.8 5.0 %slice.83 = bf16[64,32,1024]{2,1,0:T(8,128)(2,1)} slice(bf16[64,32,1152]{2,1,0:T(8,128)(2,1)} %all-to-all-done), slice={[0:64], [0:32], [0:1024]} | slice | bytes 8388608 | tf_op jit(solution)/shard_map/slice | solution.py:91
  176.8 8.1 %gather_fusion.7 = bf16[96,32,1024]{2,1,0:T(8,128)(2,1)} fusion(bf16[64,32,1024]{2,1,0:T(8,128)(2,1)} %slice.83, s32[1024]{0:T(1024)S(1)} %pad_clamp_fusion), kind=kCustom, calls=%fused_computation.9 | custom fusion | bytes 12583296 | tf_op jit(solution)/shard_map/jit(_take)/gather | solution.py:126
  184.9 1.3 bitcast_select_fusion.2
  186.3 6.7 %bitcast_select_fusion = bf16[24,128,1024]{2,1,0:T(8,128)(2,1)} fusion(pred[24,128]{1,0:T(8,128)(4,1)S(1)} %broadcast_in_dim.192, bf16[24,128,1024]{2,1,0:T(8,128)(2,1)} %bitcast.89), kind=kLoop, calls=%fused_computation.13 | loop fusion | flops 3145728 | bytes 12585984 | tf_op jit(solution)/shard_map/jit(_take)/select_n | solution.py:126
  193.0 7.6 %all-gather.7.cloned.1.call-done = bf16[1310720]{0:T(1024)(128)(2,1)} async-done(((bf16[163840]{0:T(1024)(128)(2,1)}), bf16[1310720]{0:T(1024)(128)(2,1)}) %all-gather.7.cloned.1.call-update) | async-done | bytes 2621456 | tf_op jit(solution)/shard_map/all_gather | solution.py:106
  200.5 4.4 %reshape.451 = bf16[8,163840]{1,0:T(8,128)(2,1)} reshape(bf16[1310720]{0:T(1024)(128)(2,1)} %all-gather.7.cloned.1.call-done) | data formatting | bytes 5242880 | tf_op jit(solution)/shard_map/all_gather | solution.py:106
  204.9 1.1 slice.89
  206.0 1.1 reshape.353
  207.9 1.6 gather_fusion.10
  209.5 2.5 broadcast_select_fusion.8
  212.0 1.4 copy.71
  213.4 1.4 copy.68
  214.9 1.5 fusion.11
  216.3 3.8 %fusion.13 = f32[24,64,1024]{2,1,0:T(8,128)S(1)} fusion(bf16[24,128,1024]{2,1,0:T(8,128)(2,1)} %bitcast_select_fusion, bf16[24,128,64]{1,2,0:T(8,128)(2,1)S(1)} %copy.68, pred[24,128]{1,0:T(8,128)(4,1)S(1)} %broadcast_in_dim.189), kind=kOutput, calls=%fused_computation.40 | convolution fusion | flops 402849792 | bytes 12979200 | tf_op jit(solution)/shard_map/pnr,pnd->prd/dot_general | solution.py:133
  220.1 3.6 %pad_maximum_fusion = f32[1536,1152]{1,0:T(8,128)} fusion(f32[1536,128]{1,0:T(8,128)S(1)} %bitcast.95, f32[1536,1024]{1,0:T(8,128)S(1)} %bitcast.88), kind=kLoop, calls=%fused_computation.12 | loop fusion | flops 1769472 | bytes 14155776 | tf_op jit(solution)/shard_map/concatenate | solution.py:141
  224.2 4.7 %fusion.2 = bf16[64,32,1024]{2,1,0:T(8,128)(2,1)S(1)} fusion(bf16[64,32,64]{2,1,0:T(8,128)(2,1)S(1)} %bitcast.92, bf16[64,64,1024]{2,1,0:T(8,128)(2,1)} %gather_fusion.4, pred[64]{0:T(512)(128)(4,1)S(1)} %compare_and_fusion.3), kind=kOutput, calls=%fused_computation.21 | convolution fusion | flops 274726912 | bytes 12845120 | tf_op jit(solution)/shard_map/snr,srd->snd/dot_general | solution.py:117
  228.9 2.7 pad_maximum_fusion.3
  231.6 5.2 %all-to-all-start.1 = ((bf16[64,32,1152]{2,1,0:T(8,128)(2,1)}), bf16[64,32,1152]{2,1,0:T(8,128)(2,1)}, u32[]{:S(2)}, u32[]{:S(2)}) async-start(bf16[64,32,1152]{2,1,0:T(8,128)(2,1)} %pad_maximum_fusion.3), calls=%async_computation.2 | async-start | bytes 9437184 | tf_op jit(solution)/shard_map/all_to_all | solution.py:121
  237.0 3.0 slice.93
  240.1 50.9 %all-to-all-done.1 = bf16[64,32,1152]{2,1,0:T(8,128)(2,1)} async-done(((bf16[64,32,1152]{2,1,0:T(8,128)(2,1)}), bf16[64,32,1152]{2,1,0:T(8,128)(2,1)}, u32[]{:S(2)}, u32[]{:S(2)}) %all-to-all-start.1) | async-done | bytes 4718624 | tf_op jit(solution)/shard_map/all_to_all | solution.py:121
  290.9 4.7 %gather_fusion.6 = bf16[32,32,1152]{2,1,0:T(8,128)(2,1)} fusion(bf16[64,32,1152]{2,1,0:T(8,128)(2,1)} %all-to-all-done.1, s32[1024]{0:T(1024)S(1)} %pad_clamp_fusion.2), kind=kCustom, calls=%fused_computation.8 | custom fusion | bytes 4718720 | tf_op jit(solution)/shard_map/jit(_take)/gather | solution.py:151
  295.6 2.1 bitcast_select_fusion.1
  297.8 0.8 fusion.9
  298.5 5.5 %add_convert_fusion = bf16[1024,1024]{1,0:T(8,128)(2,1)} fusion(bf16[1024,1152]{1,0:T(8,128)(2,1)S(1)} %bitcast_select_fusion.1, bf16[1024,1024]{1,0:T(8,128)(2,1)} %param.11, bf16[128,8,8,128]{3,2,1,0:T(8,128)(2,1)S(1)} %bitcast.101), kind=kOutput, calls=%fused_computation.17 | convolution fusion | flops 2150629376 | bytes 8388608 | tf_op jit(solution)/shard_map/dot_general | solution.py:148
  304.0 2.5 reduce-scatter.5.cloned.1.call-done
  306.5 1.2 convert.8
  307.8 0.8 slice.95
  (101 shorter events, 12.3 us)
Async XLA Ops:
  7.2 7.4 %copy-start = (bf16[1024,1024]{1,0:T(8,128)(2,1)S(1)}, bf16[1024,1024]{1,0:T(8,128)(2,1)}, u32[]{:S(2)}) copy-start(bf16[1024,1024]{1,0:T(8,128)(2,1)} %param.10) | copy-start | bytes 6291460
  7.2 84.5 %all-gather.5.cloned.1.call-start = ((), (), s32[]{:S(2)}) async-start(), calls=%async_computation.4 | async-start | bytes 3981312 | tf_op jit(solution)/shard_map/all_gather | solution.py:74
  22.9 5.3 %copy-start.5 = (u32[256]{0:T(256)S(1)}, u32[256]{0:T(256)}, u32[]{:S(2)}) copy-start(u32[256]{0:T(256)} %constant.209) | copy-start | bytes 3076
  22.9 70.6 %all-to-all-start = ((bf16[64,32,1152]{2,1,0:T(8,128)(2,1)}), bf16[64,32,1152]{2,1,0:T(8,128)(2,1)}, u32[]{:S(2)}, u32[]{:S(2)}) async-start(bf16[64,32,1152]{2,1,0:T(8,128)(2,1)} %pad_maximum_fusion.2), calls=%async_computation | async-start | bytes 9437184 | tf_op jit(solution)/shard_map/all_to_all | solution.py:90
  28.1 138.7 %reduce-scatter.3.cloned.1.call-start = ((), (), s32[]{:S(2)}) async-start(), calls=%async_computation.5 | async-start | bytes 5898240 | tf_op jit(solution)/shard_map/reduce_scatter | solution.py:101
  122.6 45.3 %copy-start.2 = (bf16[1024,128]{1,0:T(8,128)(2,1)S(1)}, bf16[1024,128]{1,0:T(8,128)(2,1)}, u32[]{:S(2)}) copy-start(bf16[1024,128]{1,0:T(8,128)(2,1)} %param.14) | copy-start | bytes 786436
  122.6 77.9 %all-gather.7.cloned.1.call-start = ((), (), s32[]{:S(2)}) async-start(), calls=%async_computation.7 | async-start | bytes 2949120 | tf_op jit(solution)/shard_map/all_gather | solution.py:106
  168.7 137.9 %reduce-scatter.5.cloned.1.call-start = ((), (), s32[]{:S(2)}) async-start(), calls=%async_computation.6 | async-start | bytes 7962624 | tf_op jit(solution)/shard_map/reduce_scatter | solution.py:140
  231.6 59.3 %all-to-all-start.1 = ((bf16[64,32,1152]{2,1,0:T(8,128)(2,1)}), bf16[64,32,1152]{2,1,0:T(8,128)(2,1)}, u32[]{:S(2)}, u32[]{:S(2)}) async-start(bf16[64,32,1152]{2,1,0:T(8,128)(2,1)} %pad_maximum_fusion.3), calls=%async_computation.2 | async-start | bytes 9437184 | tf_op jit(solution)/shard_map/all_to_all | solution.py:121
  240.1 57.7 %copy-start.4 = (f32[128,1280]{0,1:T(8,128)S(1)}, f32[128,1280]{0,1:T(8,128)}, u32[]{:S(2)}) copy-start(f32[128,1280]{0,1:T(8,128)} %reduce-scatter.3.cloned.1.call-done) | copy-start | bytes 1966084
  295.6 2.9 copy-start.3
  298.5 10.7 %copy-start.1 = (bf16[1024,1024]{1,0:T(8,128)(2,1)S(1)}, bf16[1024,1024]{1,0:T(8,128)(2,1)}, u32[]{:S(2)}) copy-start(bf16[1024,1024]{1,0:T(8,128)(2,1)} %param.10) | copy-start | bytes 6291460
Sparse Core Ops, SparseCore 0:
  10.4 52.4 all-gather.4
  122.7 44.0 reduce-scatter.2
  169.2 31.2 all-gather.6
  223.8 82.6 reduce-scatter.4

commit v7 on v6

--- a/solution.py
+++ b/solution.py
@@ -49,7 +49,11 @@
         jnp.where(position[None, :] == slot_ids[:, None], block_ids[None, :], 0), axis=1
     )
 
-    x_location = lax.all_gather(location, "dx", axis=0, tiled=False)
+    base_part = lax.dot_general(
+        value_weight, tokens, (((0,), (1,)), ((), ())), preferred_element_type=jnp.float32
+    )
+    location_tied, base_part = lax.optimization_barrier((location, base_part))
+    x_location = lax.all_gather(location_tied, "dx", axis=0, tiled=False)
     x_owner_x = (x_location // stored) % n_x
     x_rank = earlier_same(x_owner_x)
     in_column = (x_location // stored // n_x) * stored + x_location % stored
@@ -78,9 +82,6 @@
     up_col = both_col[:, :, width_loc:]
 
     n_mp = lax.axis_size("mp")
-    base_part = lax.dot_general(
-        value_weight, tokens, (((0,), (1,)), ((), ())), preferred_element_type=jnp.float32
-    )
 
     token_blocks = tokens.reshape(blocks, blk, width_loc)
     cot_blocks = cotangent.reshape(blocks, blk, out_loc)
@@ -106,8 +107,7 @@
     gathered = lax.all_gather(
         jnp.concatenate([cotangent.reshape(-1), prod_mine]), "mp", axis=0, tiled=False
     )
-    cot_full = gathered[:, : rows * out_loc].reshape(n_mp, rows, out_loc).transpose(1, 0, 2)
-    cot_full = cot_full.reshape(rows, n_mp * out_loc)
+    cot_parts = gathered[:, : rows * out_loc].reshape(n_mp, rows, out_loc)
     both = gathered[:, rows * out_loc:].reshape(n_mp, 2, -1, rank).transpose(1, 0, 2, 3)
     both = both.reshape(2, capacity, blk, rank)
     down_low = both[0]
@@ -145,8 +145,11 @@
     grad_a = grad_a.astype(jnp.bfloat16).reshape(stored, rank, width_loc)
     grad_b = grad_b.astype(jnp.bfloat16).reshape(stored, rank, out_loc)
 
-    base_bwd = lax.dot_general(
-        cot_full, value_weight, (((1,), (1,)), ((), ())), preferred_element_type=jnp.float32
+    base_bwd = jnp.einsum(
+        "krc,dkc->rd",
+        cot_parts,
+        value_weight.reshape(width_loc, n_mp, out_loc),
+        preferred_element_type=jnp.float32,
     )
     mine_back = jnp.take(back, position, axis=0).reshape(rows, width_loc + out_loc)
     values = (base_t.T + mine_back[:, width_loc:].astype(jnp.float32)).astype(jnp.bfloat16)

time: 317 us -> 319 us (level)
  local copies, waits for them, and re-layouts: 63.5 us -> 74.4 us
  blocking collectives: 53.4 us -> 47.5 us
    unnamed x16 -> x22, local copies, waits for them, and re-layouts: 0.91 us -> 11 us
    unnamed x1, blocking collectives: 53.4 us -> 47.5 us
    gather x1 -> x2, local copies, waits for them, and re-layouts: 4.67 us -> 9.01 us  [shards(): jnp.take(back, position, axis=0).reshape(rows, width_loc + out_loc)]
    slice x3 -> x0, local copies, waits for them, and re-layouts: 4.06 us -> none  [the longest x1 3.05 us: shards(): gathered[:, :rows * out_loc].reshape(n_mp, rows, out_loc).transpose(1, 0, 2)]
  transfers between devices with their start and end apart: 6 -> 6, of which waited for: 4 -> 3; matrix products, arithmetic and copies ran while one was open for 23% -> 26% of each run, Pallas kernels for 0% -> 0%
where the time goes in v7:
time: 319 us; the launch traced here: 318 us
  waiting for transfers between devices  103 us (32%)
  local copies, waits for them, and re-layouts  74.4 us (23%)
  blocking collectives  47.5 us (15%)
  other arithmetic  36.1 us (11%)
  matrix products  32 us (10%)
  between operations  14.8 us (5%)
  starting transfers between devices  10.6 us (3%)
    all_to_all x1, waiting for transfers between devices, shards(): lax.all_to_all(back_send, 'dx', split_axis=0, concat_axis=0, tiled=True)  50.9 us
    unnamed x1, blocking collectives  47.5 us
    reduce_scatter x1, waiting for transfers between devices, shards(): lax.psum_scatter(jnp.concatenate([base_part, prod], axis=1), 'mp', scatte...  44 us
    unnamed x22, local copies, waits for them, and re-layouts  11 us
    gather x2, local copies, waits for them, and re-layouts, shards(): jnp.take(back, position, axis=0).reshape(rows, width_loc + out_loc)  9.01 us
    gather x2, local copies, waits for them, and re-layouts, by_panel(): wide_p = jnp.take(wide, panel_slot.reshape(-1), axis=0)  8.84 us
    select_n x3, other arithmetic, by_panel(): wide_p = jnp.take(wide, panel_slot.reshape(-1), axis=0)  8.02 us
    all_gather x1, waiting for transfers between devices, shards(): lax.all_gather(jnp.concatenate([cotangent.reshape(-1), prod_mine]), 'mp',...  7.69 us
  transfers between devices with their start and end apart: 6, of which 3 were waited for; matrix products, arithmetic and copies ran while one was open for 26% of the time, Pallas kernels for 0%

profile of v7, /device:TPU:1, one launch (start us, length us, event | category | flops | bytes accessed | tf_op | source)
XLA Modules:
  0.0 318.1 jit_solution(8214834924263422159)
XLA Ops:
  7.2 2.0 pad_maximum_fusion.4
  9.9 1.4 gather_fusion
  11.2 1.4 gather_fusion.1
  12.9 1.6 gather_fusion.3
  14.6 2.7 gather_fusion.2
  17.5 2.6 broadcast_select_fusion.1
  20.1 2.8 pad_maximum_fusion.2
  22.9 5.0 %all-to-all-start = ((bf16[64,32,1152]{2,1,0:T(8,128)(2,1)}), bf16[64,32,1152]{2,1,0:T(8,128)(2,1)}, u32[]{:S(2)}, u32[]{:S(2)}) async-start(bf16[64,32,1152]{2,1,0:T(8,128)(2,1)} %pad_maximum_fusion.2), calls=%async_computation | async-start | bytes 9437184 | tf_op jit(solution)/shard_map/all_to_all | solution.py:91
  28.0 6.0 %fusion.42 = f32[1024,1024]{1,0:T(8,128)} fusion(bf16[1024,1024]{1,0:T(8,128)(2,1)} %param.11, bf16[1024,1024]{1,0:T(8,128)(2,1)S(1)} %copy-done), kind=kOutput, calls=%fused_computation.148 | convolution fusion | flops 2147483648 | bytes 8388608 | tf_op jit(solution)/shard_map/dot_general | solution.py:52
  35.4 47.5 %all-reduce = s32[128]{0:T(128)S(1)} all-reduce(s32[128]{0:T(128)S(1)} %dynamic-update-slice), channel_id=2, replica_groups=mesh['dz'=8,'dx'=4,'mp'=8] {'dx'}, use_global_device_ids=true, to_apply=%add | all-reduce | flops 128 | bytes 1024
  85.7 1.0 slice.86
  87.5 1.8 fusion.10
  89.2 1.5 stack.81
  90.7 4.1 %slice.84 = bf16[24,64,1024]{2,1,0:T(8,128)(2,1)} slice(bf16[24,64,1152]{2,1,0:T(8,128)(2,1)} %all-gather.5.cloned.1.call-done), slice={[0:24], [0:64], [0:1024]} | slice | bytes 6291456 | tf_op jit(solution)/shard_map/slice | solution.py:81
  94.8 7.3 %gather_fusion.4 = bf16[64,64,1024]{2,1,0:T(8,128)(2,1)} fusion(bf16[24,64,1024]{2,1,0:T(8,128)(2,1)} %slice.84, s32[1024]{0:T(1024)S(1)} %pad_clamp_fusion.3), kind=kCustom, calls=%fused_computation.6 | custom fusion | bytes 16777472 | tf_op jit(solution)/shard_map/jit(_take)/gather | solution.py:96
  102.1 7.1 %fusion.2 = f32[64,32,64]{2,1,0:T(8,128)S(1)} fusion(bf16[64,64,1024]{2,1,0:T(8,128)(2,1)} %gather_fusion.4, pred[64]{0:T(512)(128)(4,1)S(1)} %compare_and_fusion.3, bf16[64,32,1152]{2,1,0:T(8,128)(2,1)} %all-to-all-done), kind=kOutput, calls=%fused_computation.21 | convolution fusion | flops 272629760 | bytes 13107264 | tf_op jit(solution)/shard_map/snd,srd->snr/dot_general | solution.py:98
  109.9 0.9 maximum_bitcast_fusion
  111.7 5.0 %pad_maximum_fusion.1 = f32[1024,1280]{1,0:T(8,128)} fusion(f32[1024,256]{1,0:T(8,128)S(1)} %reshape.351, f32[1024,1024]{1,0:T(8,128)} %fusion.42), kind=kLoop, calls=%fused_computation.14 | loop fusion | flops 1310720 | bytes 10485760 | tf_op jit(solution)/shard_map/concatenate | solution.py:103
  116.8 44.0 %reduce-scatter.3.cloned.1.call-done = f32[128,1280]{1,0:T(8,128)} async-done(((f32[1024,1280]{1,0:T(8,128)}), f32[128,1280]{1,0:T(8,128)}) %reduce-scatter.3.cloned.1.call-update) | async-done | bytes 655376 | tf_op jit(solution)/shard_map/reduce_scatter | solution.py:102
  160.8 0.9 fusion.19
  164.0 1.1 slice.85
  165.8 5.0 %slice.83 = bf16[64,32,1024]{2,1,0:T(8,128)(2,1)} slice(bf16[64,32,1152]{2,1,0:T(8,128)(2,1)} %all-to-all-done), slice={[0:64], [0:32], [0:1024]} | slice | bytes 8388608 | tf_op jit(solution)/shard_map/slice | solution.py:92
  170.7 8.1 %gather_fusion.7 = bf16[96,32,1024]{2,1,0:T(8,128)(2,1)} fusion(bf16[64,32,1024]{2,1,0:T(8,128)(2,1)} %slice.83, s32[1024]{0:T(1024)S(1)} %pad_clamp_fusion), kind=kCustom, calls=%fused_computation.9 | custom fusion | bytes 12583296 | tf_op jit(solution)/shard_map/jit(_take)/gather | solution.py:126
  178.9 1.3 bitcast_select_fusion.1
  180.2 6.7 %bitcast_select_fusion = bf16[24,128,1024]{2,1,0:T(8,128)(2,1)} fusion(pred[24,128]{1,0:T(8,128)(4,1)S(1)} %broadcast_in_dim.192, bf16[24,128,1024]{2,1,0:T(8,128)(2,1)} %bitcast.95), kind=kLoop, calls=%fused_computation.13 | loop fusion | flops 3145728 | bytes 12585984 | tf_op jit(solution)/shard_map/jit(_take)/select_n | solution.py:126
  186.9 7.7 %all-gather.7.cloned.1.call-done = bf16[1310720]{0:T(1024)(128)(2,1)} async-done(((bf16[163840]{0:T(1024)(128)(2,1)}), bf16[1310720]{0:T(1024)(128)(2,1)}) %all-gather.7.cloned.1.call-update) | async-done | bytes 2621456 | tf_op jit(solution)/shard_map/all_gather | solution.py:107
  194.6 4.4 %reshape.451 = bf16[8,163840]{1,0:T(8,128)(2,1)} reshape(bf16[1310720]{0:T(1024)(128)(2,1)} %all-gather.7.cloned.1.call-done) | data formatting | bytes 5242880 | tf_op jit(solution)/shard_map/all_gather | solution.py:107
  198.9 1.1 slice.89
  200.0 1.1 reshape.353
  201.9 1.6 gather_fusion.10
  203.5 2.5 broadcast_select_fusion.9
  206.1 1.4 copy.85
  207.5 1.4 copy.82
  208.9 1.5 fusion.11
  210.4 3.8 %fusion.13 = f32[24,64,1024]{2,1,0:T(8,128)S(1)} fusion(bf16[24,128,1024]{2,1,0:T(8,128)(2,1)} %bitcast_select_fusion, bf16[24,128,64]{1,2,0:T(8,128)(2,1)S(1)} %copy.82, pred[24,128]{1,0:T(8,128)(4,1)S(1)} %broadcast_in_dim.189), kind=kOutput, calls=%fused_computation.43 | convolution fusion | flops 402849792 | bytes 12979200 | tf_op jit(solution)/shard_map/pnr,pnd->prd/dot_general | solution.py:133
  214.2 3.6 %pad_maximum_fusion = f32[1536,1152]{1,0:T(8,128)} fusion(f32[1536,128]{1,0:T(8,128)S(1)} %bitcast.102, f32[1536,1024]{1,0:T(8,128)S(1)} %bitcast.94), kind=kLoop, calls=%fused_computation.12 | loop fusion | flops 1769472 | bytes 14155776 | tf_op jit(solution)/shard_map/concatenate | solution.py:141
  218.2 4.7 %fusion.3 = bf16[64,32,1024]{2,1,0:T(8,128)(2,1)S(1)} fusion(bf16[64,32,64]{2,1,0:T(8,128)(2,1)S(1)} %bitcast.99, bf16[64,64,1024]{2,1,0:T(8,128)(2,1)} %gather_fusion.4, pred[64]{0:T(512)(128)(4,1)S(1)} %compare_and_fusion.3), kind=kOutput, calls=%fused_computation.22 | convolution fusion | flops 274726912 | bytes 12845120 | tf_op jit(solution)/shard_map/snr,srd->snd/dot_general | solution.py:117
  222.9 2.7 pad_maximum_fusion.3
  225.7 5.2 %all-to-all-start.1 = ((bf16[64,32,1152]{2,1,0:T(8,128)(2,1)}), bf16[64,32,1152]{2,1,0:T(8,128)(2,1)}, u32[]{:S(2)}, u32[]{:S(2)}) async-start(bf16[64,32,1152]{2,1,0:T(8,128)(2,1)} %pad_maximum_fusion.3), calls=%async_computation.2 | async-start | bytes 9437184 | tf_op jit(solution)/shard_map/all_to_all | solution.py:121
  231.1 3.0 slice_bitcast_fusion
  234.1 50.9 %all-to-all-done.1 = bf16[64,32,1152]{2,1,0:T(8,128)(2,1)} async-done(((bf16[64,32,1152]{2,1,0:T(8,128)(2,1)}), bf16[64,32,1152]{2,1,0:T(8,128)(2,1)}, u32[]{:S(2)}, u32[]{:S(2)}) %all-to-all-start.1) | async-done | bytes 4718624 | tf_op jit(solution)/shard_map/all_to_all | solution.py:121
  285.0 4.7 %gather_fusion.6 = bf16[32,32,1152]{2,1,0:T(8,128)(2,1)} fusion(bf16[64,32,1152]{2,1,0:T(8,128)(2,1)} %all-to-all-done.1, s32[1024]{0:T(1024)S(1)} %pad_clamp_fusion.2), kind=kCustom, calls=%fused_computation.8 | custom fusion | bytes 4718720 | tf_op jit(solution)/shard_map/jit(_take)/gather | solution.py:154
  289.6 4.3 %copy.77 = bf16[1024,1152]{0,1:T(8,128)(2,1)} copy(bf16[1024,1152]{1,0:T(8,128)(2,1)} %bitcast.96) | data formatting | bytes 4718592 | tf_op jit(solution)/shard_map/jit(_take)/gather | solution.py:154
  294.0 1.9 broadcast_select_fusion.6
  295.9 1.4 copy-done.2
  298.2 6.8 %fusion = bf16[1024,1024]{0,1:T(8,128)(2,1)} fusion(bf16[1,8,1024,128]{3,1,2,0:T(8,128)(2,1)} %slice_bitcast_fusion, bf16[1024,1152]{0,1:T(8,128)(2,1)} %copy-done.2, bf16[1024,1024]{1,0:T(8,128)(2,1)} %param.11), kind=kOutput, calls=%fused_computation.18 | convolution fusion | flops 2150629376 | bytes 8388608 | tf_op jit(solution)/shard_map/krc,dkc->rd/dot_general | solution.py:148
  305.0 3.9 %copy.87 = bf16[1024,1024]{1,0:T(8,128)(2,1)} copy(bf16[1024,1024]{0,1:T(8,128)(2,1)} %fusion) | data formatting | bytes 4194304
  308.9 1.2 convert.8
  (104 shorter events, 13.8 us)
Async XLA Ops:
  7.2 7.4 %copy-start = (bf16[1024,1024]{1,0:T(8,128)(2,1)S(1)}, bf16[1024,1024]{1,0:T(8,128)(2,1)}, u32[]{:S(2)}) copy-start(bf16[1024,1024]{1,0:T(8,128)(2,1)} %param.10) | copy-start | bytes 6291460
  7.2 78.5 %all-gather.5.cloned.1.call-start = ((), (), s32[]{:S(2)}) async-start(), calls=%async_computation.4 | async-start | bytes 3981312 | tf_op jit(solution)/shard_map/all_gather | solution.py:78
  22.9 64.6 %all-to-all-start = ((bf16[64,32,1152]{2,1,0:T(8,128)(2,1)}), bf16[64,32,1152]{2,1,0:T(8,128)(2,1)}, u32[]{:S(2)}, u32[]{:S(2)}) async-start(bf16[64,32,1152]{2,1,0:T(8,128)(2,1)} %pad_maximum_fusion.2), calls=%async_computation | async-start | bytes 9437184 | tf_op jit(solution)/shard_map/all_to_all | solution.py:91
  27.9 132.9 %reduce-scatter.3.cloned.1.call-start = ((), (), s32[]{:S(2)}) async-start(), calls=%async_computation.5 | async-start | bytes 5898240 | tf_op jit(solution)/shard_map/reduce_scatter | solution.py:102
  27.9 6.0 %copy-start.6 = (u32[256]{0:T(256)S(1)}, u32[256]{0:T(256)}, u32[]{:S(2)}) copy-start(u32[256]{0:T(256)} %constant.209) | copy-start | bytes 3076
  102.1 7.8 %copy-start.4 = (f32[1,8,16384]{2,0,1:T(1,128)S(1)}, f32[1,8,16384]{2,0,1:T(1,128)}, u32[]{:S(2)}) copy-start(f32[1,8,16384]{2,0,1:T(1,128)} %stack.81) | copy-start | bytes 1572868
  116.7 45.1 %copy-start.3 = (bf16[1024,128]{1,0:T(8,128)(2,1)S(1)}, bf16[1024,128]{1,0:T(8,128)(2,1)}, u32[]{:S(2)}) copy-start(bf16[1024,128]{1,0:T(8,128)(2,1)} %param.14) | copy-start | bytes 786436
  116.7 77.8 %all-gather.7.cloned.1.call-start = ((), (), s32[]{:S(2)}) async-start(), calls=%async_computation.7 | async-start | bytes 2949120 | tf_op jit(solution)/shard_map/all_gather | solution.py:107
  162.6 146.3 %reduce-scatter.5.cloned.1.call-start = ((), (), s32[]{:S(2)}) async-start(), calls=%async_computation.6 | async-start | bytes 7962624 | tf_op jit(solution)/shard_map/reduce_scatter | solution.py:140
  225.7 59.3 %all-to-all-start.1 = ((bf16[64,32,1152]{2,1,0:T(8,128)(2,1)}), bf16[64,32,1152]{2,1,0:T(8,128)(2,1)}, u32[]{:S(2)}, u32[]{:S(2)}) async-start(bf16[64,32,1152]{2,1,0:T(8,128)(2,1)} %pad_maximum_fusion.3), calls=%async_computation.2 | async-start | bytes 9437184 | tf_op jit(solution)/shard_map/all_to_all | solution.py:121
  289.6 7.7 %copy-start.5 = (f32[128,1280]{1,0:T(8,128)S(1)}, f32[128,1280]{1,0:T(8,128)}, u32[]{:S(2)}) copy-start(f32[128,1280]{1,0:T(8,128)} %reduce-scatter.3.cloned.1.call-done) | copy-start | bytes 1966084
  295.9 1.4 copy-start.2
  298.2 13.3 %copy-start.1 = (bf16[1024,1024]{1,0:T(8,128)(2,1)S(1)}, bf16[1024,1024]{1,0:T(8,128)(2,1)}, u32[]{:S(2)}) copy-start(bf16[1024,1024]{1,0:T(8,128)(2,1)} %param.10) | copy-start | bytes 6291460
Sparse Core Ops, SparseCore 0:
  10.4 52.4 all-gather.4
  116.9 43.9 reduce-scatter.2
  163.2 31.2 all-gather.6
  217.9 82.6 reduce-scatter.4

commit v8 on v7

--- a/solution.py
+++ b/solution.py
@@ -53,6 +53,7 @@
         value_weight, tokens, (((0,), (1,)), ((), ())), preferred_element_type=jnp.float32
     )
     location_tied, base_part = lax.optimization_barrier((location, base_part))
+    base_t = lax.psum_scatter(base_part, "mp", scatter_dimension=0, tiled=True)
     x_location = lax.all_gather(location_tied, "dx", axis=0, tiled=False)
     x_owner_x = (x_location // stored) % n_x
     x_rank = earlier_same(x_owner_x)
@@ -99,11 +100,8 @@
     up_part = jnp.einsum("snc,src->snr", cot_recv, up_sel, preferred_element_type=jnp.float32)
     prod = jnp.stack([down_part, up_part]).reshape(2, n_mp, -1).transpose(1, 0, 2)
     prod = prod.reshape(out_loc * n_mp, -1)
-    summed = lax.psum_scatter(
-        jnp.concatenate([base_part, prod], axis=1), "mp", scatter_dimension=0, tiled=True
-    )
-    base_t = summed[:, :rows]
-    prod_mine = summed[:, rows:].reshape(-1).astype(jnp.bfloat16)
+    summed = lax.psum_scatter(prod, "mp", scatter_dimension=0, tiled=True)
+    prod_mine = summed.reshape(-1).astype(jnp.bfloat16)
     gathered = lax.all_gather(
         jnp.concatenate([cotangent.reshape(-1), prod_mine]), "mp", axis=0, tiled=False
     )

time: 319 us -> 320 us (level)
    reduce_scatter x1, waiting for transfers between devices: 0.01 us -> 8.47 us  [shards(): lax.psum_scatter(jnp.concatenate([grad_a_col, grad_b_col], axis=1), 'dz',...]
    reduce_scatter x1 -> x2, waiting for transfers between devices: 44 us -> 36.3 us  [the longest x1 36.3 us: shards(): summed = lax.psum_scatter(prod, 'mp', scatter_dimension=0, tiled=True)]
    concatenate x1 -> x0, other arithmetic: 5 us -> none  [shards(): jnp.concatenate([base_part, prod], axis=1)]
    unnamed x22 -> x19, local copies, waits for them, and re-layouts: 11 us -> 9.79 us
  transfers between devices with their start and end apart: 6 -> 7, of which waited for: 3 -> 4; matrix products, arithmetic and copies ran while one was open for 26% -> 35% of each run, Pallas kernels for 0% -> 0%
where the time goes in v8:
time: 320 us; the launch traced here: 319 us
  waiting for transfers between devices  103 us (32%)
  local copies, waits for them, and re-layouts  76.6 us (24%)
  blocking collectives  47.4 us (15%)
  other arithmetic  35.8 us (11%)
  matrix products  31.1 us (10%)
  between operations  14.8 us (5%)
  starting transfers between devices  10.7 us (3%)
    all_to_all x1, waiting for transfers between devices, shards(): lax.all_to_all(back_send, 'dx', split_axis=0, concat_axis=0, tiled=True)  50.9 us
    unnamed x1, blocking collectives  47.4 us
    reduce_scatter x1, waiting for transfers between devices, shards(): summed = lax.psum_scatter(prod, 'mp', scatter_dimension=0, tiled=True)  36.3 us
    unnamed x19, local copies, waits for them, and re-layouts  9.79 us
    gather x2, local copies, waits for them, and re-layouts, shards(): jnp.take(back, position, axis=0).reshape(rows, width_loc + out_loc)  8.92 us
    gather x2, local copies, waits for them, and re-layouts, by_panel(): wide_p = jnp.take(wide, panel_slot.reshape(-1), axis=0)  8.76 us
    reduce_scatter x1, waiting for transfers between devices, shards(): lax.psum_scatter(jnp.concatenate([grad_a_col, grad_b_col], axis=1), 'dz',...  8.47 us
    select_n x3, other arithmetic, by_panel(): wide_p = jnp.take(wide, panel_slot.reshape(-1), axis=0)  8.03 us
  transfers between devices with their start and end apart: 7, of which 4 were waited for; matrix products, arithmetic and copies ran while one was open for 35% of the time, Pallas kernels for 0%

profile of v8, /device:TPU:1, one launch (start us, length us, event | category | flops | bytes accessed | tf_op | source)
XLA Modules:
  0.0 319.0 jit_solution(18310172872853368914)
XLA Ops:
  7.2 2.0 pad_maximum_fusion.3
  9.9 1.4 gather_fusion
  11.2 1.4 gather_fusion.1
  12.9 1.6 gather_fusion.3
  14.6 2.7 gather_fusion.2
  17.5 2.6 broadcast_select_fusion.1
  20.1 2.8 pad_maximum_fusion.1
  22.9 5.1 %all-to-all-start = ((bf16[64,32,1152]{2,1,0:T(8,128)(2,1)}), bf16[64,32,1152]{2,1,0:T(8,128)(2,1)}, u32[]{:S(2)}, u32[]{:S(2)}) async-start(bf16[64,32,1152]{2,1,0:T(8,128)(2,1)} %pad_maximum_fusion.1), calls=%async_computation.1 | async-start | bytes 9437184 | tf_op jit(solution)/shard_map/all_to_all | solution.py:92
  28.0 5.9 %fusion.40 = f32[1024,1024]{1,0:T(8,128)} fusion(bf16[1024,1024]{1,0:T(8,128)(2,1)} %param.11, bf16[1024,1024]{1,0:T(8,128)(2,1)S(1)} %copy-done), kind=kOutput, calls=%fused_computation.145 | convolution fusion | flops 2147483648 | bytes 8388608 | tf_op jit(solution)/shard_map/dot_general | solution.py:52
  35.5 47.4 %all-reduce = s32[128]{0:T(128)S(1)} all-reduce(s32[128]{0:T(128)S(1)} %dynamic-update-slice), channel_id=2, replica_groups=mesh['dz'=8,'dx'=4,'mp'=8] {'dx'}, use_global_device_ids=true, to_apply=%add | all-reduce | flops 128 | bytes 1024
  87.4 1.8 fusion.9
  89.8 4.0 %slice.75 = bf16[24,64,1024]{2,1,0:T(8,128)(2,1)} slice(bf16[24,64,1152]{2,1,0:T(8,128)(2,1)} %all-gather.5.cloned.1.call-done), slice={[0:24], [0:64], [0:1024]} | slice | bytes 6291456 | tf_op jit(solution)/shard_map/slice | solution.py:82
  93.9 7.3 %gather_fusion.4 = bf16[64,64,1024]{2,1,0:T(8,128)(2,1)} fusion(bf16[24,64,1024]{2,1,0:T(8,128)(2,1)} %slice.75, s32[1024]{0:T(1024)S(1)} %pad_clamp_fusion.3), kind=kCustom, calls=%fused_computation.6 | custom fusion | bytes 16777472 | tf_op jit(solution)/shard_map/jit(_take)/gather | solution.py:97
  101.2 7.0 %fusion.2 = f32[64,32,64]{2,1,0:T(8,128)S(1)} fusion(bf16[64,64,1024]{2,1,0:T(8,128)(2,1)} %gather_fusion.4, pred[64]{0:T(512)(128)(4,1)S(1)} %compare_and_fusion.2, bf16[64,32,1152]{2,1,0:T(8,128)(2,1)} %all-to-all-done), kind=kOutput, calls=%fused_computation.20 | convolution fusion | flops 272629760 | bytes 13107264 | tf_op jit(solution)/shard_map/snd,srd->snr/dot_general | solution.py:99
  108.2 1.4 stack.80
  109.7 2.0 maximum_bitcast_fusion
  111.6 1.9 reshape.352
  113.6 36.3 %reduce-scatter.6.cloned.1.call-done = f32[128,256]{1,0:T(8,128)} async-done(((f32[1024,256]{1,0:T(8,128)}), f32[128,256]{1,0:T(8,128)}) %reduce-scatter.6.cloned.1.call-update) | async-done | bytes 131088 | tf_op jit(solution)/shard_map/reduce_scatter | solution.py:103
  153.6 1.1 slice.76
  155.4 5.0 %slice.74 = bf16[64,32,1024]{2,1,0:T(8,128)(2,1)} slice(bf16[64,32,1152]{2,1,0:T(8,128)(2,1)} %all-to-all-done), slice={[0:64], [0:32], [0:1024]} | slice | bytes 8388608 | tf_op jit(solution)/shard_map/slice | solution.py:93
  160.4 8.1 %gather_fusion.7 = bf16[96,32,1024]{2,1,0:T(8,128)(2,1)} fusion(bf16[64,32,1024]{2,1,0:T(8,128)(2,1)} %slice.74, s32[1024]{0:T(1024)S(1)} %pad_clamp_fusion), kind=kCustom, calls=%fused_computation.9 | custom fusion | bytes 12583296 | tf_op jit(solution)/shard_map/jit(_take)/gather | solution.py:124
  168.4 1.3 bitcast_select_fusion.1
  169.7 6.7 %bitcast_select_fusion = bf16[24,128,1024]{2,1,0:T(8,128)(2,1)} fusion(pred[24,128]{1,0:T(8,128)(4,1)S(1)} %broadcast_in_dim.192, bf16[24,128,1024]{2,1,0:T(8,128)(2,1)} %bitcast.93), kind=kLoop, calls=%fused_computation.13 | loop fusion | flops 3145728 | bytes 12585984 | tf_op jit(solution)/shard_map/jit(_take)/select_n | solution.py:124
  176.4 6.3 %all-gather.7.cloned.1.call-done = bf16[1310720]{0:T(1024)(128)(2,1)} async-done(((bf16[163840]{0:T(1024)(128)(2,1)}), bf16[1310720]{0:T(1024)(128)(2,1)}) %all-gather.7.cloned.1.call-update) | async-done | bytes 2621456 | tf_op jit(solution)/shard_map/all_gather | solution.py:105
  182.7 4.4 %reshape.451 = bf16[8,163840]{1,0:T(8,128)(2,1)} reshape(bf16[1310720]{0:T(1024)(128)(2,1)} %all-gather.7.cloned.1.call-done) | data formatting | bytes 5242880 | tf_op jit(solution)/shard_map/all_gather | solution.py:105
  187.2 1.1 slice.78
  188.2 1.1 reshape.353
  190.2 1.6 gather_fusion.9
  191.8 2.6 gather_fusion.10
  194.4 2.8 broadcast_select_fusion.9
  197.2 1.4 copy.83
  198.6 1.4 copy.80
  200.4 3.9 %fusion.12 = f32[24,64,1024]{2,1,0:T(8,128)S(1)} fusion(bf16[24,128,1024]{2,1,0:T(8,128)(2,1)} %bitcast_select_fusion, bf16[24,128,64]{1,2,0:T(8,128)(2,1)S(1)} %copy.80, pred[24,128]{1,0:T(8,128)(4,1)S(1)} %broadcast_in_dim.189), kind=kOutput, calls=%fused_computation.41 | convolution fusion | flops 402849792 | bytes 12979200 | tf_op jit(solution)/shard_map/pnr,pnd->prd/dot_general | solution.py:131
  204.3 3.6 %pad_maximum_fusion = f32[1536,1152]{1,0:T(8,128)} fusion(f32[1536,128]{1,0:T(8,128)S(1)} %bitcast.100, f32[1536,1024]{1,0:T(8,128)S(1)} %bitcast.92), kind=kLoop, calls=%fused_computation.12 | loop fusion | flops 1769472 | bytes 14155776 | tf_op jit(solution)/shard_map/concatenate | solution.py:139
  207.9 1.0 copy-done.2
  209.4 4.9 %fusion.3 = bf16[64,32,1024]{2,1,0:T(8,128)(2,1)S(1)} fusion(bf16[64,32,64]{2,1,0:T(8,128)(2,1)S(1)} %bitcast.97, bf16[64,64,1024]{2,1,0:T(8,128)(2,1)} %gather_fusion.4, pred[64]{0:T(512)(128)(4,1)S(1)} %compare_and_fusion.2), kind=kOutput, calls=%fused_computation.21 | convolution fusion | flops 274726912 | bytes 12845120 | tf_op jit(solution)/shard_map/snr,srd->snd/dot_general | solution.py:115
  214.3 2.7 pad_maximum_fusion.2
  217.0 5.2 %all-to-all-start.1 = ((bf16[64,32,1152]{2,1,0:T(8,128)(2,1)}), bf16[64,32,1152]{2,1,0:T(8,128)(2,1)}, u32[]{:S(2)}, u32[]{:S(2)}) async-start(bf16[64,32,1152]{2,1,0:T(8,128)(2,1)} %pad_maximum_fusion.2), calls=%async_computation.3 | async-start | bytes 9437184 | tf_op jit(solution)/shard_map/all_to_all | solution.py:119
  222.4 3.1 slice_bitcast_fusion
  225.5 50.9 %all-to-all-done.1 = bf16[64,32,1152]{2,1,0:T(8,128)(2,1)} async-done(((bf16[64,32,1152]{2,1,0:T(8,128)(2,1)}), bf16[64,32,1152]{2,1,0:T(8,128)(2,1)}, u32[]{:S(2)}, u32[]{:S(2)}) %all-to-all-start.1) | async-done | bytes 4718624 | tf_op jit(solution)/shard_map/all_to_all | solution.py:119
  276.4 4.6 %gather_fusion.6 = bf16[32,32,1152]{2,1,0:T(8,128)(2,1)} fusion(bf16[64,32,1152]{2,1,0:T(8,128)(2,1)} %all-to-all-done.1, s32[1024]{0:T(1024)S(1)} %pad_clamp_fusion.2), kind=kCustom, calls=%fused_computation.8 | custom fusion | bytes 4718720 | tf_op jit(solution)/shard_map/jit(_take)/gather | solution.py:152
  281.0 4.3 %copy.75 = bf16[1024,1152]{0,1:T(8,128)(2,1)} copy(bf16[1024,1152]{1,0:T(8,128)(2,1)} %bitcast.94) | data formatting | bytes 4718592 | tf_op jit(solution)/shard_map/jit(_take)/gather | solution.py:152
  285.3 3.4 %broadcast_select_fusion.6 = bf16[1024,1152]{0,1:T(8,128)(2,1)} fusion(bf16[1024,1152]{0,1:T(8,128)(2,1)} %copy.75, pred[1024]{0:T(1024)(128)(4,1)S(1)} %broadcast_in_dim.173), kind=kLoop, calls=%fused_computation.22 | loop fusion | flops 1179648 | bytes 4719616 | tf_op jit(solution)/shard_map/jit(_take)/select_n | solution.py:152
  288.7 1.2 fusion.8
  290.7 6.7 %fusion = bf16[1024,1024]{0,1:T(8,128)(2,1)} fusion(bf16[1,8,1024,128]{3,1,2,0:T(8,128)(2,1)} %slice_bitcast_fusion, bf16[1024,1152]{0,1:T(8,128)(2,1)} %broadcast_select_fusion.6, bf16[1024,1024]{1,0:T(8,128)(2,1)} %param.11), kind=kOutput, calls=%fused_computation.17 | convolution fusion | flops 2150629376 | bytes 8388608 | tf_op jit(solution)/shard_map/krc,dkc->rd/dot_general | solution.py:146
  297.4 4.0 %copy.85 = bf16[1024,1024]{1,0:T(8,128)(2,1)} copy(bf16[1024,1024]{0,1:T(8,128)(2,1)} %fusion) | data formatting | bytes 4194304
  301.4 8.5 %reduce-scatter.8.cloned.1.call-done = f32[192,1152]{1,0:T(8,128)} async-done(((f32[1536,1152]{1,0:T(8,128)}), f32[192,1152]{1,0:T(8,128)}) %reduce-scatter.8.cloned.1.call-update) | async-done | bytes 884752 | tf_op jit(solution)/shard_map/reduce_scatter | solution.py:138
  309.8 1.2 convert.4
  (104 shorter events, 15.7 us)
Async XLA Ops:
  7.2 7.4 %copy-start = (bf16[1024,1024]{1,0:T(8,128)(2,1)S(1)}, bf16[1024,1024]{1,0:T(8,128)(2,1)}, u32[]{:S(2)}) copy-start(bf16[1024,1024]{1,0:T(8,128)(2,1)} %param.10) | copy-start | bytes 6291460
  7.2 78.4 %all-gather.5.cloned.1.call-start = ((), (), s32[]{:S(2)}) async-start(), calls=%async_computation.6 | async-start | bytes 3981312 | tf_op jit(solution)/shard_map/all_gather | solution.py:79
  22.9 64.6 %all-to-all-start = ((bf16[64,32,1152]{2,1,0:T(8,128)(2,1)}), bf16[64,32,1152]{2,1,0:T(8,128)(2,1)}, u32[]{:S(2)}, u32[]{:S(2)}) async-start(bf16[64,32,1152]{2,1,0:T(8,128)(2,1)} %pad_maximum_fusion.1), calls=%async_computation.1 | async-start | bytes 9437184 | tf_op jit(solution)/shard_map/all_to_all | solution.py:92
  28.0 121.9 %reduce-scatter.6.cloned.1.call-start = ((), (), s32[]{:S(2)}) async-start(), calls=%async_computation.7 | async-start | bytes 1179648 | tf_op jit(solution)/shard_map/reduce_scatter | solution.py:103
  28.0 6.0 %copy-start.5 = (u32[256]{0:T(256)S(1)}, u32[256]{0:T(256)}, u32[]{:S(2)}) copy-start(u32[256]{0:T(256)} %constant.209) | copy-start | bytes 3076
  108.2 42.6 %copy-start.4 = (bf16[1024,128]{1,0:T(8,128)(2,1)S(1)}, bf16[1024,128]{1,0:T(8,128)(2,1)}, u32[]{:S(2)}) copy-start(bf16[1024,128]{1,0:T(8,128)(2,1)} %param.14) | copy-start | bytes 786436
  113.5 69.2 %all-gather.7.cloned.1.call-start = ((), (), s32[]{:S(2)}) async-start(), calls=%async_computation.9 | async-start | bytes 2949120 | tf_op jit(solution)/shard_map/all_gather | solution.py:105
  151.6 137.0 %reduce-scatter.4.cloned.1.call-start = ((), (), s32[]{:S(2)}) async-start(), calls=%async_computation.5 | async-start | bytes 4718592 | tf_op jit(solution)/shard_map/reduce_scatter | solution.py:56
  152.2 157.6 %reduce-scatter.8.cloned.1.call-start = ((), (), s32[]{:S(2)}) async-start(), calls=%async_computation.8 | async-start | bytes 7962624 | tf_op jit(solution)/shard_map/reduce_scatter | solution.py:138
  190.2 9.8 %copy-start.3 = (bf16[24,128,128]{2,1,0:T(8,128)(2,1)S(1)}, bf16[24,128,128]{2,1,0:T(8,128)(2,1)}, u32[]{:S(2)}) copy-start(bf16[24,128,128]{2,1,0:T(8,128)(2,1)} %bitcast_select_fusion.1) | copy-start | bytes 2359300
  207.9 1.1 copy-start.2
  217.0 59.3 %all-to-all-start.1 = ((bf16[64,32,1152]{2,1,0:T(8,128)(2,1)}), bf16[64,32,1152]{2,1,0:T(8,128)(2,1)}, u32[]{:S(2)}, u32[]{:S(2)}) async-start(bf16[64,32,1152]{2,1,0:T(8,128)(2,1)} %pad_maximum_fusion.2), calls=%async_computation.3 | async-start | bytes 9437184 | tf_op jit(solution)/shard_map/all_to_all | solution.py:119
  290.7 21.8 %copy-start.1 = (bf16[1024,1024]{1,0:T(8,128)(2,1)S(1)}, bf16[1024,1024]{1,0:T(8,128)(2,1)}, u32[]{:S(2)}) copy-start(bf16[1024,1024]{1,0:T(8,128)(2,1)} %param.10) | copy-start | bytes 6291460
Sparse Core Ops, SparseCore 0:
  10.4 52.4 all-gather.4
  113.7 36.1 reduce-scatter.5
  152.3 30.4 all-gather.6
  185.2 37.5 reduce-scatter.3
  225.2 84.5 reduce-scatter.7

commit v9 on v8

--- a/solution.py
+++ b/solution.py
@@ -98,16 +98,8 @@
     up_sel = jnp.take(up_col, panel_at, axis=0)
     down_part = jnp.einsum("snd,srd->snr", tok_recv, down_sel, preferred_element_type=jnp.float32)
     up_part = jnp.einsum("snc,src->snr", cot_recv, up_sel, preferred_element_type=jnp.float32)
-    prod = jnp.stack([down_part, up_part]).reshape(2, n_mp, -1).transpose(1, 0, 2)
-    prod = prod.reshape(out_loc * n_mp, -1)
-    summed = lax.psum_scatter(prod, "mp", scatter_dimension=0, tiled=True)
-    prod_mine = summed.reshape(-1).astype(jnp.bfloat16)
-    gathered = lax.all_gather(
-        jnp.concatenate([cotangent.reshape(-1), prod_mine]), "mp", axis=0, tiled=False
-    )
-    cot_parts = gathered[:, : rows * out_loc].reshape(n_mp, rows, out_loc)
-    both = gathered[:, rows * out_loc:].reshape(n_mp, 2, -1, rank).transpose(1, 0, 2, 3)
-    both = both.reshape(2, capacity, blk, rank)
+    both = lax.psum(jnp.stack([down_part, up_part]), "mp").astype(jnp.bfloat16)
+    cot_parts = lax.all_gather(cotangent, "mp", axis=0, tiled=False)
     down_low = both[0]
     up_grad = both[1]
 

time: 320 us -> 314 us (0.981)
  blocking collectives: 47.4 us -> 108 us
  waiting for transfers between devices: 103 us -> 52.9 us
  local copies, waits for them, and re-layouts: 76.6 us -> 59.8 us
    psum x0 -> x1, blocking collectives: none -> 55.4 us  [shards(): both = lax.psum(jnp.stack([down_part, up_part]), 'mp').astype(jnp.bfloat16)]
    reduce_scatter x1 -> x0, waiting for transfers between devices: 36.3 us -> none  [shards(): summed = lax.psum_scatter(prod, 'mp', scatter_dimension=0, tiled=True)]
    reduce_scatter x1, waiting for transfers between devices: 8.47 us -> 0.01 us  [shards(): lax.psum_scatter(jnp.concatenate([grad_a_col, grad_b_col], axis=1), 'dz',...]
    all_gather x1, waiting for transfers between devices: 6.31 us -> 0.01 us  [shards(): cot_parts = lax.all_gather(cotangent, 'mp', axis=0, tiled=False)]
    unnamed x1, blocking collectives: 47.4 us -> 52.6 us
    all_gather x1 -> x0, local copies, waits for them, and re-layouts: 4.41 us -> none  [shards(): lax.all_gather(jnp.concatenate([cotangent.reshape(-1), prod_mine]), 'mp',...]
    unnamed x19 -> x25, local copies, waits for them, and re-layouts: 9.79 us -> 6.95 us
  transfers between devices with their start and end apart: 7 -> 6, of which waited for: 4 -> 1; matrix products, arithmetic and copies ran while one was open for 35% -> 38% of each run, Pallas kernels for 0% -> 0%
where the time goes in v9:
time: 314 us; the launch traced here: 311 us
  blocking collectives  108 us (34%)
  local copies, waits for them, and re-layouts  59.8 us (19%)
  waiting for transfers between devices  52.9 us (17%)
  other arithmetic  32.7 us (10%)
  matrix products  30.8 us (10%)
  between operations  16.5 us (5%)
  starting transfers between devices  10.3 us (3%)
    psum x1, blocking collectives, shards(): both = lax.psum(jnp.stack([down_part, up_part]), 'mp').astype(jnp.bfloat16)  55.4 us
    unnamed x1, blocking collectives  52.6 us
    all_to_all x1, waiting for transfers between devices, shards(): lax.all_to_all(back_send, 'dx', split_axis=0, concat_axis=0, tiled=True)  52.2 us
    gather x2, local copies, waits for them, and re-layouts, shards(): jnp.take(back, position, axis=0).reshape(rows, width_loc + out_loc)  8.93 us
    gather x2, local copies, waits for them, and re-layouts, by_panel(): wide_p = jnp.take(wide, panel_slot.reshape(-1), axis=0)  8.81 us
    select_n x3, other arithmetic, by_panel(): wide_p = jnp.take(wide, panel_slot.reshape(-1), axis=0)  8.03 us
    gather x1, local copies, waits for them, and re-layouts, shards(): down_sel = jnp.take(down_col, panel_at, axis=0)  7.28 us
    dot_general x1, matrix products, shards(): jnp.einsum('snd,srd->snr', tok_recv, down_sel, preferred_element_type=jnp...  7.03 us
  transfers between devices with their start and end apart: 6, of which 1 were waited for; matrix products, arithmetic and copies ran while one was open for 38% of the time, Pallas kernels for 0%

profile of v9, /device:TPU:1, one launch (start us, length us, event | category | flops | bytes accessed | tf_op | source)
XLA Modules:
  0.0 311.1 jit_solution(7198488466678263234)
XLA Ops:
  8.1 2.0 pad_maximum_fusion.4
  10.1 0.7 pad_clamp_fusion.6
  10.8 1.4 gather_fusion
  12.1 1.4 gather_fusion.1
  13.5 6.0 %fusion.37 = f32[1024,1024]{1,0:T(8,128)} fusion(bf16[1024,1024]{1,0:T(8,128)(2,1)} %param.11, bf16[1024,1024]{1,0:T(8,128)(2,1)S(1)} %copy-done), kind=kOutput, calls=%fused_computation.142 | convolution fusion | flops 2147483648 | bytes 8388608 | tf_op jit(solution)/shard_map/dot_general | solution.py:52
  19.5 0.5 and_select_fusion.1
  20.4 0.7 gather_fusion.3
  21.1 2.7 gather_fusion.2
  24.0 2.6 broadcast_select_fusion.1
  26.6 2.8 pad_maximum_fusion.1
  29.4 5.1 %all-to-all-start = ((bf16[64,32,1152]{2,1,0:T(8,128)(2,1)}), bf16[64,32,1152]{2,1,0:T(8,128)(2,1)}, u32[]{:S(2)}, u32[]{:S(2)}) async-start(bf16[64,32,1152]{2,1,0:T(8,128)(2,1)} %pad_maximum_fusion.1), calls=%async_computation.1 | async-start | bytes 9437184 | tf_op jit(solution)/shard_map/all_to_all | solution.py:92
  34.5 0.7 all-gather.7.cloned.1.call-update
  35.3 0.6 dynamic-slice
  36.8 52.6 %all-reduce = s32[128]{0:T(128)S(1)} all-reduce(s32[128]{0:T(128)S(1)} %dynamic-update-slice), channel_id=2, replica_groups=mesh['dz'=8,'dx'=4,'mp'=8] {'dx'}, use_global_device_ids=true, to_apply=%add | all-reduce | flops 128 | bytes 1024
  93.3 1.1 slice.66
  94.4 0.7 gather_fusion.8
  95.1 5.0 %slice.64 = bf16[64,32,1024]{2,1,0:T(8,128)(2,1)} slice(bf16[64,32,1152]{2,1,0:T(8,128)(2,1)} %all-to-all-done), slice={[0:64], [0:32], [0:1024]} | slice | bytes 8388608 | tf_op jit(solution)/shard_map/slice | solution.py:93
  100.1 8.1 %gather_fusion.7 = bf16[96,32,1024]{2,1,0:T(8,128)(2,1)} fusion(bf16[64,32,1024]{2,1,0:T(8,128)(2,1)} %slice.64, s32[1024]{0:T(1024)S(1)} %pad_clamp_fusion), kind=kCustom, calls=%fused_computation.9 | custom fusion | bytes 12583296 | tf_op jit(solution)/shard_map/jit(_take)/gather | solution.py:116
  108.3 1.3 bitcast_select_fusion.1
  109.6 6.7 %bitcast_select_fusion = bf16[24,128,1024]{2,1,0:T(8,128)(2,1)} fusion(pred[24,128]{1,0:T(8,128)(4,1)S(1)} %broadcast_in_dim.192, bf16[24,128,1024]{2,1,0:T(8,128)(2,1)} %bitcast.89), kind=kLoop, calls=%fused_computation.13 | loop fusion | flops 3145728 | bytes 12585984 | tf_op jit(solution)/shard_map/jit(_take)/select_n | solution.py:116
  116.3 1.0 slice.67
  117.3 0.7 gather_fusion.5
  118.1 4.5 %slice.65 = bf16[24,64,1024]{2,1,0:T(8,128)(2,1)} slice(bf16[24,64,1152]{2,1,0:T(8,128)(2,1)} %all-gather.5.cloned.1.call-done), slice={[0:24], [0:64], [0:1024]} | slice | bytes 6291456 | tf_op jit(solution)/shard_map/slice | solution.py:82
  122.6 7.3 %gather_fusion.4 = bf16[64,64,1024]{2,1,0:T(8,128)(2,1)} fusion(bf16[24,64,1024]{2,1,0:T(8,128)(2,1)} %slice.65, s32[1024]{0:T(1024)S(1)} %pad_clamp_fusion.3), kind=kCustom, calls=%fused_computation.6 | custom fusion | bytes 16777472 | tf_op jit(solution)/shard_map/jit(_take)/gather | solution.py:97
  129.8 7.0 %fusion.6 = f32[1,64,32,64]{3,2,1,0:T(8,128)S(1)} fusion(bf16[64,64,1024]{2,1,0:T(8,128)(2,1)} %gather_fusion.4, pred[64]{0:T(512)(128)(4,1)S(1)} %compare_and_fusion.2, bf16[64,32,1152]{2,1,0:T(8,128)(2,1)} %all-to-all-done), kind=kOutput, calls=%fused_computation.26 | convolution fusion | flops 272629760 | bytes 13107264 | tf_op jit(solution)/shard_map/snd,srd->snr/dot_general | solution.py:99
  136.9 1.8 convolution_bitcast_fusion
  138.9 55.4 %all-reduce.2 = bf16[2,64,32,64]{3,2,1,0:T(8,128)(2,1)S(1)} all-reduce(f32[2,64,32,64]{3,2,1,0:T(8,128)S(1)} %pad_maximum_fusion.3), channel_id=1, replica_groups=mesh['dz'=8,'dx'=4,'mp'=8] {'mp'}, use_global_device_ids=true, to_apply=%region_20.21 | all-reduce | flops 262144 | bytes 1572864 | tf_op jit(solution)/shard_map/psum | solution.py:101
  194.4 1.6 gather_fusion.9
  196.0 1.6 gather_fusion.10
  197.6 2.5 broadcast_select_fusion.11
  200.1 1.4 copy.77
  202.2 3.8 %fusion.10 = f32[24,64,1024]{2,1,0:T(8,128)S(1)} fusion(bf16[24,128,1024]{2,1,0:T(8,128)(2,1)} %bitcast_select_fusion, bf16[24,128,64]{1,2,0:T(8,128)(2,1)S(1)} %copy.74, pred[24,128]{1,0:T(8,128)(4,1)S(1)} %broadcast_in_dim.189), kind=kOutput, calls=%fused_computation.41 | convolution fusion | flops 402849792 | bytes 12979200 | tf_op jit(solution)/shard_map/pnr,pnd->prd/dot_general | solution.py:123
  205.9 3.6 %pad_maximum_fusion = f32[1536,1152]{1,0:T(8,128)} fusion(f32[1536,128]{1,0:T(8,128)S(1)} %bitcast.91, f32[1536,1024]{1,0:T(8,128)S(1)} %bitcast.88), kind=kLoop, calls=%fused_computation.12 | loop fusion | flops 1769472 | bytes 14155776 | tf_op jit(solution)/shard_map/concatenate | solution.py:131
  209.5 1.2 copy-done.3
  211.2 4.7 %fusion.3 = bf16[64,32,1024]{2,1,0:T(8,128)(2,1)S(1)} fusion(bf16[64,64,1024]{2,1,0:T(8,128)(2,1)} %gather_fusion.4, pred[64]{0:T(512)(128)(4,1)S(1)} %copy-done.8, bf16[2,64,32,64]{3,2,1,0:T(8,128)(2,1)S(1)} %all-reduce.2), kind=kOutput, calls=%fused_computation.21 | convolution fusion | flops 274726912 | bytes 13107712 | tf_op jit(solution)/shard_map/snr,srd->snd/dot_general | solution.py:107
  215.9 2.7 pad_maximum_fusion.2
  218.6 5.1 %all-to-all-start.1 = ((bf16[64,32,1152]{2,1,0:T(8,128)(2,1)}), bf16[64,32,1152]{2,1,0:T(8,128)(2,1)}, u32[]{:S(2)}, u32[]{:S(2)}) async-start(bf16[64,32,1152]{2,1,0:T(8,128)(2,1)} %pad_maximum_fusion.2), calls=%async_computation.2 | async-start | bytes 9437184 | tf_op jit(solution)/shard_map/all_to_all | solution.py:111
  223.9 52.2 %all-to-all-done.1 = bf16[64,32,1152]{2,1,0:T(8,128)(2,1)} async-done(((bf16[64,32,1152]{2,1,0:T(8,128)(2,1)}), bf16[64,32,1152]{2,1,0:T(8,128)(2,1)}, u32[]{:S(2)}, u32[]{:S(2)}) %all-to-all-start.1) | async-done | bytes 4718624 | tf_op jit(solution)/shard_map/all_to_all | solution.py:111
  276.1 4.6 %gather_fusion.6 = bf16[32,32,1152]{2,1,0:T(8,128)(2,1)} fusion(bf16[64,32,1152]{2,1,0:T(8,128)(2,1)} %all-to-all-done.1, s32[1024]{0:T(1024)S(1)} %pad_clamp_fusion.2), kind=kCustom, calls=%fused_computation.8 | custom fusion | bytes 4718720 | tf_op jit(solution)/shard_map/jit(_take)/gather | solution.py:144
  280.7 4.3 %copy.69 = bf16[1024,1152]{0,1:T(8,128)(2,1)} copy(bf16[1024,1152]{1,0:T(8,128)(2,1)} %bitcast.90) | data formatting | bytes 4718592 | tf_op jit(solution)/shard_map/jit(_take)/gather | solution.py:144
  285.0 3.4 %broadcast_select_fusion.6 = bf16[1024,1152]{0,1:T(8,128)(2,1)} fusion(bf16[1024,1152]{0,1:T(8,128)(2,1)} %copy.69, pred[1024]{0:T(1024)(128)(4,1)S(1)} %broadcast_in_dim.173), kind=kLoop, calls=%fused_computation.22 | loop fusion | flops 1179648 | bytes 4719616 | tf_op jit(solution)/shard_map/jit(_take)/select_n | solution.py:144
  288.4 1.2 fusion.7
  289.5 0.8 copy.78
  290.4 6.7 %fusion = bf16[1024,1024]{0,1:T(8,128)(2,1)} fusion(bf16[8,1024,128]{2,1,0:T(8,128)(2,1)} %bitcast.114, bf16[1024,1152]{0,1:T(8,128)(2,1)} %broadcast_select_fusion.6, bf16[1024,1024]{1,0:T(8,128)(2,1)} %param.11), kind=kOutput, calls=%fused_computation.17 | convolution fusion | flops 2150629376 | bytes 8388608 | tf_op jit(solution)/shard_map/krc,dkc->rd/dot_general | solution.py:138
  297.1 3.9 %copy.79 = bf16[1024,1024]{1,0:T(8,128)(2,1)} copy(bf16[1024,1024]{0,1:T(8,128)(2,1)} %fusion) | data formatting | bytes 4194304
  301.0 1.2 convert.4
  302.2 0.8 slice.72
  303.0 0.6 slice.73
  (100 shorter events, 6.4 us)
Async XLA Ops:
  8.0 5.5 %copy-start = (bf16[1024,1024]{1,0:T(8,128)(2,1)S(1)}, bf16[1024,1024]{1,0:T(8,128)(2,1)}, u32[]{:S(2)}) copy-start(bf16[1024,1024]{1,0:T(8,128)(2,1)} %param.10) | copy-start | bytes 6291460
  8.0 108.3 %all-gather.5.cloned.1.call-start = ((), (), s32[]{:S(2)}) async-start(), calls=%async_computation.5 | async-start | bytes 3981312 | tf_op jit(solution)/shard_map/all_gather | solution.py:79
  10.0 278.3 %reduce-scatter.3.cloned.1.call-start = ((), (), s32[]{:S(2)}) async-start(), calls=%async_computation.4 | async-start | bytes 4718592 | tf_op jit(solution)/shard_map/reduce_scatter | solution.py:56
  19.5 1.0 copy-start.5
  29.4 5.9 %copy-start.9 = (u32[256]{0:T(256)S(1)}, u32[256]{0:T(256)}, u32[]{:S(2)}) copy-start(u32[256]{0:T(256)} %constant.209) | copy-start | bytes 3076
  29.4 63.9 %all-to-all-start = ((bf16[64,32,1152]{2,1,0:T(8,128)(2,1)}), bf16[64,32,1152]{2,1,0:T(8,128)(2,1)}, u32[]{:S(2)}, u32[]{:S(2)}) async-start(bf16[64,32,1152]{2,1,0:T(8,128)(2,1)} %pad_maximum_fusion.1), calls=%async_computation.1 | async-start | bytes 9437184 | tf_op jit(solution)/shard_map/all_to_all | solution.py:92
  34.5 255.9 %all-gather.7.cloned.1.call-start = ((), (), s32[]{:S(2)}) async-start(), calls=%async_computation.7 | async-start | bytes 2359296 | tf_op jit(solution)/shard_map/all_gather | solution.py:102
  35.2 265.8 %reduce-scatter.5.cloned.1.call-start = ((), (), s32[]{:S(2)}) async-start(), calls=%async_computation.6 | async-start | bytes 7962624 | tf_op jit(solution)/shard_map/reduce_scatter | solution.py:130
  93.3 43.6 %copy-start.7 = (pred[64]{0:T(512)(128)(4,1)}, pred[64]{0:T(512)(128)(4,1)S(1)}, u32[]{:S(2)}) copy-start(pred[64]{0:T(512)(128)(4,1)S(1)} %compare_and_fusion.2) | copy-start | bytes 196
  118.1 18.8 %copy-start.2 = (bf16[64,64,128]{2,1,0:T(8,128)(2,1)}, bf16[64,64,128]{2,1,0:T(8,128)(2,1)S(1)}, u32[]{:S(2)}) copy-start(bf16[64,64,128]{2,1,0:T(8,128)(2,1)S(1)} %gather_fusion.5) | copy-start | bytes 3145732
  194.4 7.4 %copy-start.4 = (bf16[24,128,128]{2,1,0:T(8,128)(2,1)S(1)}, bf16[24,128,128]{2,1,0:T(8,128)(2,1)}, u32[]{:S(2)}) copy-start(bf16[24,128,128]{2,1,0:T(8,128)(2,1)} %bitcast_select_fusion.1) | copy-start | bytes 2359300
  209.5 1.2 copy-start.3
  209.5 1.2 copy-start.8
  218.6 5.2 %copy-start.6 = (s32[32]{0:T(128)S(1)}, s32[32]{0:T(128)}, u32[]{:S(2)}) copy-start(s32[32]{0:T(128)} %get-tuple-element.44) | copy-start | bytes 388
  218.6 57.4 %all-to-all-start.1 = ((bf16[64,32,1152]{2,1,0:T(8,128)(2,1)}), bf16[64,32,1152]{2,1,0:T(8,128)(2,1)}, u32[]{:S(2)}, u32[]{:S(2)}) async-start(bf16[64,32,1152]{2,1,0:T(8,128)(2,1)} %pad_maximum_fusion.2), calls=%async_computation.2 | async-start | bytes 9437184 | tf_op jit(solution)/shard_map/all_to_all | solution.py:111
  290.4 13.3 %copy-start.1 = (bf16[1024,1024]{1,0:T(8,128)(2,1)S(1)}, bf16[1024,1024]{1,0:T(8,128)(2,1)}, u32[]{:S(2)}) copy-start(bf16[1024,1024]{1,0:T(8,128)(2,1)} %param.10) | copy-start | bytes 6291460
Sparse Core Ops, SparseCore 0:
  11.2 52.4 all-gather.4
  65.6 26.7 all-gather.6
Sparse Core Ops, SparseCore 1:
  19.6 42.4 reduce-scatter.2
  209.6 83.4 reduce-scatter.4

commit v10 on v9

--- a/solution.py
+++ b/solution.py
@@ -41,7 +41,7 @@
     tenant = jnp.take(device_tenant_list, block_list_entry, mode="clip")
     location = jnp.take(tenant_location_map, tenant, mode="clip")
     owner_x = (location // stored) % n_x
-    position = owner_x * per_x + earlier_same(owner_x)
+    position = jnp.clip(owner_x * per_x + earlier_same(owner_x), 0, capacity - 1)
 
     slot_ids = jnp.arange(capacity, dtype=jnp.int32)
     block_ids = jnp.arange(blocks, dtype=jnp.int32)
@@ -87,15 +87,15 @@
     token_blocks = tokens.reshape(blocks, blk, width_loc)
     cot_blocks = cotangent.reshape(blocks, blk, out_loc)
     send = jnp.concatenate(
-        [jnp.take(token_blocks, source, axis=0), jnp.take(cot_blocks, source, axis=0)], axis=2
+        [jnp.take(token_blocks, source, axis=0, mode="clip"), jnp.take(cot_blocks, source, axis=0, mode="clip")], axis=2
     )
     recv = lax.all_to_all(send, "dx", split_axis=0, concat_axis=0, tiled=True)
     tok_recv = recv[:, :, :width_loc]
     cot_recv = recv[:, :, width_loc:]
 
     panel_at = jnp.clip(slot_panel, 0, column - 1)
-    down_sel = jnp.take(down_col, panel_at, axis=0)
-    up_sel = jnp.take(up_col, panel_at, axis=0)
+    down_sel = jnp.take(down_col, panel_at, axis=0, mode="clip")
+    up_sel = jnp.take(up_col, panel_at, axis=0, mode="clip")
     down_part = jnp.einsum("snd,srd->snr", tok_recv, down_sel, preferred_element_type=jnp.float32)
     up_part = jnp.einsum("snc,src->snr", cot_recv, up_sel, preferred_element_type=jnp.float32)
     both = lax.psum(jnp.stack([down_part, up_part]), "mp").astype(jnp.bfloat16)
@@ -111,9 +111,9 @@
     back = lax.all_to_all(back_send, "dx", split_axis=0, concat_axis=0, tiled=True)
 
     def by_panel(small, wide):
-        small_p = jnp.take(small, panel_slot.reshape(-1), axis=0).reshape(column, n_x, blk, rank)
+        small_p = jnp.take(small, panel_slot.reshape(-1), axis=0, mode="clip").reshape(column, n_x, blk, rank)
         small_p = jnp.where(panel_used[:, :, None, None], small_p, jnp.zeros_like(small_p))
-        wide_p = jnp.take(wide, panel_slot.reshape(-1), axis=0)
+        wide_p = jnp.take(wide, panel_slot.reshape(-1), axis=0, mode="clip")
         return (
             small_p.reshape(column, n_x * blk, rank),
             wide_p.reshape(column, n_x * blk, wide.shape[2]),
@@ -141,7 +141,7 @@
         value_weight.reshape(width_loc, n_mp, out_loc),
         preferred_element_type=jnp.float32,
     )
-    mine_back = jnp.take(back, position, axis=0).reshape(rows, width_loc + out_loc)
+    mine_back = jnp.take(back, position, axis=0, mode="clip").reshape(rows, width_loc + out_loc)
     values = (base_t.T + mine_back[:, width_loc:].astype(jnp.float32)).astype(jnp.bfloat16)
     token_gradient = (base_bwd + mine_back[:, :width_loc].astype(jnp.float32)).astype(jnp.bfloat16)
     return (values, token_gradient, grad_a, grad_b)

time: 314 us -> 298 us (0.949)
  other arithmetic: 32.7 us -> 19 us
  local copies, waits for them, and re-layouts: 59.8 us -> 53.8 us
  waiting for transfers between devices: 52.9 us -> 57.2 us
    select_n x11 -> x0, other arithmetic: 16.7 us -> none  [the longest x3 8.03 us: by_panel(): wide_p = jnp.take(wide, panel_slot.reshape(-1), axis=0)]
    unnamed x25 -> x15, local copies, waits for them, and re-layouts: 6.95 us -> 2.45 us
    reduce_scatter x1, waiting for transfers between devices: 0.01 us -> 3.71 us  [shards(): lax.psum_scatter(jnp.concatenate([grad_a_col, grad_b_col], axis=1), 'dz',...]
    gather x10 -> x9, local copies, waits for them, and re-layouts: 32.3 us -> 29 us  [the longest x2 9.73 us: by_panel(): wide_p = jnp.take(wide, panel_slot.reshape(-1), axis=0, mode='clip')]
  transfers between devices with their start and end apart: 6 -> 6, of which waited for: 1 -> 2; matrix products, arithmetic and copies ran while one was open for 38% -> 33% of each run, Pallas kernels for 0% -> 0%
where the time goes in v10:
time: 298 us; the launch traced here: 297 us
  blocking collectives  109 us (37%)
  waiting for transfers between devices  57.2 us (19%)
  local copies, waits for them, and re-layouts  53.8 us (18%)
  matrix products  31.4 us (11%)
  other arithmetic  19 us (6%)
  between operations  16.4 us (6%)
  starting transfers between devices  10.2 us (3%)
    psum x1, blocking collectives, shards(): both = lax.psum(jnp.stack([down_part, up_part]), 'mp').astype(jnp.bfloat16)  55.9 us
    unnamed x1, blocking collectives  52.8 us
    all_to_all x1, waiting for transfers between devices, shards(): lax.all_to_all(back_send, 'dx', split_axis=0, concat_axis=0, tiled=True)  52.7 us
    gather x2, local copies, waits for them, and re-layouts, by_panel(): wide_p = jnp.take(wide, panel_slot.reshape(-1), axis=0, mode='clip')  9.73 us
    gather x1, local copies, waits for them, and re-layouts, shards(): down_sel = jnp.take(down_col, panel_at, axis=0, mode='clip')  7.24 us
    dot_general x1, matrix products, shards(): jnp.einsum('snd,srd->snr', tok_recv, down_sel, preferred_element_type=jnp...  6.97 us
    dot_general x1, matrix products, shards(): jnp.einsum('krc,dkc->rd', cot_parts, value_weight.reshape(width_loc, n_mp...  6.69 us
    dot_general x1, matrix products, shards(): lax.dot_general(value_weight, tokens, (((0,), (1,)), ((), ())), preferred...  5.98 us
  transfers between devices with their start and end apart: 6, of which 2 were waited for; matrix products, arithmetic and copies ran while one was open for 33% of the time, Pallas kernels for 0%

profile of v10, /device:TPU:1, one launch (start us, length us, event | category | flops | bytes accessed | tf_op | source)
XLA Modules:
  0.0 296.6 jit_solution(17786913563109329040)
XLA Ops:
  8.1 2.0 pad_maximum_fusion.4
  10.1 0.7 pad_clamp_fusion.5
  10.8 1.4 gather_fusion
  12.1 1.4 gather_fusion.1
  13.5 6.0 %fusion.25 = f32[1024,1024]{1,0:T(8,128)} fusion(bf16[1024,1024]{1,0:T(8,128)(2,1)} %param.9, bf16[1024,1024]{1,0:T(8,128)(2,1)S(1)} %copy-done), kind=kOutput, calls=%fused_computation.109 | convolution fusion | flops 2147483648 | bytes 8388608 | tf_op jit(solution)/shard_map/dot_general | solution.py:52
  19.8 0.6 copy-done.3
  20.4 0.7 gather_fusion.3
  21.1 2.8 gather_fusion.2
  23.9 4.9 %pad_maximum_fusion.1 = bf16[64,32,1152]{2,1,0:T(8,128)(2,1)} fusion(bf16[64,32,128]{2,1,0:T(8,128)(2,1)S(1)} %gather_fusion.3, bf16[64,32,1024]{2,1,0:T(8,128)(2,1)} %gather_fusion.2), kind=kLoop, calls=%fused_computation.12 | loop fusion | flops 9437184 | bytes 9437184 | tf_op jit(solution)/shard_map/concatenate | solution.py:89
  28.8 5.1 %all-to-all-start = ((bf16[64,32,1152]{2,1,0:T(8,128)(2,1)}), bf16[64,32,1152]{2,1,0:T(8,128)(2,1)}, u32[]{:S(2)}, u32[]{:S(2)}) async-start(bf16[64,32,1152]{2,1,0:T(8,128)(2,1)} %pad_maximum_fusion.1), calls=%async_computation.1 | async-start | bytes 9437184 | tf_op jit(solution)/shard_map/all_to_all | solution.py:92
  34.0 0.7 all-gather.7.cloned.1.call-update
  34.8 0.6 dynamic-slice
  36.0 0.2 dynamic-update-slice
  36.2 52.8 %all-reduce = s32[128]{0:T(128)S(1)} all-reduce(s32[128]{0:T(128)S(1)} %dynamic-update-slice), channel_id=2, replica_groups=mesh['dz'=8,'dx'=4,'mp'=8] {'dx'}, use_global_device_ids=true, to_apply=%add | all-reduce | flops 128 | bytes 1024
  89.6 0.4 select_reduce_fusion.2
  92.4 1.1 slice.66
  93.5 1.6 gather_fusion.10
  95.0 4.9 %slice.64 = bf16[64,32,1024]{2,1,0:T(8,128)(2,1)} slice(bf16[64,32,1152]{2,1,0:T(8,128)(2,1)} %all-to-all-done), slice={[0:64], [0:32], [0:1024]} | slice | bytes 8388608 | tf_op jit(solution)/shard_map/slice | solution.py:93
  100.0 8.1 %gather_fusion.8 = bf16[96,32,1024]{2,1,0:T(8,128)(2,1)} fusion(bf16[64,32,1024]{2,1,0:T(8,128)(2,1)} %slice.64, s32[1024]{0:T(1024)S(1)} %pad_clamp_fusion), kind=kCustom, calls=%fused_computation.8 | custom fusion | bytes 12583296 | tf_op jit(solution)/shard_map/jit(_take)/gather | solution.py:116
  108.1 1.0 slice.67
  109.1 0.7 gather_fusion.5
  109.9 4.1 %slice.65 = bf16[24,64,1024]{2,1,0:T(8,128)(2,1)} slice(bf16[24,64,1152]{2,1,0:T(8,128)(2,1)} %all-gather.5.cloned.1.call-done), slice={[0:24], [0:64], [0:1024]} | slice | bytes 6291456 | tf_op jit(solution)/shard_map/slice | solution.py:82
  114.0 7.2 %gather_fusion.4 = bf16[64,64,1024]{2,1,0:T(8,128)(2,1)} fusion(bf16[24,64,1024]{2,1,0:T(8,128)(2,1)} %slice.65, s32[1024]{0:T(1024)S(1)} %pad_clamp_fusion.2), kind=kCustom, calls=%fused_computation.4 | custom fusion | bytes 16777472 | tf_op jit(solution)/shard_map/jit(_take)/gather | solution.py:97
  121.2 1.7 convolution_bitcast_fusion.1
  122.9 7.0 %convolution_bitcast_fusion = f32[1,64,32,64]{3,2,1,0:T(8,128)S(1)} fusion(bf16[64,64,1024]{2,1,0:T(8,128)(2,1)} %gather_fusion.4, bf16[64,32,1152]{2,1,0:T(8,128)(2,1)} %all-to-all-done), kind=kOutput, calls=%fused_computation.20 | convolution fusion | flops 268435456 | bytes 13107200 | tf_op jit(solution)/shard_map/snd,srd->snr/dot_general | solution.py:99
  129.9 1.6 pad_maximum_fusion.3
  131.5 55.9 %all-reduce.2 = bf16[2,64,32,64]{3,2,1,0:T(8,128)(2,1)S(1)} all-reduce(f32[2,64,32,64]{3,2,1,0:T(8,128)} %pad_maximum_fusion.3), channel_id=1, replica_groups=mesh['dz'=8,'dx'=4,'mp'=8] {'mp'}, use_global_device_ids=true, to_apply=%region_20.21 | all-reduce | flops 262144 | bytes 1572864 | tf_op jit(solution)/shard_map/psum | solution.py:101
  187.5 1.6 gather_fusion.9
  189.0 2.2 copy.68
  191.2 1.6 gather_fusion.7
  192.8 1.4 copy.67
  194.2 1.3 fusion.4
  195.6 3.8 %fusion.6 = f32[24,64,1024]{2,1,0:T(8,128)S(1)} fusion(bf16[24,128,1024]{2,1,0:T(8,128)(2,1)} %bitcast.81, bf16[24,128,64]{1,2,0:T(8,128)(2,1)S(1)} %copy.67, pred[24,128]{1,0:T(8,128)(4,1)S(1)} %broadcast_in_dim.110), kind=kOutput, calls=%fused_computation.30 | convolution fusion | flops 402849792 | bytes 12979200 | tf_op jit(solution)/shard_map/pnr,pnd->prd/dot_general | solution.py:123
  199.3 3.6 %pad_maximum_fusion = f32[1536,1152]{1,0:T(8,128)} fusion(f32[1536,128]{1,0:T(8,128)S(1)} %bitcast.82, f32[1536,1024]{1,0:T(8,128)S(1)} %bitcast.80), kind=kLoop, calls=%fused_computation.11 | loop fusion | flops 1769472 | bytes 14155776 | tf_op jit(solution)/shard_map/concatenate | solution.py:131
  202.9 0.4 convolution_convert_fusion.1
  203.3 4.6 %convolution_convert_fusion = bf16[64,32,1024]{2,1,0:T(8,128)(2,1)S(1)} fusion(bf16[64,64,1024]{2,1,0:T(8,128)(2,1)} %gather_fusion.4, bf16[2,64,32,64]{3,2,1,0:T(8,128)(2,1)S(1)} %all-reduce.2), kind=kOutput, calls=%fused_computation.16 | convolution fusion | flops 270532608 | bytes 13107200 | tf_op jit(solution)/shard_map/snr,srd->snd/dot_general | solution.py:107
  208.0 2.7 pad_maximum_fusion.2
  210.7 4.9 %all-to-all-start.1 = ((bf16[64,32,1152]{2,1,0:T(8,128)(2,1)}), bf16[64,32,1152]{2,1,0:T(8,128)(2,1)}, u32[]{:S(2)}, u32[]{:S(2)}) async-start(bf16[64,32,1152]{2,1,0:T(8,128)(2,1)} %pad_maximum_fusion.2), calls=%async_computation.2 | async-start | bytes 9437184 | tf_op jit(solution)/shard_map/all_to_all | solution.py:111
  215.7 52.7 %all-to-all-done.1 = bf16[64,32,1152]{2,1,0:T(8,128)(2,1)} async-done(((bf16[64,32,1152]{2,1,0:T(8,128)(2,1)}), bf16[64,32,1152]{2,1,0:T(8,128)(2,1)}, u32[]{:S(2)}, u32[]{:S(2)}) %all-to-all-start.1) | async-done | bytes 4718624 | tf_op jit(solution)/shard_map/all_to_all | solution.py:111
  268.4 4.6 %gather_fusion.6 = bf16[32,32,1152]{2,1,0:T(8,128)(2,1)} fusion(bf16[64,32,1152]{2,1,0:T(8,128)(2,1)} %all-to-all-done.1, s32[1024]{0:T(1024)S(1)} %pad_clamp_fusion.1), kind=kCustom, calls=%fused_computation.6 | custom fusion | bytes 4718720 | tf_op jit(solution)/shard_map/jit(_take)/gather | solution.py:144
  273.0 1.0 slice.70
  274.2 1.1 fusion.3
  275.3 0.8 copy.69
  276.1 6.7 %fusion = bf16[1024,1024]{1,0:T(8,128)(2,1)} fusion(bf16[8,1024,128]{2,1,0:T(8,128)(2,1)} %bitcast.107, bf16[1024,1152]{1,0:T(8,128)(2,1)} %bitcast.87, bf16[1024,1024]{1,0:T(8,128)(2,1)} %param.9), kind=kOutput, calls=%fused_computation.15 | convolution fusion | flops 2150629376 | bytes 8388608 | tf_op jit(solution)/shard_map/krc,dkc->rd/dot_general | solution.py:138
  282.8 3.7 %reduce-scatter.5.cloned.1.call-done = f32[192,1152]{1,0:T(8,128)} async-done(((f32[1536,1152]{1,0:T(8,128)}), f32[192,1152]{1,0:T(8,128)}) %reduce-scatter.5.cloned.1.call-update) | async-done | bytes 884752 | tf_op jit(solution)/shard_map/reduce_scatter | solution.py:130
  286.6 1.2 convert.4
  287.8 0.8 slice.72
  288.6 0.6 slice.73
  (69 shorter events, 3.7 us)
Async XLA Ops:
  8.0 5.5 %copy-start = (bf16[1024,1024]{1,0:T(8,128)(2,1)S(1)}, bf16[1024,1024]{1,0:T(8,128)(2,1)}, u32[]{:S(2)}) copy-start(bf16[1024,1024]{1,0:T(8,128)(2,1)} %param.8) | copy-start | bytes 6291460
  8.0 100.1 %all-gather.5.cloned.1.call-start = ((), (), s32[]{:S(2)}) async-start(), calls=%async_computation.5 | async-start | bytes 3981312 | tf_op jit(solution)/shard_map/all_gather | solution.py:79
  10.0 264.1 %reduce-scatter.3.cloned.1.call-start = ((), (), s32[]{:S(2)}) async-start(), calls=%async_computation.4 | async-start | bytes 4718592 | tf_op jit(solution)/shard_map/reduce_scatter | solution.py:56
  19.5 0.9 copy-start.3
  28.8 5.9 %copy-start.4 = (u32[256]{0:T(256)S(1)}, u32[256]{0:T(256)}, u32[]{:S(2)}) copy-start(u32[256]{0:T(256)} %constant.108) | copy-start | bytes 3076
  28.8 63.5 %all-to-all-start = ((bf16[64,32,1152]{2,1,0:T(8,128)(2,1)}), bf16[64,32,1152]{2,1,0:T(8,128)(2,1)}, u32[]{:S(2)}, u32[]{:S(2)}) async-start(bf16[64,32,1152]{2,1,0:T(8,128)(2,1)} %pad_maximum_fusion.1), calls=%async_computation.1 | async-start | bytes 9437184 | tf_op jit(solution)/shard_map/all_to_all | solution.py:92
  33.9 242.2 %all-gather.7.cloned.1.call-start = ((), (), s32[]{:S(2)}) async-start(), calls=%async_computation.7 | async-start | bytes 2359296 | tf_op jit(solution)/shard_map/all_gather | solution.py:102
  34.7 251.9 %reduce-scatter.5.cloned.1.call-start = ((), (), s32[]{:S(2)}) async-start(), calls=%async_computation.6 | async-start | bytes 7962624 | tf_op jit(solution)/shard_map/reduce_scatter | solution.py:130
  189.0 5.2 %copy-start.2 = (bf16[96,32,128]{2,1,0:T(8,128)(2,1)S(1)}, bf16[96,32,128]{2,1,0:T(8,128)(2,1)}, u32[]{:S(2)}) copy-start(bf16[96,32,128]{2,1,0:T(8,128)(2,1)} %gather_fusion.10) | copy-start | bytes 2359300
  210.7 57.7 %all-to-all-start.1 = ((bf16[64,32,1152]{2,1,0:T(8,128)(2,1)}), bf16[64,32,1152]{2,1,0:T(8,128)(2,1)}, u32[]{:S(2)}, u32[]{:S(2)}) async-start(bf16[64,32,1152]{2,1,0:T(8,128)(2,1)} %pad_maximum_fusion.2), calls=%async_computation.2 | async-start | bytes 9437184 | tf_op jit(solution)/shard_map/all_to_all | solution.py:111
  276.1 13.0 %copy-start.1 = (bf16[1024,1024]{1,0:T(8,128)(2,1)S(1)}, bf16[1024,1024]{1,0:T(8,128)(2,1)}, u32[]{:S(2)}) copy-start(bf16[1024,1024]{1,0:T(8,128)(2,1)} %param.8) | copy-start | bytes 6291460
Sparse Core Ops, SparseCore 0:
  11.2 52.4 all-gather.4
  65.6 26.7 all-gather.6
Sparse Core Ops, SparseCore 1:
  19.6 42.3 reduce-scatter.2
  203.0 83.5 reduce-scatter.4

commit v11 on v10

--- a/solution.py
+++ b/solution.py
@@ -110,25 +110,20 @@
     )
     back = lax.all_to_all(back_send, "dx", split_axis=0, concat_axis=0, tiled=True)
 
-    def by_panel(small, wide):
+    def by_panel(small):
         small_p = jnp.take(small, panel_slot.reshape(-1), axis=0, mode="clip").reshape(column, n_x, blk, rank)
         small_p = jnp.where(panel_used[:, :, None, None], small_p, jnp.zeros_like(small_p))
-        wide_p = jnp.take(wide, panel_slot.reshape(-1), axis=0, mode="clip")
-        return (
-            small_p.reshape(column, n_x * blk, rank),
-            wide_p.reshape(column, n_x * blk, wide.shape[2]),
-        )
+        return small_p.reshape(column, n_x * blk, rank)
 
-    up_p, tok_p = by_panel(up_grad, tok_recv)
-    grad_a_col = jnp.einsum(
-        "pnr,pnd->prd", up_p, tok_p, preferred_element_type=jnp.float32
-    ).reshape(column * rank, width_loc)
-    low_p, cot_p = by_panel(down_low, cot_recv)
-    grad_b_col = jnp.einsum(
-        "pnr,pnc->prc", low_p, cot_p, preferred_element_type=jnp.float32
-    ).reshape(column * rank, out_loc)
+    rows_p = jnp.take(recv, panel_slot.reshape(-1), axis=0, mode="clip").reshape(
+        column, n_x * blk, width_loc + out_loc
+    )
+    grad_up = jnp.einsum("pnr,pnd->prd", by_panel(up_grad), rows_p, preferred_element_type=jnp.float32)
+    grad_low = jnp.einsum("pnr,pnd->prd", by_panel(down_low), rows_p, preferred_element_type=jnp.float32)
+    feature = jnp.arange(width_loc + out_loc, dtype=jnp.int32)[None, None, :]
+    grads_col = jnp.where(feature < width_loc, grad_up, grad_low)
     grads = lax.psum_scatter(
-        jnp.concatenate([grad_a_col, grad_b_col], axis=1), "dz", scatter_dimension=0, tiled=True
+        grads_col.reshape(column * rank, width_loc + out_loc), "dz", scatter_dimension=0, tiled=True
     )
     grad_a = grads[:, :width_loc]
     grad_b = grads[:, width_loc:]

time: 298 us -> 292 us (0.980)
  local copies, waits for them, and re-layouts: 53.8 us -> 44.8 us
  matrix products: 31.4 us -> 38.2 us
  other arithmetic: 19 us -> 15.5 us
    dot_general x2, matrix products: 5.1 us -> 11.9 us  [the longest x1 7.59 us: shards(): jnp.einsum('pnr,pnd->prd', by_panel(down_low), rows_p, preferred_element_...]
    slice x2 -> x0, local copies, waits for them, and re-layouts: 6 us -> none  [the longest x1 4.92 us: shards(): tok_recv = recv[:, :, :width_loc]]
    concatenate x1 -> x0, other arithmetic: 3.56 us -> none  [shards(): jnp.concatenate([grad_a_col, grad_b_col], axis=1)]
    gather x2 -> x1, local copies, waits for them, and re-layouts: 9.73 us -> 8.76 us  [shards(): jnp.take(recv, panel_slot.reshape(-1), axis=0, mode='clip')]
  transfers between devices with their start and end apart: 6 -> 6, of which waited for: 2 -> 2; matrix products, arithmetic and copies ran while one was open for 33% -> 32% of each run, Pallas kernels for 0% -> 0%
where the time goes in v11:
time: 292 us; the launch traced here: 291 us
  blocking collectives  109 us (37%)
  waiting for transfers between devices  57 us (20%)
  local copies, waits for them, and re-layouts  44.8 us (15%)
  matrix products  38.2 us (13%)
  between operations  16.4 us (6%)
  other arithmetic  15.5 us (5%)
  starting transfers between devices  10.2 us (3%)
    psum x1, blocking collectives, shards(): both = lax.psum(jnp.stack([down_part, up_part]), 'mp').astype(jnp.bfloat16)  55.8 us
    unnamed x1, blocking collectives  52.9 us
    all_to_all x1, waiting for transfers between devices, shards(): lax.all_to_all(back_send, 'dx', split_axis=0, concat_axis=0, tiled=True)  52.7 us
    gather x1, local copies, waits for them, and re-layouts, shards(): jnp.take(recv, panel_slot.reshape(-1), axis=0, mode='clip')  8.76 us
    dot_general x1, matrix products, shards(): jnp.einsum('pnr,pnd->prd', by_panel(down_low), rows_p, preferred_element_...  7.59 us
    gather x1, local copies, waits for them, and re-layouts, shards(): down_sel = jnp.take(down_col, panel_at, axis=0, mode='clip')  7.4 us
    dot_general x1, matrix products, shards(): jnp.einsum('snd,srd->snr', tok_recv, down_sel, preferred_element_type=jnp...  6.96 us
    dot_general x1, matrix products, shards(): jnp.einsum('krc,dkc->rd', cot_parts, value_weight.reshape(width_loc, n_mp...  6.69 us
  transfers between devices with their start and end apart: 6, of which 2 were waited for; matrix products, arithmetic and copies ran while one was open for 32% of the time, Pallas kernels for 0%

profile of v11, /device:TPU:1, one launch (start us, length us, event | category | flops | bytes accessed | tf_op | source)
XLA Modules:
  0.0 290.7 jit_solution(3961038016917458817)
XLA Ops:
  8.1 2.0 pad_maximum_fusion.3
  10.1 0.7 pad_clamp_fusion.5
  10.8 1.4 gather_fusion
  12.1 1.4 gather_fusion.1
  13.5 5.9 %fusion.28 = f32[1024,1024]{1,0:T(8,128)} fusion(bf16[1024,1024]{1,0:T(8,128)(2,1)} %param.9, bf16[1024,1024]{1,0:T(8,128)(2,1)S(1)} %copy-done), kind=kOutput, calls=%fused_computation.109 | convolution fusion | flops 2147483648 | bytes 8388608 | tf_op jit(solution)/shard_map/dot_general | solution.py:52
  19.4 0.2 convert_reduce_fusion.1
  19.7 0.6 copy-done.2
  20.3 0.7 gather_fusion.3
  21.0 2.9 gather_fusion.2
  23.9 4.9 %pad_maximum_fusion = bf16[64,32,1152]{2,1,0:T(8,128)(2,1)} fusion(bf16[64,32,128]{2,1,0:T(8,128)(2,1)S(1)} %gather_fusion.3, bf16[64,32,1024]{2,1,0:T(8,128)(2,1)} %gather_fusion.2), kind=kLoop, calls=%fused_computation.11 | loop fusion | flops 9437184 | bytes 9437184 | tf_op jit(solution)/shard_map/concatenate | solution.py:89
  28.8 5.1 %all-to-all-start = ((bf16[64,32,1152]{2,1,0:T(8,128)(2,1)}), bf16[64,32,1152]{2,1,0:T(8,128)(2,1)}, u32[]{:S(2)}, u32[]{:S(2)}) async-start(bf16[64,32,1152]{2,1,0:T(8,128)(2,1)} %pad_maximum_fusion), calls=%async_computation.1 | async-start | bytes 9437184 | tf_op jit(solution)/shard_map/all_to_all | solution.py:92
  33.9 0.7 all-gather.7.cloned.1.call-update
  34.7 0.6 dynamic-slice
  36.0 0.2 dynamic-update-slice
  36.2 52.9 %all-reduce = s32[128]{0:T(128)S(1)} all-reduce(s32[128]{0:T(128)S(1)} %dynamic-update-slice), channel_id=2, replica_groups=mesh['dz'=8,'dx'=4,'mp'=8] {'dx'}, use_global_device_ids=true, to_apply=%add | all-reduce | flops 128 | bytes 1024
  89.4 0.2 convert_reduce_fusion
  89.6 0.4 select_reduce_fusion.2
  91.7 0.1 select_reduce_fusion
  92.4 8.8 %gather_fusion.8 = bf16[96,32,1152]{2,1,0:T(8,128)(2,1)} fusion(bf16[64,32,1152]{2,1,0:T(8,128)(2,1)} %all-to-all-done, s32[1024]{0:T(1024)S(1)} %pad_clamp_fusion), kind=kCustom, calls=%fused_computation.8 | custom fusion | bytes 14156160 | tf_op jit(solution)/shard_map/jit(_take)/gather | solution.py:118
  101.2 1.0 slice.65
  102.2 0.7 gather_fusion.5
  102.9 1.7 convolution_bitcast_fusion
  104.6 4.0 %slice.63 = bf16[24,64,1024]{2,1,0:T(8,128)(2,1)} slice(bf16[24,64,1152]{2,1,0:T(8,128)(2,1)} %all-gather.5.cloned.1.call-done), slice={[0:24], [0:64], [0:1024]} | slice | bytes 6291456 | tf_op jit(solution)/shard_map/slice | solution.py:82
  108.6 7.4 %gather_fusion.4 = bf16[64,64,1024]{2,1,0:T(8,128)(2,1)} fusion(bf16[24,64,1024]{2,1,0:T(8,128)(2,1)} %slice.63, s32[1024]{0:T(1024)S(1)} %pad_clamp_fusion.2), kind=kCustom, calls=%fused_computation.4 | custom fusion | bytes 16777472 | tf_op jit(solution)/shard_map/jit(_take)/gather | solution.py:97
  116.0 7.0 %fusion.5 = f32[1,64,32,64]{3,2,1,0:T(8,128)S(1)} fusion(bf16[64,64,1024]{2,1,0:T(8,128)(2,1)} %gather_fusion.4, bf16[64,32,1152]{2,1,0:T(8,128)(2,1)} %all-to-all-done), kind=kOutput, calls=%fused_computation.21 | convolution fusion | flops 268435456 | bytes 13107200 | tf_op jit(solution)/shard_map/snd,srd->snr/dot_general | solution.py:99
  123.0 1.6 pad_maximum_fusion.2
  124.6 55.8 %all-reduce.2 = bf16[2,64,32,64]{3,2,1,0:T(8,128)(2,1)S(1)} all-reduce(f32[2,64,32,64]{3,2,1,0:T(8,128)} %pad_maximum_fusion.2), channel_id=1, replica_groups=mesh['dz'=8,'dx'=4,'mp'=8] {'mp'}, use_global_device_ids=true, to_apply=%region_20.21 | all-reduce | flops 262144 | bytes 1572864 | tf_op jit(solution)/shard_map/psum | solution.py:101
  180.4 1.6 gather_fusion.7
  182.0 2.1 copy.67
  184.1 0.7 gather_fusion.9
  184.8 0.3 copy.68
  185.2 4.3 %fusion.11 = f32[24,64,1152]{2,1,0:T(8,128)S(1)} fusion(bf16[24,128,1152]{2,1,0:T(8,128)(2,1)} %bitcast.78, bf16[24,128,64]{1,2,0:T(8,128)(2,1)} %copy.67, pred[24,128]{1,0:T(8,128)(4,1)S(1)} %broadcast_in_dim.118), kind=kOutput, calls=%fused_computation.31 | convolution fusion | flops 453181440 | bytes 14552064 | tf_op jit(solution)/shard_map/pnr,pnd->prd/dot_general | solution.py:121
  189.5 7.6 %convolution_select_fusion = f32[24,64,1152]{2,1,0:T(8,128)} fusion(f32[24,64,1152]{2,1,0:T(8,128)S(1)} %fusion.11, bf16[24,128,1152]{2,1,0:T(8,128)(2,1)} %bitcast.79, pred[1152]{0:T(1024)(128)(4,1)S(1)} %iota_compare_fusion.3, bf16[24,128,64]{1,2,0:T(8,128)(2,1)S(1)} %copy.68, pred[24,128]{1,0:T(8,128)(4,1)S(1)} %broadcast_in_dim.118), kind=kOutput, calls=%fused_computation.10 | convolution fusion | flops 454950912 | bytes 21631104 | tf_op jit(solution)/shard_map/pnr,pnd->prd/dot_general | solution.py:122
  197.1 0.4 convolution_convert_fusion.1
  197.5 4.6 %convolution_convert_fusion = bf16[64,32,1024]{2,1,0:T(8,128)(2,1)S(1)} fusion(bf16[64,64,1024]{2,1,0:T(8,128)(2,1)} %gather_fusion.4, bf16[2,64,32,64]{3,2,1,0:T(8,128)(2,1)S(1)} %all-reduce.2), kind=kOutput, calls=%fused_computation.17 | convolution fusion | flops 270532608 | bytes 13107200 | tf_op jit(solution)/shard_map/snr,srd->snd/dot_general | solution.py:107
  202.1 2.8 pad_maximum_fusion.1
  205.0 5.0 %all-to-all-start.1 = ((bf16[64,32,1152]{2,1,0:T(8,128)(2,1)}), bf16[64,32,1152]{2,1,0:T(8,128)(2,1)}, u32[]{:S(2)}, u32[]{:S(2)}) async-start(bf16[64,32,1152]{2,1,0:T(8,128)(2,1)} %pad_maximum_fusion.1), calls=%async_computation.2 | async-start | bytes 9437184 | tf_op jit(solution)/shard_map/all_to_all | solution.py:111
  210.0 52.7 %all-to-all-done.1 = bf16[64,32,1152]{2,1,0:T(8,128)(2,1)} async-done(((bf16[64,32,1152]{2,1,0:T(8,128)(2,1)}), bf16[64,32,1152]{2,1,0:T(8,128)(2,1)}, u32[]{:S(2)}, u32[]{:S(2)}) %all-to-all-start.1) | async-done | bytes 4718624 | tf_op jit(solution)/shard_map/all_to_all | solution.py:111
  262.7 4.6 %gather_fusion.6 = bf16[32,32,1152]{2,1,0:T(8,128)(2,1)} fusion(bf16[64,32,1152]{2,1,0:T(8,128)(2,1)} %all-to-all-done.1, s32[1024]{0:T(1024)S(1)} %pad_clamp_fusion.1), kind=kCustom, calls=%fused_computation.6 | custom fusion | bytes 4718720 | tf_op jit(solution)/shard_map/jit(_take)/gather | solution.py:139
  267.3 1.0 slice.68
  268.3 0.1 copy.70
  268.5 1.1 fusion.9
  269.6 0.8 copy.69
  270.4 6.7 %fusion.2 = bf16[1024,1024]{1,0:T(8,128)(2,1)} fusion(bf16[8,1024,128]{2,1,0:T(8,128)(2,1)} %bitcast.104, bf16[1024,1152]{1,0:T(8,128)(2,1)} %bitcast.84, bf16[1024,1024]{1,0:T(8,128)(2,1)} %param.9), kind=kOutput, calls=%fused_computation.16 | convolution fusion | flops 2150629376 | bytes 8388608 | tf_op jit(solution)/shard_map/krc,dkc->rd/dot_general | solution.py:133
  277.1 3.5 %reduce-scatter.5.cloned.1.call-done = f32[192,1152]{1,0:T(8,128)} async-done(((f32[1536,1152]{1,0:T(8,128)}), f32[192,1152]{1,0:T(8,128)}) %reduce-scatter.5.cloned.1.call-update) | async-done | bytes 884752 | tf_op jit(solution)/shard_map/reduce_scatter | solution.py:125
  280.6 1.2 convert.4
  281.8 0.8 slice.70
  282.6 0.6 slice.71
  (64 shorter events, 3.0 us)
Async XLA Ops:
  8.0 5.5 %copy-start = (bf16[1024,1024]{1,0:T(8,128)(2,1)S(1)}, bf16[1024,1024]{1,0:T(8,128)(2,1)}, u32[]{:S(2)}) copy-start(bf16[1024,1024]{1,0:T(8,128)(2,1)} %param.8) | copy-start | bytes 6291460
  8.0 93.1 %all-gather.5.cloned.1.call-start = ((), (), s32[]{:S(2)}) async-start(), calls=%async_computation.5 | async-start | bytes 3981312 | tf_op jit(solution)/shard_map/all_gather | solution.py:79
  10.0 258.4 %reduce-scatter.3.cloned.1.call-start = ((), (), s32[]{:S(2)}) async-start(), calls=%async_computation.4 | async-start | bytes 4718592 | tf_op jit(solution)/shard_map/reduce_scatter | solution.py:56
  19.4 0.9 copy-start.2
  28.8 5.9 %copy-start.3 = (u32[256]{0:T(256)S(1)}, u32[256]{0:T(256)}, u32[]{:S(2)}) copy-start(u32[256]{0:T(256)} %constant.110) | copy-start | bytes 3076
  28.8 63.6 %all-to-all-start = ((bf16[64,32,1152]{2,1,0:T(8,128)(2,1)}), bf16[64,32,1152]{2,1,0:T(8,128)(2,1)}, u32[]{:S(2)}, u32[]{:S(2)}) async-start(bf16[64,32,1152]{2,1,0:T(8,128)(2,1)} %pad_maximum_fusion), calls=%async_computation.1 | async-start | bytes 9437184 | tf_op jit(solution)/shard_map/all_to_all | solution.py:92
  33.9 236.5 %all-gather.7.cloned.1.call-start = ((), (), s32[]{:S(2)}) async-start(), calls=%async_computation.7 | async-start | bytes 2359296 | tf_op jit(solution)/shard_map/all_gather | solution.py:102
  34.6 245.9 %reduce-scatter.5.cloned.1.call-start = ((), (), s32[]{:S(2)}) async-start(), calls=%async_computation.6 | async-start | bytes 7962624 | tf_op jit(solution)/shard_map/reduce_scatter | solution.py:125
  205.0 57.7 %all-to-all-start.1 = ((bf16[64,32,1152]{2,1,0:T(8,128)(2,1)}), bf16[64,32,1152]{2,1,0:T(8,128)(2,1)}, u32[]{:S(2)}, u32[]{:S(2)}) async-start(bf16[64,32,1152]{2,1,0:T(8,128)(2,1)} %pad_maximum_fusion.1), calls=%async_computation.2 | async-start | bytes 9437184 | tf_op jit(solution)/shard_map/all_to_all | solution.py:111
  270.4 12.8 %copy-start.1 = (bf16[1024,1024]{1,0:T(8,128)(2,1)S(1)}, bf16[1024,1024]{1,0:T(8,128)(2,1)}, u32[]{:S(2)}) copy-start(bf16[1024,1024]{1,0:T(8,128)(2,1)} %param.8) | copy-start | bytes 6291460
Sparse Core Ops, SparseCore 0:
  11.2 52.4 all-gather.4
  65.6 26.7 all-gather.6
Sparse Core Ops, SparseCore 1:
  19.5 42.3 reduce-scatter.2
  197.2 83.3 reduce-scatter.4

commit v12 on v11

--- a/solution.py
+++ b/solution.py
@@ -90,24 +90,23 @@
         [jnp.take(token_blocks, source, axis=0, mode="clip"), jnp.take(cot_blocks, source, axis=0, mode="clip")], axis=2
     )
     recv = lax.all_to_all(send, "dx", split_axis=0, concat_axis=0, tiled=True)
-    tok_recv = recv[:, :, :width_loc]
-    cot_recv = recv[:, :, width_loc:]
-
+    width_all = width_loc + out_loc
+    feature = jnp.arange(width_all, dtype=jnp.int32)[None, None, :]
     panel_at = jnp.clip(slot_panel, 0, column - 1)
-    down_sel = jnp.take(down_col, panel_at, axis=0, mode="clip")
-    up_sel = jnp.take(up_col, panel_at, axis=0, mode="clip")
-    down_part = jnp.einsum("snd,srd->snr", tok_recv, down_sel, preferred_element_type=jnp.float32)
-    up_part = jnp.einsum("snc,src->snr", cot_recv, up_sel, preferred_element_type=jnp.float32)
+    sel = jnp.take(both_col, panel_at, axis=0, mode="clip")
+    down_sel = jnp.where(feature < width_loc, sel, jnp.zeros_like(sel))
+    up_sel = jnp.where(feature >= width_loc, sel, jnp.zeros_like(sel))
+    down_part = jnp.einsum("snd,srd->snr", recv, down_sel, preferred_element_type=jnp.float32)
+    up_part = jnp.einsum("snd,srd->snr", recv, up_sel, preferred_element_type=jnp.float32)
     both = lax.psum(jnp.stack([down_part, up_part]), "mp").astype(jnp.bfloat16)
     cot_parts = lax.all_gather(cotangent, "mp", axis=0, tiled=False)
     down_low = both[0]
     up_grad = both[1]
 
-    adapter_out = jnp.einsum("snr,src->snc", down_low, up_sel, preferred_element_type=jnp.float32)
-    adapter_bwd = jnp.einsum("snr,srd->snd", up_grad, down_sel, preferred_element_type=jnp.float32)
-    back_send = jnp.concatenate(
-        [adapter_bwd.astype(jnp.bfloat16), adapter_out.astype(jnp.bfloat16)], axis=2
-    )
+    back_send = (
+        jnp.einsum("snr,srd->snd", up_grad, down_sel, preferred_element_type=jnp.float32)
+        + jnp.einsum("snr,srd->snd", down_low, up_sel, preferred_element_type=jnp.float32)
+    ).astype(jnp.bfloat16)
     back = lax.all_to_all(back_send, "dx", split_axis=0, concat_axis=0, tiled=True)
 
     def by_panel(small):
@@ -120,7 +119,6 @@
     )
     grad_up = jnp.einsum("pnr,pnd->prd", by_panel(up_grad), rows_p, preferred_element_type=jnp.float32)
     grad_low = jnp.einsum("pnr,pnd->prd", by_panel(down_low), rows_p, preferred_element_type=jnp.float32)
-    feature = jnp.arange(width_loc + out_loc, dtype=jnp.int32)[None, None, :]
     grads_col = jnp.where(feature < width_loc, grad_up, grad_low)
     grads = lax.psum_scatter(
         grads_col.reshape(column * rank, width_loc + out_loc), "dz", scatter_dimension=0, tiled=True

time: 292 us -> 293 us (level)
  matrix products: 38.2 us -> 52.6 us
  local copies, waits for them, and re-layouts: 44.8 us -> 36.3 us
  waiting for transfers between devices: 57 us -> 52.6 us
    dot_general x3, matrix products: 9.04 us -> 19 us  [the longest x1 8.09 us: shards(): jnp.einsum('snd,srd->snr', recv, down_sel, preferred_element_type=jnp.flo...]
    slice x2 -> x0, local copies, waits for them, and re-layouts: 5.01 us -> none  [the longest x1 3.98 us: shards(): down_col = both_col[:, :, :width_loc]]
    dot_general x1, matrix products: 4.63 us -> 9.02 us  [shards(): jnp.einsum('snr,srd->snd', up_grad, down_sel, preferred_element_type=jnp....]
    reduce_scatter x1, waiting for transfers between devices: 3.47 us -> 0.01 us  [shards(): lax.psum_scatter(grads_col.reshape(column * rank, width_loc + out_loc), '...]
    gather x2 -> x1, local copies, waits for them, and re-layouts: 8.15 us -> 8.01 us  [shards(): sel = jnp.take(both_col, panel_at, axis=0, mode='clip')]
  transfers between devices with their start and end apart: 6 -> 6, of which waited for: 2 -> 1; matrix products, arithmetic and copies ran while one was open for 32% -> 33% of each run, Pallas kernels for 0% -> 0%
where the time goes in v12:
time: 293 us; the launch traced here: 289 us
  blocking collectives  109 us (37%)
  waiting for transfers between devices  52.6 us (18%)
  matrix products  52.6 us (18%)
  local copies, waits for them, and re-layouts  36.3 us (12%)
  between operations  16.5 us (6%)
  other arithmetic  12.6 us (4%)
  starting transfers between devices  10.2 us (3%)
    psum x1, blocking collectives, shards(): both = lax.psum(jnp.stack([down_part, up_part]), 'mp').astype(jnp.bfloat16)  56 us
    unnamed x1, blocking collectives  52.6 us
    all_to_all x1, waiting for transfers between devices, shards(): lax.all_to_all(back_send, 'dx', split_axis=0, concat_axis=0, tiled=True)  51.8 us
    dot_general x1, matrix products, shards(): jnp.einsum('snr,srd->snd', up_grad, down_sel, preferred_element_type=jnp....  9.02 us
    gather x1, local copies, waits for them, and re-layouts, shards(): jnp.take(recv, panel_slot.reshape(-1), axis=0, mode='clip')  8.73 us
    dot_general x1, matrix products, shards(): jnp.einsum('snd,srd->snr', recv, down_sel, preferred_element_type=jnp.flo...  8.09 us
    gather x1, local copies, waits for them, and re-layouts, shards(): sel = jnp.take(both_col, panel_at, axis=0, mode='clip')  8.01 us
    dot_general x1, matrix products, shards(): jnp.einsum('pnr,pnd->prd', by_panel(down_low), rows_p, preferred_element_...  7.51 us
  transfers between devices with their start and end apart: 6, of which 1 were waited for; matrix products, arithmetic and copies ran while one was open for 33% of the time, Pallas kernels for 0%

profile of v12, /device:TPU:1, one launch (start us, length us, event | category | flops | bytes accessed | tf_op | source)
XLA Modules:
  0.0 289.3 jit_solution(3021803860884918831)
XLA Ops:
  8.1 2.0 pad_maximum_fusion.2
  10.1 0.7 pad_clamp_fusion.5
  10.8 1.4 gather_fusion
  12.1 1.4 gather_fusion.1
  13.5 6.1 %fusion.36 = f32[1024,1024]{1,0:T(8,128)} fusion(bf16[1024,1024]{1,0:T(8,128)(2,1)} %param.9, bf16[1024,1024]{1,0:T(8,128)(2,1)S(1)} %copy-done), kind=kOutput, calls=%fused_computation.118 | convolution fusion | flops 2147483648 | bytes 8388608 | tf_op jit(solution)/shard_map/dot_general | solution.py:52
  19.6 0.2 convert_reduce_fusion.1
  19.9 0.7 gather_fusion.3
  20.6 2.8 gather_fusion.2
  23.4 4.9 %pad_maximum_fusion = bf16[64,32,1152]{2,1,0:T(8,128)(2,1)} fusion(bf16[64,32,128]{2,1,0:T(8,128)(2,1)S(1)} %gather_fusion.3, bf16[64,32,1024]{2,1,0:T(8,128)(2,1)} %gather_fusion.2), kind=kLoop, calls=%fused_computation.17 | loop fusion | flops 9437184 | bytes 9437184 | tf_op jit(solution)/shard_map/concatenate | solution.py:89
  28.3 5.1 %all-to-all-start = ((bf16[64,32,1152]{2,1,0:T(8,128)(2,1)}), bf16[64,32,1152]{2,1,0:T(8,128)(2,1)}, u32[]{:S(2)}, u32[]{:S(2)}) async-start(bf16[64,32,1152]{2,1,0:T(8,128)(2,1)} %pad_maximum_fusion), calls=%async_computation.1 | async-start | bytes 9437184 | tf_op jit(solution)/shard_map/all_to_all | solution.py:92
  33.5 0.7 all-gather.7.cloned.1.call-update
  34.3 0.6 dynamic-slice
  35.5 0.2 dynamic-update-slice
  35.7 52.6 %all-reduce = s32[128]{0:T(128)S(1)} all-reduce(s32[128]{0:T(128)S(1)} %dynamic-update-slice), channel_id=2, replica_groups=mesh['dz'=8,'dx'=4,'mp'=8] {'dx'}, use_global_device_ids=true, to_apply=%add | all-reduce | flops 128 | bytes 1024
  88.7 0.2 convert_reduce_fusion
  88.9 0.4 select_reduce_fusion.2
  89.3 0.1 copy.61
  89.7 0.1 copy.57
  90.8 0.1 stack.76
  91.0 0.2 select_reduce_fusion
  91.1 0.1 copy.65
  91.3 0.1 broadcast_in_dim.131
  91.5 0.1 reshape.310
  91.7 8.7 %gather_fusion.7 = bf16[96,32,1152]{2,1,0:T(8,128)(2,1)} fusion(bf16[64,32,1152]{2,1,0:T(8,128)(2,1)} %all-to-all-done, s32[1024]{0:T(1024)S(1)} %pad_clamp_fusion), kind=kCustom, calls=%fused_computation.7 | custom fusion | bytes 14156160 | tf_op jit(solution)/shard_map/jit(_take)/gather | solution.py:117
  100.4 8.0 %gather_fusion.4 = bf16[64,64,1152]{2,1,0:T(8,128)(2,1)} fusion(bf16[24,64,1152]{2,1,0:T(8,128)(2,1)} %all-gather.5.cloned.1.call-done, s32[1024]{0:T(1024)S(1)} %pad_clamp_fusion.2), kind=kCustom, calls=%fused_computation.4 | custom fusion | bytes 18874624 | tf_op jit(solution)/shard_map/jit(_take)/gather | solution.py:96
  108.4 8.1 %fusion.12 = f32[1,64,32,64]{3,2,1,0:T(8,128)S(1)} fusion(bf16[64,32,1152]{2,1,0:T(8,128)(2,1)} %all-to-all-done, bf16[64,64,1152]{2,1,0:T(8,128)(2,1)} %gather_fusion.4, pred[1152]{0:T(1024)(128)(4,1)S(1)} %iota_compare_fusion.4), kind=kOutput, calls=%fused_computation.28 | convolution fusion | flops 306708480 | bytes 14681216 | tf_op jit(solution)/shard_map/snd,srd->snr/dot_general | solution.py:99
  116.5 4.7 %fusion.11 = f32[1,64,32,64]{3,2,1,0:T(8,128)S(1)} fusion(bf16[64,32,1152]{2,1,0:T(8,128)(2,1)} %all-to-all-done, bf16[64,64,1152]{2,1,0:T(8,128)(2,1)S(1)} %copy-done.2, pred[1152]{0:T(1024)(128)(4,1)S(1)} %iota_compare_fusion.3), kind=kOutput, calls=%fused_computation.27 | convolution fusion | flops 306708480 | bytes 14681216 | tf_op jit(solution)/shard_map/snd,srd->snr/dot_general | solution.py:100
  121.3 1.6 pad_maximum_fusion.1
  122.8 56.0 %all-reduce.2 = bf16[2,64,32,64]{3,2,1,0:T(8,128)(2,1)S(1)} all-reduce(f32[2,64,32,64]{3,2,1,0:T(8,128)} %pad_maximum_fusion.1), channel_id=1, replica_groups=mesh['dz'=8,'dx'=4,'mp'=8] {'mp'}, use_global_device_ids=true, to_apply=%region_20.21 | all-reduce | flops 262144 | bytes 1572864 | tf_op jit(solution)/shard_map/psum | solution.py:101
  178.9 0.7 gather_fusion.8
  179.6 0.3 copy.68
  179.9 0.7 gather_fusion.6
  180.7 0.3 copy.67
  181.0 4.2 %fusion.15 = f32[24,64,1152]{2,1,0:T(8,128)S(1)} fusion(bf16[24,128,1152]{2,1,0:T(8,128)(2,1)} %bitcast.76, bf16[24,128,64]{1,2,0:T(8,128)(2,1)S(1)} %copy.67, pred[24,128]{1,0:T(8,128)(4,1)S(1)} %broadcast_in_dim.131), kind=kOutput, calls=%fused_computation.35 | convolution fusion | flops 453181440 | bytes 14552064 | tf_op jit(solution)/shard_map/pnr,pnd->prd/dot_general | solution.py:120
  185.1 7.5 %convolution_select_fusion = f32[24,64,1152]{2,1,0:T(8,128)} fusion(f32[24,64,1152]{2,1,0:T(8,128)S(1)} %fusion.15, bf16[24,128,1152]{2,1,0:T(8,128)(2,1)} %bitcast.77, pred[1152]{0:T(1024)(128)(4,1)S(1)} %iota_compare_fusion.4, bf16[24,128,64]{1,2,0:T(8,128)(2,1)S(1)} %copy.68, pred[24,128]{1,0:T(8,128)(4,1)S(1)} %broadcast_in_dim.131), kind=kOutput, calls=%fused_computation.16 | convolution fusion | flops 454950912 | bytes 21631104 | tf_op jit(solution)/shard_map/pnr,pnd->prd/dot_general | solution.py:121
  192.7 9.0 %fusion = f32[64,32,1152]{2,1,0:T(8,128)} fusion(bf16[64,64,1152]{2,1,0:T(8,128)(2,1)} %gather_fusion.4, pred[1152]{0:T(1024)(128)(4,1)S(1)} %iota_compare_fusion.4, bf16[2,64,32,64]{3,2,1,0:T(8,128)(2,1)S(1)} %all-reduce.2), kind=kOutput, calls=%fused_computation.12 | convolution fusion | flops 306708480 | bytes 19400704 | tf_op jit(solution)/shard_map/snr,srd->snd/dot_general | solution.py:107
  201.7 6.2 %add_convert_fusion = bf16[64,32,1152]{2,1,0:T(8,128)(2,1)} fusion(f32[64,32,1152]{2,1,0:T(8,128)} %fusion, bf16[64,64,1152]{2,1,0:T(8,128)(2,1)S(1)} %bitcast.79, pred[1152]{0:T(1024)(128)(4,1)S(1)} %iota_compare_fusion.3, bf16[2,64,32,64]{3,2,1,0:T(8,128)(2,1)S(1)} %all-reduce.2), kind=kOutput, calls=%fused_computation.9 | convolution fusion | flops 311427072 | bytes 24119296 | tf_op jit(solution)/shard_map/snr,srd->snd/dot_general | solution.py:108
  208.0 4.9 %all-to-all-start.1 = ((bf16[64,32,1152]{2,1,0:T(8,128)(2,1)}), bf16[64,32,1152]{2,1,0:T(8,128)(2,1)}, u32[]{:S(2)}, u32[]{:S(2)}) async-start(bf16[64,32,1152]{2,1,0:T(8,128)(2,1)} %add_convert_fusion), calls=%async_computation.2 | async-start | bytes 9437184 | tf_op jit(solution)/shard_map/all_to_all | solution.py:110
  212.9 51.8 %all-to-all-done.1 = bf16[64,32,1152]{2,1,0:T(8,128)(2,1)} async-done(((bf16[64,32,1152]{2,1,0:T(8,128)(2,1)}), bf16[64,32,1152]{2,1,0:T(8,128)(2,1)}, u32[]{:S(2)}, u32[]{:S(2)}) %all-to-all-start.1) | async-done | bytes 4718624 | tf_op jit(solution)/shard_map/all_to_all | solution.py:110
  264.7 4.6 %gather_fusion.5 = bf16[32,32,1152]{2,1,0:T(8,128)(2,1)} fusion(bf16[64,32,1152]{2,1,0:T(8,128)(2,1)} %all-to-all-done.1, s32[1024]{0:T(1024)S(1)} %pad_clamp_fusion.1), kind=kCustom, calls=%fused_computation.5 | custom fusion | bytes 4718720 | tf_op jit(solution)/shard_map/jit(_take)/gather | solution.py:137
  269.3 1.0 slice.46
  270.3 0.1 copy.70
  270.5 1.1 fusion.13
  271.6 0.8 copy.69
  272.4 6.8 %fusion.8 = bf16[1024,1024]{1,0:T(8,128)(2,1)} fusion(bf16[8,1024,128]{2,1,0:T(8,128)(2,1)} %bitcast.104, bf16[1024,1152]{1,0:T(8,128)(2,1)} %bitcast.84, bf16[1024,1024]{1,0:T(8,128)(2,1)} %param.9), kind=kOutput, calls=%fused_computation.23 | convolution fusion | flops 2150629376 | bytes 8388608 | tf_op jit(solution)/shard_map/krc,dkc->rd/dot_general | solution.py:131
  279.2 1.2 convert.4
  280.4 0.6 slice.49
  281.0 0.8 slice.48
  (70 shorter events, 2.4 us)
Async XLA Ops:
  8.0 5.5 %copy-start = (bf16[1024,1024]{1,0:T(8,128)(2,1)S(1)}, bf16[1024,1024]{1,0:T(8,128)(2,1)}, u32[]{:S(2)}) copy-start(bf16[1024,1024]{1,0:T(8,128)(2,1)} %param.8) | copy-start | bytes 6291460
  8.0 92.4 %all-gather.5.cloned.1.call-start = ((), (), s32[]{:S(2)}) async-start(), calls=%async_computation.5 | async-start | bytes 3981312 | tf_op jit(solution)/shard_map/all_gather | solution.py:79
  10.0 260.4 %reduce-scatter.3.cloned.1.call-start = ((), (), s32[]{:S(2)}) async-start(), calls=%async_computation.4 | async-start | bytes 4718592 | tf_op jit(solution)/shard_map/reduce_scatter | solution.py:56
  13.5 6.4 %copy-start.3 = (bf16[1024,128]{1,0:T(8,128)(2,1)S(1)}, bf16[1024,128]{1,0:T(8,128)(2,1)}, u32[]{:S(2)}) copy-start(bf16[1024,128]{1,0:T(8,128)(2,1)} %param.12) | copy-start | bytes 786436
  28.3 5.9 %copy-start.4 = (u32[256]{0:T(256)S(1)}, u32[256]{0:T(256)}, u32[]{:S(2)}) copy-start(u32[256]{0:T(256)} %constant.111) | copy-start | bytes 3076
  28.3 63.4 %all-to-all-start = ((bf16[64,32,1152]{2,1,0:T(8,128)(2,1)}), bf16[64,32,1152]{2,1,0:T(8,128)(2,1)}, u32[]{:S(2)}, u32[]{:S(2)}) async-start(bf16[64,32,1152]{2,1,0:T(8,128)(2,1)} %pad_maximum_fusion), calls=%async_computation.1 | async-start | bytes 9437184 | tf_op jit(solution)/shard_map/all_to_all | solution.py:92
  33.4 239.0 %all-gather.7.cloned.1.call-start = ((), (), s32[]{:S(2)}) async-start(), calls=%async_computation.7 | async-start | bytes 2359296 | tf_op jit(solution)/shard_map/all_gather | solution.py:102
  34.2 245.0 %reduce-scatter.5.cloned.1.call-start = ((), (), s32[]{:S(2)}) async-start(), calls=%async_computation.6 | async-start | bytes 7962624 | tf_op jit(solution)/shard_map/reduce_scatter | solution.py:123
  108.4 8.1 %copy-start.2 = (bf16[64,64,1152]{2,1,0:T(8,128)(2,1)S(1)}, bf16[64,64,1152]{2,1,0:T(8,128)(2,1)}, u32[]{:S(2)}) copy-start(bf16[64,64,1152]{2,1,0:T(8,128)(2,1)} %gather_fusion.4) | copy-start | bytes 28311556
  192.7 9.1 %slice-start = ((s8[9437184]{0:T(1024)(128)(4,1)}), s8[1048576]{0:T(1024)(128)(4,1)S(1)}, s32[]{:S(2)}) async-start(s8[9437184]{0:T(1024)(128)(4,1)} %bitcast.78), calls=%async_computation.8 | async-start | bytes 2097152
  192.7 9.0 %slice-start.1 = ((s8[9437184]{0:T(1024)(128)(4,1)}), s8[4194304]{0:T(1024)(128)(4,1)S(1)}, s32[]{:S(2)}) async-start(s8[9437184]{0:T(1024)(128)(4,1)} %bitcast.78), calls=%async_computation.9 | async-start | bytes 8388608
  192.7 9.0 %slice-start.2 = ((s8[9437184]{0:T(1024)(128)(4,1)}), s8[4194304]{0:T(1024)(128)(4,1)S(1)}, s32[]{:S(2)}) async-start(s8[9437184]{0:T(1024)(128)(4,1)} %bitcast.78), calls=%async_computation.10 | async-start | bytes 8388608
  208.0 56.8 %all-to-all-start.1 = ((bf16[64,32,1152]{2,1,0:T(8,128)(2,1)}), bf16[64,32,1152]{2,1,0:T(8,128)(2,1)}, u32[]{:S(2)}, u32[]{:S(2)}) async-start(bf16[64,32,1152]{2,1,0:T(8,128)(2,1)} %add_convert_fusion), calls=%async_computation.2 | async-start | bytes 9437184 | tf_op jit(solution)/shard_map/all_to_all | solution.py:110
  272.4 9.4 %copy-start.1 = (bf16[1024,1024]{1,0:T(8,128)(2,1)S(1)}, bf16[1024,1024]{1,0:T(8,128)(2,1)}, u32[]{:S(2)}) copy-start(bf16[1024,1024]{1,0:T(8,128)(2,1)} %param.8) | copy-start | bytes 6291460
Sparse Core Ops, SparseCore 0:
  11.2 52.4 all-gather.4
  65.6 26.7 all-gather.6
Sparse Core Ops, SparseCore 1:
  19.7 42.3 reduce-scatter.2
  192.8 83.5 reduce-scatter.4

commit v13 on v11

--- a/solution.py
+++ b/solution.py
@@ -7,6 +7,7 @@
 
 MOST = 2
 DP = ("dz", "dx")
+MP = ("my", "mc")
 
 
 def earlier_same(group):
@@ -53,7 +54,7 @@
         value_weight, tokens, (((0,), (1,)), ((), ())), preferred_element_type=jnp.float32
     )
     location_tied, base_part = lax.optimization_barrier((location, base_part))
-    base_t = lax.psum_scatter(base_part, "mp", scatter_dimension=0, tiled=True)
+    base_t = lax.psum_scatter(base_part, MP, scatter_dimension=0, tiled=True)
     x_location = lax.all_gather(location_tied, "dx", axis=0, tiled=False)
     x_owner_x = (x_location // stored) % n_x
     x_rank = earlier_same(x_owner_x)
@@ -82,7 +83,7 @@
     down_col = both_col[:, :, :width_loc]
     up_col = both_col[:, :, width_loc:]
 
-    n_mp = lax.axis_size("mp")
+    n_mp = lax.axis_size("my") * lax.axis_size("mc")
 
     token_blocks = tokens.reshape(blocks, blk, width_loc)
     cot_blocks = cotangent.reshape(blocks, blk, out_loc)
@@ -98,8 +99,8 @@
     up_sel = jnp.take(up_col, panel_at, axis=0, mode="clip")
     down_part = jnp.einsum("snd,srd->snr", tok_recv, down_sel, preferred_element_type=jnp.float32)
     up_part = jnp.einsum("snc,src->snr", cot_recv, up_sel, preferred_element_type=jnp.float32)
-    both = lax.psum(jnp.stack([down_part, up_part]), "mp").astype(jnp.bfloat16)
-    cot_parts = lax.all_gather(cotangent, "mp", axis=0, tiled=False)
+    both = lax.psum(lax.psum(jnp.stack([down_part, up_part]), "mc"), "my").astype(jnp.bfloat16)
+    cot_parts = lax.all_gather(cotangent, MP, axis=0, tiled=False)
     down_low = both[0]
     up_grad = both[1]
 
@@ -151,21 +152,22 @@
         n_x = 1
     if n_x < 1 or n_dp % n_x:
         n_x = 1
-    return Mesh(devices.reshape(n_dp // n_x, n_x, n_mp), ("dz", "dx", "mp"))
+    n_c = 2 if n_mp % 2 == 0 else 1
+    return Mesh(devices.reshape(n_dp // n_x, n_x, n_mp // n_c, n_c), ("dz", "dx", "my", "mc"))
 
 
 def solution(mesh):
     in_specs = (
-        P(DP, "mp"),
-        P("mp", None),
-        P(DP, None, "mp"),
-        P(DP, None, "mp"),
-        P(DP, "mp"),
+        P(DP, MP),
+        P(MP, None),
+        P(DP, None, MP),
+        P(DP, None, MP),
+        P(DP, MP),
         P(DP),
         P(DP),
         P(),
     )
-    out_specs = (P(DP, "mp"), P(DP, "mp"), P(DP, None, "mp"), P(DP, None, "mp"))
+    out_specs = (P(DP, MP), P(DP, MP), P(DP, None, MP), P(DP, None, MP))
     return jax.shard_map(
         shards, mesh=split_dp(mesh), in_specs=in_specs, out_specs=out_specs, check_vma=False
     )

time: 292 us -> 311 us (1.065)
  waiting for transfers between devices: 57 us -> 83.5 us
  blocking collectives: 109 us -> 101 us
    psum x0 -> x1, waiting for transfers between devices: none -> 26.3 us  [shards(): lax.psum(jnp.stack([down_part, up_part]), 'mc')]
    unnamed x1, blocking collectives: 52.9 us -> 47.5 us
  transfers between devices with their start and end apart: 6 -> 7, of which waited for: 2 -> 3; matrix products, arithmetic and copies ran while one was open for 32% -> 27% of each run, Pallas kernels for 0% -> 0%
where the time goes in v13:
time: 311 us; the launch traced here: 310 us
  blocking collectives  101 us (32%)
  waiting for transfers between devices  83.5 us (27%)
  local copies, waits for them, and re-layouts  44.9 us (14%)
  matrix products  38.3 us (12%)
  between operations  16.6 us (5%)
  other arithmetic  15.4 us (5%)
  starting transfers between devices  10.2 us (3%)
    psum x1, blocking collectives, shards(): lax.psum(lax.psum(jnp.stack([down_part, up_part]), 'mc'), 'my')  53.8 us
    all_to_all x1, waiting for transfers between devices, shards(): lax.all_to_all(back_send, 'dx', split_axis=0, concat_axis=0, tiled=True)  53.2 us
    unnamed x1, blocking collectives  47.5 us
    psum x1, waiting for transfers between devices, shards(): lax.psum(jnp.stack([down_part, up_part]), 'mc')  26.3 us
    gather x1, local copies, waits for them, and re-layouts, shards(): jnp.take(recv, panel_slot.reshape(-1), axis=0, mode='clip')  8.74 us
    dot_general x1, matrix products, shards(): jnp.einsum('pnr,pnd->prd', by_panel(down_low), rows_p, preferred_element_...  7.55 us
    gather x1, local copies, waits for them, and re-layouts, shards(): down_sel = jnp.take(down_col, panel_at, axis=0, mode='clip')  7.29 us
    dot_general x1, matrix products, shards(): jnp.einsum('snd,srd->snr', tok_recv, down_sel, preferred_element_type=jnp...  6.97 us
  transfers between devices with their start and end apart: 7, of which 3 were waited for; matrix products, arithmetic and copies ran while one was open for 27% of the time, Pallas kernels for 0%

profile of v13, /device:TPU:1, one launch (start us, length us, event | category | flops | bytes accessed | tf_op | source)
XLA Modules:
  0.0 310.1 jit_solution(2468955325735221592)
XLA Ops:
  8.1 2.0 pad_maximum_fusion.3
  10.0 0.7 pad_clamp_fusion.5
  10.7 1.4 gather_fusion
  12.1 1.4 gather_fusion.1
  13.5 0.2 convert_reduce_fusion.1
  13.8 1.6 gather_fusion.3
  15.4 2.7 gather_fusion.2
  18.1 4.9 %pad_maximum_fusion = bf16[64,32,1152]{2,1,0:T(8,128)(2,1)} fusion(bf16[64,32,128]{2,1,0:T(8,128)(2,1)S(1)} %gather_fusion.3, bf16[64,32,1024]{2,1,0:T(8,128)(2,1)} %gather_fusion.2), kind=kLoop, calls=%fused_computation.11 | loop fusion | flops 9437184 | bytes 9437184 | tf_op jit(solution)/shard_map/concatenate | solution.py:90
  23.0 5.0 %all-to-all-start = ((bf16[64,32,1152]{2,1,0:T(8,128)(2,1)}), bf16[64,32,1152]{2,1,0:T(8,128)(2,1)}, u32[]{:S(2)}, u32[]{:S(2)}) async-start(bf16[64,32,1152]{2,1,0:T(8,128)(2,1)} %pad_maximum_fusion), calls=%async_computation.1 | async-start | bytes 9437184 | tf_op jit(solution)/shard_map/all_to_all | solution.py:93
  28.1 6.0 %fusion.28 = f32[1024,1024]{1,0:T(8,128)} fusion(bf16[1024,1024]{1,0:T(8,128)(2,1)} %param.9, bf16[1024,1024]{1,0:T(8,128)(2,1)S(1)} %copy-done), kind=kOutput, calls=%fused_computation.109 | convolution fusion | flops 2147483648 | bytes 8388608 | tf_op jit(solution)/shard_map/dot_general | solution.py:53
  34.1 0.6 dynamic-slice
  35.4 0.2 dynamic-update-slice
  35.6 47.5 %all-reduce = s32[128]{0:T(128)S(1)} all-reduce(s32[128]{0:T(128)S(1)} %dynamic-update-slice), channel_id=2, replica_groups=mesh['dz'=8,'dx'=4,'my'=4,'mc'=2] {'dx'}, use_global_device_ids=true, to_apply=%add | all-reduce | flops 128 | bytes 1024
  83.5 0.2 convert_reduce_fusion
  83.7 0.4 select_reduce_fusion.2
  85.8 1.0 slice.65
  86.8 0.7 gather_fusion.5
  87.6 4.0 %slice.63 = bf16[24,64,1024]{2,1,0:T(8,128)(2,1)} slice(bf16[24,64,1152]{2,1,0:T(8,128)(2,1)} %all-gather.5.cloned.1.call-done), slice={[0:24], [0:64], [0:1024]} | slice | bytes 6291456 | tf_op jit(solution)/shard_map/slice | solution.py:83
  91.5 7.3 %gather_fusion.4 = bf16[64,64,1024]{2,1,0:T(8,128)(2,1)} fusion(bf16[24,64,1024]{2,1,0:T(8,128)(2,1)} %slice.63, s32[1024]{0:T(1024)S(1)} %pad_clamp_fusion.2), kind=kCustom, calls=%fused_computation.4 | custom fusion | bytes 16777472 | tf_op jit(solution)/shard_map/jit(_take)/gather | solution.py:98
  98.8 1.7 convolution_bitcast_fusion
  100.5 7.0 %fusion.5 = f32[1,64,32,64]{3,2,1,0:T(8,128)S(1)} fusion(bf16[64,64,1024]{2,1,0:T(8,128)(2,1)} %gather_fusion.4, bf16[64,32,1152]{2,1,0:T(8,128)(2,1)} %all-to-all-done), kind=kOutput, calls=%fused_computation.21 | convolution fusion | flops 268435456 | bytes 13107200 | tf_op jit(solution)/shard_map/snd,srd->snr/dot_general | solution.py:100
  107.5 1.6 pad_maximum_fusion.2
  109.2 0.5 reduce-scatter.3.cloned.1.call-update
  109.7 0.5 all-gather.7.cloned.1.call-update
  110.3 0.1 select_reduce_fusion
  111.0 8.7 %gather_fusion.8 = bf16[96,32,1152]{2,1,0:T(8,128)(2,1)} fusion(bf16[64,32,1152]{2,1,0:T(8,128)(2,1)} %all-to-all-done, s32[1024]{0:T(1024)S(1)} %pad_clamp_fusion), kind=kCustom, calls=%fused_computation.8 | custom fusion | bytes 14156160 | tf_op jit(solution)/shard_map/jit(_take)/gather | solution.py:119
  119.7 26.3 %all-reduce.4.cloned.1.call-done = f32[2,64,32,64]{3,2,1,0:T(8,128)} async-done(((f32[2,64,32,64]{3,2,1,0:T(8,128)}), f32[2,64,32,64]{3,2,1,0:T(8,128)}) %all-reduce.4.cloned.1.call-update) | async-done | bytes 1048592 | tf_op jit(solution)/shard_map/psum | solution.py:102
  146.1 53.8 %all-reduce.5 = bf16[2,64,32,64]{3,2,1,0:T(8,128)(2,1)S(1)} all-reduce(f32[2,64,32,64]{3,2,1,0:T(8,128)} %all-reduce.4.cloned.1.call-done), channel_id=1, replica_groups=mesh['dz'=8,'dx'=4,'my'=4,'mc'=2] {'my'}, use_global_device_ids=true, to_apply=%region_21.22 | all-reduce | flops 262144 | bytes 1572864 | tf_op jit(solution)/shard_map/psum | solution.py:102
  200.0 1.6 gather_fusion.7
  201.5 2.1 copy.67
  203.7 0.7 gather_fusion.9
  204.4 0.3 copy.68
  204.7 4.3 %fusion.11 = f32[24,64,1152]{2,1,0:T(8,128)S(1)} fusion(bf16[24,128,1152]{2,1,0:T(8,128)(2,1)} %bitcast.78, bf16[24,128,64]{1,2,0:T(8,128)(2,1)} %copy.67, pred[24,128]{1,0:T(8,128)(4,1)S(1)} %broadcast_in_dim.118), kind=kOutput, calls=%fused_computation.31 | convolution fusion | flops 453181440 | bytes 14552064 | tf_op jit(solution)/shard_map/pnr,pnd->prd/dot_general | solution.py:122
  209.0 7.6 %convolution_select_fusion = f32[24,64,1152]{2,1,0:T(8,128)} fusion(f32[24,64,1152]{2,1,0:T(8,128)S(1)} %fusion.11, bf16[24,128,1152]{2,1,0:T(8,128)(2,1)} %bitcast.79, pred[1152]{0:T(1024)(128)(4,1)S(1)} %iota_compare_fusion.3, bf16[24,128,64]{1,2,0:T(8,128)(2,1)S(1)} %copy.68, pred[24,128]{1,0:T(8,128)(4,1)S(1)} %broadcast_in_dim.118), kind=kOutput, calls=%fused_computation.10 | convolution fusion | flops 454950912 | bytes 21631104 | tf_op jit(solution)/shard_map/pnr,pnd->prd/dot_general | solution.py:123
  216.6 0.4 convolution_convert_fusion.1
  217.0 4.6 %convolution_convert_fusion = bf16[64,32,1024]{2,1,0:T(8,128)(2,1)S(1)} fusion(bf16[64,64,1024]{2,1,0:T(8,128)(2,1)} %gather_fusion.4, bf16[2,64,32,64]{3,2,1,0:T(8,128)(2,1)S(1)} %all-reduce.5), kind=kOutput, calls=%fused_computation.17 | convolution fusion | flops 270532608 | bytes 13107200 | tf_op jit(solution)/shard_map/snr,srd->snd/dot_general | solution.py:108
  221.6 2.7 pad_maximum_fusion.1
  224.4 4.9 %all-to-all-start.1 = ((bf16[64,32,1152]{2,1,0:T(8,128)(2,1)}), bf16[64,32,1152]{2,1,0:T(8,128)(2,1)}, u32[]{:S(2)}, u32[]{:S(2)}) async-start(bf16[64,32,1152]{2,1,0:T(8,128)(2,1)} %pad_maximum_fusion.1), calls=%async_computation.2 | async-start | bytes 9437184 | tf_op jit(solution)/shard_map/all_to_all | solution.py:112
  229.3 53.2 %all-to-all-done.1 = bf16[64,32,1152]{2,1,0:T(8,128)(2,1)} async-done(((bf16[64,32,1152]{2,1,0:T(8,128)(2,1)}), bf16[64,32,1152]{2,1,0:T(8,128)(2,1)}, u32[]{:S(2)}, u32[]{:S(2)}) %all-to-all-start.1) | async-done | bytes 4718624 | tf_op jit(solution)/shard_map/all_to_all | solution.py:112
  282.5 4.7 %gather_fusion.6 = bf16[32,32,1152]{2,1,0:T(8,128)(2,1)} fusion(bf16[64,32,1152]{2,1,0:T(8,128)(2,1)} %all-to-all-done.1, s32[1024]{0:T(1024)S(1)} %pad_clamp_fusion.1), kind=kCustom, calls=%fused_computation.6 | custom fusion | bytes 4718720 | tf_op jit(solution)/shard_map/jit(_take)/gather | solution.py:140
  287.2 1.0 slice.68
  288.3 1.1 fusion.9
  289.5 0.8 copy.69
  290.3 6.7 %fusion.2 = bf16[1024,1024]{1,0:T(8,128)(2,1)} fusion(bf16[8,1024,128]{2,1,0:T(8,128)(2,1)} %bitcast.104, bf16[1024,1152]{1,0:T(8,128)(2,1)} %bitcast.84, bf16[1024,1024]{1,0:T(8,128)(2,1)} %param.9), kind=kOutput, calls=%fused_computation.16 | convolution fusion | flops 2150629376 | bytes 8388608 | tf_op jit(solution)/shard_map/krc,dkc->rd/dot_general | solution.py:134
  297.0 2.9 reduce-scatter.5.cloned.1.call-done
  299.9 1.2 convert.4
  301.1 0.8 slice.70
  301.9 0.6 slice.71
  (65 shorter events, 3.2 us)
Async XLA Ops:
  8.0 7.4 %copy-start = (bf16[1024,1024]{1,0:T(8,128)(2,1)S(1)}, bf16[1024,1024]{1,0:T(8,128)(2,1)}, u32[]{:S(2)}) copy-start(bf16[1024,1024]{1,0:T(8,128)(2,1)} %param.8) | copy-start | bytes 6291460
  8.0 77.8 %all-gather.5.cloned.1.call-start = ((), (), s32[]{:S(2)}) async-start(), calls=%async_computation.5 | async-start | bytes 3981312 | tf_op jit(solution)/shard_map/all_gather | solution.py:80
  23.0 75.8 %all-to-all-start = ((bf16[64,32,1152]{2,1,0:T(8,128)(2,1)}), bf16[64,32,1152]{2,1,0:T(8,128)(2,1)}, u32[]{:S(2)}, u32[]{:S(2)}) async-start(bf16[64,32,1152]{2,1,0:T(8,128)(2,1)} %pad_maximum_fusion), calls=%async_computation.1 | async-start | bytes 9437184 | tf_op jit(solution)/shard_map/all_to_all | solution.py:93
  28.1 118.0 %all-reduce.4.cloned.1.call-start = ((), (), s32[]{:S(2)}) async-start(), calls=%async_computation.6 | async-start | bytes 4194304 | tf_op jit(solution)/shard_map/psum | solution.py:102
  28.1 6.0 %copy-start.2 = (u32[256]{0:T(256)S(1)}, u32[256]{0:T(256)}, u32[]{:S(2)}) copy-start(u32[256]{0:T(256)} %constant.110) | copy-start | bytes 3076
  109.1 179.2 %reduce-scatter.3.cloned.1.call-start = ((), (), s32[]{:S(2)}) async-start(), calls=%async_computation.4 | async-start | bytes 4718592 | tf_op jit(solution)/shard_map/reduce_scatter | solution.py:57
  109.7 180.6 %all-gather.7.cloned.1.call-start = ((), (), s32[]{:S(2)}) async-start(), calls=%async_computation.8 | async-start | bytes 2359296 | tf_op jit(solution)/shard_map/all_gather | solution.py:103
  110.3 189.6 %reduce-scatter.5.cloned.1.call-start = ((), (), s32[]{:S(2)}) async-start(), calls=%async_computation.7 | async-start | bytes 7962624 | tf_op jit(solution)/shard_map/reduce_scatter | solution.py:126
  224.4 58.2 %all-to-all-start.1 = ((bf16[64,32,1152]{2,1,0:T(8,128)(2,1)}), bf16[64,32,1152]{2,1,0:T(8,128)(2,1)}, u32[]{:S(2)}, u32[]{:S(2)}) async-start(bf16[64,32,1152]{2,1,0:T(8,128)(2,1)} %pad_maximum_fusion.1), calls=%async_computation.2 | async-start | bytes 9437184 | tf_op jit(solution)/shard_map/all_to_all | solution.py:112
  290.3 12.3 %copy-start.1 = (bf16[1024,1024]{1,0:T(8,128)(2,1)S(1)}, bf16[1024,1024]{1,0:T(8,128)(2,1)}, u32[]{:S(2)}) copy-start(bf16[1024,1024]{1,0:T(8,128)(2,1)} %param.8) | copy-start | bytes 6291460
Sparse Core Ops, SparseCore 0:
  11.2 52.4 all-gather.4
  109.2 36.7 all-reduce.3
Sparse Core Ops, SparseCore 1:
  112.1 41.7 reduce-scatter.2
  155.7 41.5 all-gather.6
  216.7 83.2 reduce-scatter.4

commit v14 on v11

--- a/solution.py
+++ b/solution.py
@@ -123,7 +123,10 @@
     feature = jnp.arange(width_loc + out_loc, dtype=jnp.int32)[None, None, :]
     grads_col = jnp.where(feature < width_loc, grad_up, grad_low)
     grads = lax.psum_scatter(
-        grads_col.reshape(column * rank, width_loc + out_loc), "dz", scatter_dimension=0, tiled=True
+        grads_col.astype(jnp.bfloat16).reshape(column * rank, width_loc + out_loc),
+        "dz",
+        scatter_dimension=0,
+        tiled=True,
     )
     grad_a = grads[:, :width_loc]
     grad_b = grads[:, width_loc:]
@@ -136,6 +139,7 @@
         value_weight.reshape(width_loc, n_mp, out_loc),
         preferred_element_type=jnp.float32,
     )
+    base_bwd = lax.optimization_barrier(base_bwd)
     mine_back = jnp.take(back, position, axis=0, mode="clip").reshape(rows, width_loc + out_loc)
     values = (base_t.T + mine_back[:, width_loc:].astype(jnp.float32)).astype(jnp.bfloat16)
     token_gradient = (base_bwd + mine_back[:, :width_loc].astype(jnp.float32)).astype(jnp.bfloat16)

time: 292 us -> 286 us (0.979)
  waiting for transfers between devices: 57 us -> 46.4 us
  other arithmetic: 15.5 us -> 19.3 us
    all_to_all x1, waiting for transfers between devices: 52.7 us -> 45.6 us  [shards(): lax.all_to_all(back_send, 'dx', split_axis=0, concat_axis=0, tiled=True)]
    convert_element_type x0 -> x1, other arithmetic: none -> 4.96 us  [shards(): (base_bwd + mine_back[:, :width_loc].astype(jnp.float32)).astype(jnp.bflo...]
    reduce_scatter x1, waiting for transfers between devices: 3.47 us -> 0.01 us  [shards(): lax.psum_scatter(grads_col.astype(jnp.bfloat16).reshape(column * rank, wi...]
  transfers between devices with their start and end apart: 6 -> 6, of which waited for: 2 -> 1; matrix products, arithmetic and copies ran while one was open for 32% -> 34% of each run, Pallas kernels for 0% -> 0%
where the time goes in v14:
time: 286 us; the launch traced here: 284 us
  blocking collectives  109 us (38%)
  local copies, waits for them, and re-layouts  46.7 us (16%)
  waiting for transfers between devices  46.4 us (16%)
  matrix products  37.1 us (13%)
  other arithmetic  19.3 us (7%)
  between operations  14.7 us (5%)
  starting transfers between devices  10.2 us (4%)
    psum x1, blocking collectives, shards(): both = lax.psum(jnp.stack([down_part, up_part]), 'mp').astype(jnp.bfloat16)  55.8 us
    unnamed x1, blocking collectives  53.7 us
    all_to_all x1, waiting for transfers between devices, shards(): lax.all_to_all(back_send, 'dx', split_axis=0, concat_axis=0, tiled=True)  45.6 us
    gather x1, local copies, waits for them, and re-layouts, shards(): jnp.take(recv, panel_slot.reshape(-1), axis=0, mode='clip')  8.81 us
    gather x1, local copies, waits for them, and re-layouts, shards(): down_sel = jnp.take(down_col, panel_at, axis=0, mode='clip')  7.42 us
    dot_general x1, matrix products, shards(): jnp.einsum('snd,srd->snr', tok_recv, down_sel, preferred_element_type=jnp...  7.23 us
    dot_general x1, matrix products, shards(): jnp.einsum('krc,dkc->rd', cot_parts, value_weight.reshape(width_loc, n_mp...  6.69 us
    dot_general x1, matrix products, shards(): jnp.einsum('pnr,pnd->prd', by_panel(down_low), rows_p, preferred_element_...  6.16 us
  transfers between devices with their start and end apart: 6, of which 1 were waited for; matrix products, arithmetic and copies ran while one was open for 34% of the time, Pallas kernels for 0%

profile of v14, /device:TPU:1, one launch (start us, length us, event | category | flops | bytes accessed | tf_op | source)
XLA Modules:
  0.0 283.8 jit_solution(7799087887903923186)
XLA Ops:
  7.2 2.0 pad_maximum_fusion.3
  9.3 0.7 all-gather.7.cloned.1.call-update
  10.0 0.7 pad_clamp_fusion.5
  10.7 1.4 gather_fusion
  12.0 1.4 gather_fusion.1
  13.4 6.0 %fusion.27 = f32[1024,1024]{1,0:T(8,128)} fusion(bf16[1024,1024]{1,0:T(8,128)(2,1)} %param.9, bf16[1024,1024]{1,0:T(8,128)(2,1)S(1)} %copy-done), kind=kOutput, calls=%fused_computation.109 | convolution fusion | flops 2147483648 | bytes 8388608 | tf_op jit(solution)/shard_map/dot_general | solution.py:52
  19.4 0.2 convert_reduce_fusion.1
  19.7 0.6 copy-done.2
  20.3 0.7 gather_fusion.3
  21.0 2.8 gather_fusion.2
  23.8 5.0 %pad_maximum_fusion = bf16[64,32,1152]{2,1,0:T(8,128)(2,1)} fusion(bf16[64,32,128]{2,1,0:T(8,128)(2,1)S(1)} %gather_fusion.3, bf16[64,32,1024]{2,1,0:T(8,128)(2,1)} %gather_fusion.2), kind=kLoop, calls=%fused_computation.11 | loop fusion | flops 9437184 | bytes 9437184 | tf_op jit(solution)/shard_map/concatenate | solution.py:89
  28.8 5.1 %all-to-all-start = ((bf16[64,32,1152]{2,1,0:T(8,128)(2,1)}), bf16[64,32,1152]{2,1,0:T(8,128)(2,1)}, u32[]{:S(2)}, u32[]{:S(2)}) async-start(bf16[64,32,1152]{2,1,0:T(8,128)(2,1)} %pad_maximum_fusion), calls=%async_computation.1 | async-start | bytes 9437184 | tf_op jit(solution)/shard_map/all_to_all | solution.py:92
  34.0 0.6 dynamic-slice
  35.3 0.2 dynamic-update-slice
  35.5 53.7 %all-reduce = s32[128]{0:T(128)S(1)} all-reduce(s32[128]{0:T(128)S(1)} %dynamic-update-slice), channel_id=2, replica_groups=mesh['dz'=8,'dx'=4,'mp'=8] {'dx'}, use_global_device_ids=true, to_apply=%add | all-reduce | flops 128 | bytes 1024
  89.5 0.2 convert_reduce_fusion
  89.7 0.4 select_reduce_fusion.2
  91.6 0.1 stack.76
  91.8 0.1 select_reduce_fusion
  92.5 8.8 %gather_fusion.8 = bf16[96,32,1152]{2,1,0:T(8,128)(2,1)} fusion(bf16[64,32,1152]{2,1,0:T(8,128)(2,1)} %all-to-all-done, s32[1024]{0:T(1024)S(1)} %pad_clamp_fusion), kind=kCustom, calls=%fused_computation.8 | custom fusion | bytes 14156160 | tf_op jit(solution)/shard_map/jit(_take)/gather | solution.py:118
  101.3 1.0 slice.63
  102.3 0.7 gather_fusion.5
  103.1 4.1 %slice.61 = bf16[24,64,1024]{2,1,0:T(8,128)(2,1)} slice(bf16[24,64,1152]{2,1,0:T(8,128)(2,1)} %all-gather.5.cloned.1.call-done), slice={[0:24], [0:64], [0:1024]} | slice | bytes 6291456 | tf_op jit(solution)/shard_map/slice | solution.py:82
  107.2 7.4 %gather_fusion.4 = bf16[64,64,1024]{2,1,0:T(8,128)(2,1)} fusion(bf16[24,64,1024]{2,1,0:T(8,128)(2,1)} %slice.61, s32[1024]{0:T(1024)S(1)} %pad_clamp_fusion.2), kind=kCustom, calls=%fused_computation.4 | custom fusion | bytes 16777472 | tf_op jit(solution)/shard_map/jit(_take)/gather | solution.py:97
  114.6 1.7 convolution_bitcast_fusion.1
  116.3 7.2 %fusion.4 = f32[1,64,32,64]{3,2,1,0:T(8,128)S(1)} fusion(bf16[64,64,1024]{2,1,0:T(8,128)(2,1)} %gather_fusion.4, bf16[64,32,1152]{2,1,0:T(8,128)(2,1)} %all-to-all-done), kind=kOutput, calls=%fused_computation.21 | convolution fusion | flops 268435456 | bytes 13107200 | tf_op jit(solution)/shard_map/snd,srd->snr/dot_general | solution.py:99
  123.5 1.6 pad_maximum_fusion.2
  125.1 55.8 %all-reduce.2 = bf16[2,64,32,64]{3,2,1,0:T(8,128)(2,1)S(1)} all-reduce(f32[2,64,32,64]{3,2,1,0:T(8,128)} %pad_maximum_fusion.2), channel_id=1, replica_groups=mesh['dz'=8,'dx'=4,'mp'=8] {'mp'}, use_global_device_ids=true, to_apply=%region_20.21 | all-reduce | flops 262144 | bytes 1572864 | tf_op jit(solution)/shard_map/psum | solution.py:101
  181.0 1.6 gather_fusion.7
  182.6 2.1 copy.67
  184.8 0.7 gather_fusion.9
  185.5 0.3 copy.68
  185.8 4.3 %fusion.10 = bf16[24,64,1152]{2,1,0:T(8,128)(2,1)S(1)} fusion(bf16[24,128,1152]{2,1,0:T(8,128)(2,1)} %bitcast.76, bf16[24,128,64]{1,2,0:T(8,128)(2,1)} %copy.67, pred[24,128]{1,0:T(8,128)(4,1)S(1)} %broadcast_in_dim.118), kind=kOutput, calls=%fused_computation.31 | convolution fusion | flops 453181440 | bytes 11013120 | tf_op jit(solution)/shard_map/pnr,pnd->prd/dot_general | solution.py:121
  190.1 6.2 %select_convert_fusion = bf16[24,64,1152]{2,1,0:T(8,128)(2,1)} fusion(bf16[24,64,1152]{2,1,0:T(8,128)(2,1)S(1)} %fusion.10, bf16[24,128,1152]{2,1,0:T(8,128)(2,1)} %bitcast.77, pred[1152]{0:T(1024)(128)(4,1)S(1)} %iota_compare_fusion.3, bf16[24,128,64]{1,2,0:T(8,128)(2,1)S(1)} %copy.68, pred[24,128]{1,0:T(8,128)(4,1)S(1)} %broadcast_in_dim.118), kind=kOutput, calls=%fused_computation.10 | convolution fusion | flops 454950912 | bytes 14553216 | tf_op jit(solution)/shard_map/pnr,pnd->prd/dot_general | solution.py:122
  196.3 0.4 convolution_convert_fusion.1
  196.7 4.6 %convolution_convert_fusion = bf16[64,32,1024]{2,1,0:T(8,128)(2,1)S(1)} fusion(bf16[64,64,1024]{2,1,0:T(8,128)(2,1)} %gather_fusion.4, bf16[2,64,32,64]{3,2,1,0:T(8,128)(2,1)S(1)} %all-reduce.2), kind=kOutput, calls=%fused_computation.16 | convolution fusion | flops 270532608 | bytes 13107200 | tf_op jit(solution)/shard_map/snr,srd->snd/dot_general | solution.py:107
  201.3 2.8 pad_maximum_fusion.1
  204.1 4.9 %all-to-all-start.1 = ((bf16[64,32,1152]{2,1,0:T(8,128)(2,1)}), bf16[64,32,1152]{2,1,0:T(8,128)(2,1)}, u32[]{:S(2)}, u32[]{:S(2)}) async-start(bf16[64,32,1152]{2,1,0:T(8,128)(2,1)} %pad_maximum_fusion.1), calls=%async_computation.2 | async-start | bytes 9437184 | tf_op jit(solution)/shard_map/all_to_all | solution.py:111
  209.1 6.7 %convolution_bitcast_fusion = f32[1024,1024]{1,0:T(8,128)} fusion(bf16[8,1024,128]{2,1,0:T(8,128)(2,1)} %bitcast.102, bf16[1024,1024]{1,0:T(8,128)(2,1)} %param.9), kind=kOutput, calls=%fused_computation.17 | convolution fusion | flops 2147483648 | bytes 8388608 | tf_op jit(solution)/shard_map/krc,dkc->rd/dot_general | solution.py:136
  215.8 45.6 %all-to-all-done.1 = bf16[64,32,1152]{2,1,0:T(8,128)(2,1)} async-done(((bf16[64,32,1152]{2,1,0:T(8,128)(2,1)}), bf16[64,32,1152]{2,1,0:T(8,128)(2,1)}, u32[]{:S(2)}, u32[]{:S(2)}) %all-to-all-start.1) | async-done | bytes 4718624 | tf_op jit(solution)/shard_map/all_to_all | solution.py:111
  261.4 4.6 %gather_fusion.6 = bf16[32,32,1152]{2,1,0:T(8,128)(2,1)} fusion(bf16[64,32,1152]{2,1,0:T(8,128)(2,1)} %all-to-all-done.1, s32[1024]{0:T(1024)S(1)} %pad_clamp_fusion.1), kind=kCustom, calls=%fused_computation.6 | custom fusion | bytes 4718720 | tf_op jit(solution)/shard_map/jit(_take)/gather | solution.py:143
  266.0 1.0 slice.66
  267.0 0.1 copy.70
  267.2 1.1 fusion.8
  268.3 0.8 copy.69
  269.1 5.0 %add_convert_fusion = bf16[1024,1024]{1,0:T(8,128)(2,1)} fusion(f32[1024,1024]{1,0:T(8,128)} %convolution_bitcast_fusion, bf16[1024,1152]{1,0:T(8,128)(2,1)} %bitcast.80), kind=kLoop, calls=%fused_computation.15 | loop fusion | flops 3145728 | bytes 8388608 | tf_op jit(solution)/shard_map/convert_element_type | solution.py:145
  274.1 1.8 slice.68
  275.9 1.4 slice.69
  (64 shorter events, 2.9 us)
Async XLA Ops:
  7.2 6.2 %copy-start = (bf16[1024,1024]{1,0:T(8,128)(2,1)S(1)}, bf16[1024,1024]{1,0:T(8,128)(2,1)}, u32[]{:S(2)}) copy-start(bf16[1024,1024]{1,0:T(8,128)(2,1)} %param.8) | copy-start | bytes 6291460
  7.2 94.1 %all-gather.5.cloned.1.call-start = ((), (), s32[]{:S(2)}) async-start(), calls=%async_computation.5 | async-start | bytes 3981312 | tf_op jit(solution)/shard_map/all_gather | solution.py:79
  9.2 199.9 %all-gather.7.cloned.1.call-start = ((), (), s32[]{:S(2)}) async-start(), calls=%async_computation.7 | async-start | bytes 2359296 | tf_op jit(solution)/shard_map/all_gather | solution.py:102
  10.0 257.2 %reduce-scatter.3.cloned.1.call-start = ((), (), s32[]{:S(2)}) async-start(), calls=%async_computation.4 | async-start | bytes 4718592 | tf_op jit(solution)/shard_map/reduce_scatter | solution.py:56
  19.4 0.9 copy-start.2
  28.8 5.2 %copy-start.3 = (u32[256]{0:T(256)S(1)}, u32[256]{0:T(256)}, u32[]{:S(2)}) copy-start(u32[256]{0:T(256)} %constant.110) | copy-start | bytes 3076
  28.8 63.7 %all-to-all-start = ((bf16[64,32,1152]{2,1,0:T(8,128)(2,1)}), bf16[64,32,1152]{2,1,0:T(8,128)(2,1)}, u32[]{:S(2)}, u32[]{:S(2)}) async-start(bf16[64,32,1152]{2,1,0:T(8,128)(2,1)} %pad_maximum_fusion), calls=%async_computation.1 | async-start | bytes 9437184 | tf_op jit(solution)/shard_map/all_to_all | solution.py:92
  34.0 240.1 %reduce-scatter.5.cloned.1.call-start = ((), (), s32[]{:S(2)}) async-start(), calls=%async_computation.6 | async-start | bytes 3981312 | tf_op jit(solution)/shard_map/reduce_scatter | solution.py:125
  204.1 57.3 %all-to-all-start.1 = ((bf16[64,32,1152]{2,1,0:T(8,128)(2,1)}), bf16[64,32,1152]{2,1,0:T(8,128)(2,1)}, u32[]{:S(2)}, u32[]{:S(2)}) async-start(bf16[64,32,1152]{2,1,0:T(8,128)(2,1)} %pad_maximum_fusion.1), calls=%async_computation.2 | async-start | bytes 9437184 | tf_op jit(solution)/shard_map/all_to_all | solution.py:111
  268.3 9.0 %copy-start.1 = (bf16[1024,1024]{1,0:T(8,128)(2,1)S(1)}, bf16[1024,1024]{1,0:T(8,128)(2,1)}, u32[]{:S(2)}) copy-start(bf16[1024,1024]{1,0:T(8,128)(2,1)} %param.8) | copy-start | bytes 6291460
Sparse Core Ops, SparseCore 0:
  10.4 52.4 all-gather.4
  64.7 26.7 all-gather.6
  94.1 37.3 reduce-scatter.2
  196.4 50.0 reduce-scatter.4

commit v15 on v11

--- a/solution.py
+++ b/solution.py
@@ -136,6 +136,7 @@
         value_weight.reshape(width_loc, n_mp, out_loc),
         preferred_element_type=jnp.float32,
     )
+    base_bwd = lax.optimization_barrier(base_bwd)
     mine_back = jnp.take(back, position, axis=0, mode="clip").reshape(rows, width_loc + out_loc)
     values = (base_t.T + mine_back[:, width_loc:].astype(jnp.float32)).astype(jnp.bfloat16)
     token_gradient = (base_bwd + mine_back[:, :width_loc].astype(jnp.float32)).astype(jnp.bfloat16)

time: 292 us -> 291 us (level)
  other arithmetic: 15.5 us -> 20.6 us
  waiting for transfers between devices: 57 us -> 52.1 us
    all_to_all x1, waiting for transfers between devices: 52.7 us -> 45.8 us  [shards(): lax.all_to_all(back_send, 'dx', split_axis=0, concat_axis=0, tiled=True)]
    convert_element_type x0 -> x1, other arithmetic: none -> 4.96 us  [shards(): (base_bwd + mine_back[:, :width_loc].astype(jnp.float32)).astype(jnp.bflo...]
  transfers between devices with their start and end apart: 6 -> 6, of which waited for: 2 -> 2; matrix products, arithmetic and copies ran while one was open for 32% -> 34% of each run, Pallas kernels for 0% -> 0%
where the time goes in v15:
time: 291 us; the launch traced here: 290 us
  blocking collectives  110 us (38%)
  waiting for transfers between devices  52.1 us (18%)
  local copies, waits for them, and re-layouts  44.8 us (15%)
  matrix products  38.4 us (13%)
  other arithmetic  20.6 us (7%)
  between operations  14.7 us (5%)
  starting transfers between devices  10.2 us (4%)
    psum x1, blocking collectives, shards(): both = lax.psum(jnp.stack([down_part, up_part]), 'mp').astype(jnp.bfloat16)  55.6 us
    unnamed x1, blocking collectives  54 us
    all_to_all x1, waiting for transfers between devices, shards(): lax.all_to_all(back_send, 'dx', split_axis=0, concat_axis=0, tiled=True)  45.8 us
    gather x1, local copies, waits for them, and re-layouts, shards(): jnp.take(recv, panel_slot.reshape(-1), axis=0, mode='clip')  8.67 us
    dot_general x1, matrix products, shards(): jnp.einsum('pnr,pnd->prd', by_panel(down_low), rows_p, preferred_element_...  7.59 us
    gather x1, local copies, waits for them, and re-layouts, shards(): down_sel = jnp.take(down_col, panel_at, axis=0, mode='clip')  7.41 us
    dot_general x1, matrix products, shards(): jnp.einsum('snd,srd->snr', tok_recv, down_sel, preferred_element_type=jnp...  7.23 us
    dot_general x1, matrix products, shards(): jnp.einsum('krc,dkc->rd', cot_parts, value_weight.reshape(width_loc, n_mp...  6.6 us
  transfers between devices with their start and end apart: 6, of which 2 were waited for; matrix products, arithmetic and copies ran while one was open for 34% of the time, Pallas kernels for 0%

profile of v15, /device:TPU:1, one launch (start us, length us, event | category | flops | bytes accessed | tf_op | source)
XLA Modules:
  0.0 290.4 jit_solution(1340633771889160610)
XLA Ops:
  7.2 2.0 pad_maximum_fusion.3
  9.3 0.7 all-gather.7.cloned.1.call-update
  10.0 0.7 pad_clamp_fusion.5
  10.7 1.4 gather_fusion
  12.0 1.4 gather_fusion.1
  13.4 5.9 %fusion.27 = f32[1024,1024]{1,0:T(8,128)} fusion(bf16[1024,1024]{1,0:T(8,128)(2,1)} %param.9, bf16[1024,1024]{1,0:T(8,128)(2,1)S(1)} %copy-done), kind=kOutput, calls=%fused_computation.109 | convolution fusion | flops 2147483648 | bytes 8388608 | tf_op jit(solution)/shard_map/dot_general | solution.py:52
  19.4 0.2 convert_reduce_fusion.1
  19.6 0.6 copy-done.2
  20.3 0.7 gather_fusion.3
  20.9 2.8 gather_fusion.2
  23.7 5.1 %pad_maximum_fusion = bf16[64,32,1152]{2,1,0:T(8,128)(2,1)} fusion(bf16[64,32,128]{2,1,0:T(8,128)(2,1)S(1)} %gather_fusion.3, bf16[64,32,1024]{2,1,0:T(8,128)(2,1)} %gather_fusion.2), kind=kLoop, calls=%fused_computation.11 | loop fusion | flops 9437184 | bytes 9437184 | tf_op jit(solution)/shard_map/concatenate | solution.py:89
  28.8 5.1 %all-to-all-start = ((bf16[64,32,1152]{2,1,0:T(8,128)(2,1)}), bf16[64,32,1152]{2,1,0:T(8,128)(2,1)}, u32[]{:S(2)}, u32[]{:S(2)}) async-start(bf16[64,32,1152]{2,1,0:T(8,128)(2,1)} %pad_maximum_fusion), calls=%async_computation.1 | async-start | bytes 9437184 | tf_op jit(solution)/shard_map/all_to_all | solution.py:92
  33.9 0.6 dynamic-slice
  35.2 0.2 dynamic-update-slice
  35.4 54.0 %all-reduce = s32[128]{0:T(128)S(1)} all-reduce(s32[128]{0:T(128)S(1)} %dynamic-update-slice), channel_id=2, replica_groups=mesh['dz'=8,'dx'=4,'mp'=8] {'dx'}, use_global_device_ids=true, to_apply=%add | all-reduce | flops 128 | bytes 1024
  89.7 0.2 convert_reduce_fusion
  89.9 0.4 select_reduce_fusion.2
  92.0 0.1 select_reduce_fusion
  92.7 8.7 %gather_fusion.8 = bf16[96,32,1152]{2,1,0:T(8,128)(2,1)} fusion(bf16[64,32,1152]{2,1,0:T(8,128)(2,1)} %all-to-all-done, s32[1024]{0:T(1024)S(1)} %pad_clamp_fusion), kind=kCustom, calls=%fused_computation.8 | custom fusion | bytes 14156160 | tf_op jit(solution)/shard_map/jit(_take)/gather | solution.py:118
  101.4 1.0 slice.65
  102.4 0.7 gather_fusion.5
  103.2 4.1 %slice.63 = bf16[24,64,1024]{2,1,0:T(8,128)(2,1)} slice(bf16[24,64,1152]{2,1,0:T(8,128)(2,1)} %all-gather.5.cloned.1.call-done), slice={[0:24], [0:64], [0:1024]} | slice | bytes 6291456 | tf_op jit(solution)/shard_map/slice | solution.py:82
  107.3 7.4 %gather_fusion.4 = bf16[64,64,1024]{2,1,0:T(8,128)(2,1)} fusion(bf16[24,64,1024]{2,1,0:T(8,128)(2,1)} %slice.63, s32[1024]{0:T(1024)S(1)} %pad_clamp_fusion.2), kind=kCustom, calls=%fused_computation.4 | custom fusion | bytes 16777472 | tf_op jit(solution)/shard_map/jit(_take)/gather | solution.py:97
  114.7 1.7 convolution_bitcast_fusion.1
  116.4 7.2 %fusion.4 = f32[1,64,32,64]{3,2,1,0:T(8,128)S(1)} fusion(bf16[64,64,1024]{2,1,0:T(8,128)(2,1)} %gather_fusion.4, bf16[64,32,1152]{2,1,0:T(8,128)(2,1)} %all-to-all-done), kind=kOutput, calls=%fused_computation.21 | convolution fusion | flops 268435456 | bytes 13107200 | tf_op jit(solution)/shard_map/snd,srd->snr/dot_general | solution.py:99
  123.6 1.6 pad_maximum_fusion.2
  125.2 55.6 %all-reduce.2 = bf16[2,64,32,64]{3,2,1,0:T(8,128)(2,1)S(1)} all-reduce(f32[2,64,32,64]{3,2,1,0:T(8,128)} %pad_maximum_fusion.2), channel_id=1, replica_groups=mesh['dz'=8,'dx'=4,'mp'=8] {'mp'}, use_global_device_ids=true, to_apply=%region_20.21 | all-reduce | flops 262144 | bytes 1572864 | tf_op jit(solution)/shard_map/psum | solution.py:101
  180.9 1.6 gather_fusion.7
  182.5 2.1 copy.67
  184.6 0.7 gather_fusion.9
  185.3 0.3 copy.68
  185.6 4.3 %fusion.10 = f32[24,64,1152]{2,1,0:T(8,128)S(1)} fusion(bf16[24,128,1152]{2,1,0:T(8,128)(2,1)} %bitcast.76, bf16[24,128,64]{1,2,0:T(8,128)(2,1)} %copy.67, pred[24,128]{1,0:T(8,128)(4,1)S(1)} %broadcast_in_dim.118), kind=kOutput, calls=%fused_computation.31 | convolution fusion | flops 453181440 | bytes 14552064 | tf_op jit(solution)/shard_map/pnr,pnd->prd/dot_general | solution.py:121
  190.0 7.6 %convolution_select_fusion = f32[24,64,1152]{2,1,0:T(8,128)} fusion(f32[24,64,1152]{2,1,0:T(8,128)S(1)} %fusion.10, bf16[24,128,1152]{2,1,0:T(8,128)(2,1)} %bitcast.77, pred[1152]{0:T(1024)(128)(4,1)S(1)} %iota_compare_fusion.3, bf16[24,128,64]{1,2,0:T(8,128)(2,1)S(1)} %copy.68, pred[24,128]{1,0:T(8,128)(4,1)S(1)} %broadcast_in_dim.118), kind=kOutput, calls=%fused_computation.10 | convolution fusion | flops 454950912 | bytes 21631104 | tf_op jit(solution)/shard_map/pnr,pnd->prd/dot_general | solution.py:122
  197.6 0.4 convolution_convert_fusion.1
  198.0 4.6 %convolution_convert_fusion = bf16[64,32,1024]{2,1,0:T(8,128)(2,1)S(1)} fusion(bf16[64,64,1024]{2,1,0:T(8,128)(2,1)} %gather_fusion.4, bf16[2,64,32,64]{3,2,1,0:T(8,128)(2,1)S(1)} %all-reduce.2), kind=kOutput, calls=%fused_computation.16 | convolution fusion | flops 270532608 | bytes 13107200 | tf_op jit(solution)/shard_map/snr,srd->snd/dot_general | solution.py:107
  202.6 2.9 pad_maximum_fusion.1
  205.5 5.0 %all-to-all-start.1 = ((bf16[64,32,1152]{2,1,0:T(8,128)(2,1)}), bf16[64,32,1152]{2,1,0:T(8,128)(2,1)}, u32[]{:S(2)}, u32[]{:S(2)}) async-start(bf16[64,32,1152]{2,1,0:T(8,128)(2,1)} %pad_maximum_fusion.1), calls=%async_computation.2 | async-start | bytes 9437184 | tf_op jit(solution)/shard_map/all_to_all | solution.py:111
  210.5 6.6 %convolution_bitcast_fusion = f32[1024,1024]{1,0:T(8,128)} fusion(bf16[8,1024,128]{2,1,0:T(8,128)(2,1)} %bitcast.102, bf16[1024,1024]{1,0:T(8,128)(2,1)} %param.9), kind=kOutput, calls=%fused_computation.17 | convolution fusion | flops 2147483648 | bytes 8388608 | tf_op jit(solution)/shard_map/krc,dkc->rd/dot_general | solution.py:133
  217.1 45.8 %all-to-all-done.1 = bf16[64,32,1152]{2,1,0:T(8,128)(2,1)} async-done(((bf16[64,32,1152]{2,1,0:T(8,128)(2,1)}), bf16[64,32,1152]{2,1,0:T(8,128)(2,1)}, u32[]{:S(2)}, u32[]{:S(2)}) %all-to-all-start.1) | async-done | bytes 4718624 | tf_op jit(solution)/shard_map/all_to_all | solution.py:111
  262.9 4.7 %gather_fusion.6 = bf16[32,32,1152]{2,1,0:T(8,128)(2,1)} fusion(bf16[64,32,1152]{2,1,0:T(8,128)(2,1)} %all-to-all-done.1, s32[1024]{0:T(1024)S(1)} %pad_clamp_fusion.1), kind=kCustom, calls=%fused_computation.6 | custom fusion | bytes 4718720 | tf_op jit(solution)/shard_map/jit(_take)/gather | solution.py:140
  267.6 1.0 slice.68
  268.7 1.1 fusion.8
  269.9 0.8 copy.69
  270.7 5.0 %add_convert_fusion = bf16[1024,1024]{1,0:T(8,128)(2,1)} fusion(f32[1024,1024]{1,0:T(8,128)} %convolution_bitcast_fusion, bf16[1024,1152]{1,0:T(8,128)(2,1)} %bitcast.80), kind=kLoop, calls=%fused_computation.15 | loop fusion | flops 3145728 | bytes 8388608 | tf_op jit(solution)/shard_map/convert_element_type | solution.py:142
  275.7 5.6 %reduce-scatter.5.cloned.1.call-done = f32[192,1152]{1,0:T(8,128)} async-done(((f32[1536,1152]{1,0:T(8,128)}), f32[192,1152]{1,0:T(8,128)}) %reduce-scatter.5.cloned.1.call-update) | async-done | bytes 884752 | tf_op jit(solution)/shard_map/reduce_scatter | solution.py:125
  281.2 1.2 convert.4
  282.4 0.8 slice.70
  283.2 0.6 slice.71
  (65 shorter events, 3.1 us)
Async XLA Ops:
  7.2 6.2 %copy-start = (bf16[1024,1024]{1,0:T(8,128)(2,1)S(1)}, bf16[1024,1024]{1,0:T(8,128)(2,1)}, u32[]{:S(2)}) copy-start(bf16[1024,1024]{1,0:T(8,128)(2,1)} %param.8) | copy-start | bytes 6291460
  7.2 94.2 %all-gather.5.cloned.1.call-start = ((), (), s32[]{:S(2)}) async-start(), calls=%async_computation.5 | async-start | bytes 3981312 | tf_op jit(solution)/shard_map/all_gather | solution.py:79
  9.2 201.3 %all-gather.7.cloned.1.call-start = ((), (), s32[]{:S(2)}) async-start(), calls=%async_computation.7 | async-start | bytes 2359296 | tf_op jit(solution)/shard_map/all_gather | solution.py:102
  10.0 258.7 %reduce-scatter.3.cloned.1.call-start = ((), (), s32[]{:S(2)}) async-start(), calls=%async_computation.4 | async-start | bytes 4718592 | tf_op jit(solution)/shard_map/reduce_scatter | solution.py:56
  19.3 0.9 copy-start.2
  28.8 5.2 %copy-start.3 = (u32[256]{0:T(256)S(1)}, u32[256]{0:T(256)}, u32[]{:S(2)}) copy-start(u32[256]{0:T(256)} %constant.110) | copy-start | bytes 3076
  28.8 63.9 %all-to-all-start = ((bf16[64,32,1152]{2,1,0:T(8,128)(2,1)}), bf16[64,32,1152]{2,1,0:T(8,128)(2,1)}, u32[]{:S(2)}, u32[]{:S(2)}) async-start(bf16[64,32,1152]{2,1,0:T(8,128)(2,1)} %pad_maximum_fusion), calls=%async_computation.1 | async-start | bytes 9437184 | tf_op jit(solution)/shard_map/all_to_all | solution.py:92
  33.9 247.4 %reduce-scatter.5.cloned.1.call-start = ((), (), s32[]{:S(2)}) async-start(), calls=%async_computation.6 | async-start | bytes 7962624 | tf_op jit(solution)/shard_map/reduce_scatter | solution.py:125
  205.5 57.4 %all-to-all-start.1 = ((bf16[64,32,1152]{2,1,0:T(8,128)(2,1)}), bf16[64,32,1152]{2,1,0:T(8,128)(2,1)}, u32[]{:S(2)}, u32[]{:S(2)}) async-start(bf16[64,32,1152]{2,1,0:T(8,128)(2,1)} %pad_maximum_fusion.1), calls=%async_computation.2 | async-start | bytes 9437184 | tf_op jit(solution)/shard_map/all_to_all | solution.py:111
  269.8 14.0 %copy-start.1 = (bf16[1024,1024]{1,0:T(8,128)(2,1)S(1)}, bf16[1024,1024]{1,0:T(8,128)(2,1)}, u32[]{:S(2)}) copy-start(bf16[1024,1024]{1,0:T(8,128)(2,1)} %param.8) | copy-start | bytes 6291460
Sparse Core Ops, SparseCore 0:
  10.4 52.4 all-gather.4
  64.7 26.7 all-gather.6
  94.1 37.3 reduce-scatter.2
  197.7 83.4 reduce-scatter.4
